TPU v7x, 32 devices: a whole 2x2x4 slice. The times are simulated.
32 devices in a mesh: wide: 8 (over z, x), narrow: 4 (over y, core).
Axes of the slice: x: 2, y: 2, z: 4, core: 2. Of those that a mesh axis runs over, the one named last changes fastest.
Arguments:
- query_states: bfloat16 [4096, 8192], P('wide', 'narrow'), may hold values from -8 to 8
- key_states: bfloat16 [4096, 8192], P('wide', 'narrow'), may hold values from -8 to 8
- value_states: bfloat16 [4096, 8192], P('wide', 'narrow'), may hold values from -6 to 6
- cache_keys: bfloat16 [4096, 1024], P('wide'), may hold values from -8 to 8
- cache_values: bfloat16 [4096, 1024], P('wide'), may hold values from -6 to 6
- gate_fast: bfloat16 [8, 512, 512], P('narrow'), may hold values from -0.25 to 0.25
- lift_fast: bfloat16 [8, 512, 512], P('narrow'), may hold values from -0.25 to 0.25
- down_fast: bfloat16 [8, 512, 512], P('narrow'), may hold values from -0.25 to 0.25
- token_rates: float32 [8, 8192], replicated, may hold values from 0.05 to 1
Outputs:
- attended: bfloat16 [4096, 8192], P('wide', 'narrow')
- recalled: bfloat16 [4096, 8192], P('wide', 'narrow')
All inputs are finite; a program needn't handle non-finite values.
Results may differ from a plain program's by a relative error of at most 0.0094.
Values may be sent and summed in bfloat16 or wider, within the bound.
No kernel may reach another device: no remote copies, remote signals or barrier semaphores. Data moves between devices by JAX's collectives and lax.ppermute only.
A program may use at most 128 MiB of HBM per device.

v0:
```python
import math

import jax
import jax.numpy as jnp
from jax import lax
from jax.sharding import PartitionSpec as P

FD = 512
HEAD_SIZE = 128
WINDOW = 1024
NS_ITERS = 2


EPS = 1e-06
COEF_A = 3.4445
COEF_B = -4.775
COEF_C = 2.0315


def swapped(array, axis, distance):
    return lax.ppermute(array, axis, [(i, i ^ 1 << distance) for i in range(lax.axis_size(axis))])


def shortened(array):

    def short(part):
        return part.astype(jnp.bfloat16) if part.dtype == jnp.float32 else part

    return jax.tree.map(short, array)


def from_behind(value, axis, steps):
    count = lax.axis_size(axis)
    initial, last = (max(0, -steps), min(count, count - steps))
    return lax.ppermute(value, axis, [(source, source + steps) for source in range(initial, last)])


def stored(value):
    return lax.optimization_barrier(value.astype(jnp.bfloat16))


def attend_local(query_states, ext_keys, ext_values, key_start):
    features, tok_count = query_states.shape
    head_count = features // HEAD_SIZE
    block_rows = min(512, tok_count)
    block_count = tok_count // block_rows
    key_span = WINDOW + block_rows
    scaling = 1.0 / math.sqrt(HEAD_SIZE)
    rows_at = lax.broadcasted_iota(jnp.int32, (block_rows, key_span), 0)
    cols_at = lax.broadcasted_iota(jnp.int32, (block_rows, key_span), 1)
    visible = (cols_at > rows_at) & (cols_at <= rows_at + WINDOW)

    def one_block(block_index):
        offset = block_index * block_rows
        query_part = lax.dynamic_slice_in_dim(query_states, offset, block_rows, 1).reshape(
            head_count, HEAD_SIZE, block_rows
        )
        key_part = lax.dynamic_slice_in_dim(ext_keys, key_start + offset, key_span, 1).reshape(
            head_count, HEAD_SIZE, key_span
        )
        value_part = lax.dynamic_slice_in_dim(ext_values, key_start + offset, key_span, 1).reshape(
            head_count, HEAD_SIZE, key_span
        )
        scores = (
            jnp.einsum("hdq,hdk->hqk", query_part, key_part, preferred_element_type=jnp.float32)
            * scaling
        )
        scores = jnp.where(visible[None], scores, -jnp.inf)
        highest = jnp.max(scores, axis=2, keepdims=True)
        raised = jnp.exp(scores - highest)
        weights = (raised / jnp.sum(raised, axis=2, keepdims=True)).astype(jnp.bfloat16)
        blended = jnp.einsum(
            "hdk,hqk->hdq", value_part, weights, preferred_element_type=jnp.float32
        )
        return blended.astype(jnp.bfloat16).reshape(features, block_rows)

    blocks_out = lax.map(one_block, jnp.arange(block_count, dtype=jnp.int32))
    return jnp.transpose(blocks_out, (1, 0, 2)).reshape(features, tok_count)


def attend_paired(query_states, ext_keys, ext_values):
    features, tok_count = query_states.shape
    half_rows = tok_count // 2
    lower = lax.axis_index("wide") % 2 == 0
    query_send = jnp.where(lower, query_states[:, half_rows:], query_states[:, :half_rows])
    query_keep = jnp.where(lower, query_states[:, :half_rows], query_states[:, half_rows:])
    other_keys, other_values, other_queries = swapped((ext_keys, ext_values, query_send), "wide", 0)
    full_keys = jnp.where(
        lower,
        jnp.concatenate([ext_keys, other_keys], axis=0),
        jnp.concatenate([other_keys, ext_keys], axis=0),
    )
    full_values = jnp.where(
        lower,
        jnp.concatenate([ext_values, other_values], axis=0),
        jnp.concatenate([other_values, ext_values], axis=0),
    )
    full_queries = jnp.where(
        lower,
        jnp.concatenate([query_keep, other_queries], axis=0),
        jnp.concatenate([other_queries, query_keep], axis=0),
    )
    key_start = jnp.where(lower, 0, half_rows).astype(jnp.int32)
    head_out = attend_local(full_queries, full_keys, full_values, key_start)
    out_keep = jnp.where(lower, head_out[:features], head_out[features:])
    out_send = jnp.where(lower, head_out[features:], head_out[:features])
    out_other = swapped(shortened(out_send), "wide", 0).astype(out_send.dtype)
    return jnp.where(
        lower,
        jnp.concatenate([out_keep, out_other], axis=1),
        jnp.concatenate([out_other, out_keep], axis=1),
    )


def fast_terms(gate_weight, lift_weight, down_weight, key_heads, value_heads, rates_here):
    pre_gate = jnp.einsum(
        "hcf,hft->hct", gate_weight, key_heads, preferred_element_type=jnp.float32
    )
    pre_lift = jnp.einsum(
        "hcf,hft->hct", lift_weight, key_heads, preferred_element_type=jnp.float32
    )
    sigmoid_gate = jax.nn.sigmoid(pre_gate)
    silu_gate = pre_gate * sigmoid_gate
    hidden = (silu_gate * pre_lift).astype(jnp.bfloat16)
    target = (-(value_heads.astype(jnp.float32) * rates_here[:, None, :])).astype(jnp.bfloat16)
    grad_down = jnp.einsum("hft,hct->hfc", target, hidden, preferred_element_type=jnp.float32)
    back_hidden = jnp.einsum(
        "hfc,hft->hct", down_weight, target, preferred_element_type=jnp.float32
    )
    back_lift = (back_hidden * silu_gate).astype(jnp.bfloat16)
    back_gate = (
        back_hidden * pre_lift * sigmoid_gate * (1.0 + pre_gate * (1.0 - sigmoid_gate))
    ).astype(jnp.bfloat16)
    grad_gate = jnp.einsum("hct,hft->hcf", back_gate, key_heads, preferred_element_type=jnp.float32)
    grad_lift = jnp.einsum("hct,hft->hcf", back_lift, key_heads, preferred_element_type=jnp.float32)
    return (grad_gate, grad_lift, grad_down)


def scaled_start(rounded):
    widened = rounded.astype(jnp.float32)
    norm_val = jnp.sqrt(jnp.sum(jnp.square(widened), axis=(1, 2), keepdims=True) + EPS)
    return stored(widened / norm_val)


def starting(grad_gate, grad_lift, grad_down):
    sum_gate, sum_lift, sum_down = lax.psum((grad_gate, grad_lift, grad_down), "wide")
    return (
        scaled_start(stored(sum_gate)),
        scaled_start(stored(sum_lift)),
        scaled_start(stored(sum_down)),
    )


def orthogonal(current):
    for sweep_index in range(NS_ITERS):
        gram_mat = jnp.einsum(
            "hrc,hrd->hcd", current, current, preferred_element_type=jnp.float32
        ).astype(jnp.bfloat16)
        lifted = stored(
            jnp.einsum("hrc,hcd->hrd", current, gram_mat, preferred_element_type=jnp.float32)
        )
        current = stored(
            COEF_A * current.astype(jnp.float32)
            + COEF_B * lifted.astype(jnp.float32)
            + COEF_C
            * jnp.einsum("hrc,hcd->hrd", lifted, gram_mat, preferred_element_type=jnp.float32)
        )
    return current


def refreshed(weight, ortho):
    initial = weight.astype(jnp.float32)
    moved_rows = initial - ortho.astype(jnp.float32)
    wanted = jnp.sqrt(jnp.mean(jnp.square(initial), axis=-1, keepdims=True) + EPS)
    present = jnp.sqrt(jnp.mean(jnp.square(moved_rows), axis=-1, keepdims=True) + EPS)
    return (moved_rows * (wanted / present)).astype(jnp.bfloat16)


def fast_group(
    gate_weight, lift_weight, down_weight, query_heads, key_heads, value_heads, rates_here
):
    grad_gate, grad_lift, grad_down = fast_terms(
        gate_weight, lift_weight, down_weight, key_heads, value_heads, rates_here
    )
    start_gate, start_lift, start_down = starting(grad_gate, grad_lift, grad_down)
    fresh_gate = refreshed(gate_weight, orthogonal(start_gate))
    fresh_lift = refreshed(lift_weight, orthogonal(start_lift))
    fresh_down = refreshed(down_weight, orthogonal(start_down))
    query_gate = jnp.einsum(
        "hcf,hft->hct", fresh_gate, query_heads, preferred_element_type=jnp.float32
    )
    query_lift = jnp.einsum(
        "hcf,hft->hct", fresh_lift, query_heads, preferred_element_type=jnp.float32
    )
    query_hidden = (jax.nn.silu(query_gate) * query_lift).astype(jnp.bfloat16)
    return jnp.einsum(
        "hfc,hct->hft", fresh_down, query_hidden, preferred_element_type=jnp.float32
    ).astype(jnp.bfloat16)


def per_device(
    query_states,
    key_states,
    value_states,
    cache_keys,
    cache_values,
    gate_fast,
    lift_fast,
    down_fast,
    token_rates,
):
    features, tok_count = query_states.shape
    edge_cols = jnp.stack(
        [key_states[:, tok_count - WINDOW :], value_states[:, tok_count - WINDOW :]]
    )
    arrived = from_behind(edge_cols, "narrow", 1)
    leading = lax.axis_index("narrow") == 0
    prior_cols = jnp.where(leading, jnp.stack([cache_keys, cache_values]), arrived)
    ext_keys = jnp.concatenate([prior_cols[0], key_states], axis=1)
    ext_values = jnp.concatenate([prior_cols[1], value_states], axis=1)
    if features % HEAD_SIZE == 0:
        attended = attend_local(query_states, ext_keys, ext_values, 0)
    else:
        attended = attend_paired(query_states, ext_keys, ext_values)
    query_fast, key_fast, value_fast = (
        lax.all_to_all(
            lax.all_to_all(query_states, "wide", split_axis=1, concat_axis=0, tiled=True),
            "narrow",
            split_axis=0,
            concat_axis=1,
            tiled=True,
        ),
        lax.all_to_all(
            lax.all_to_all(key_states, "wide", split_axis=1, concat_axis=0, tiled=True),
            "narrow",
            split_axis=0,
            concat_axis=1,
            tiled=True,
        ),
        lax.all_to_all(
            lax.all_to_all(value_states, "wide", split_axis=1, concat_axis=0, tiled=True),
            "narrow",
            split_axis=0,
            concat_axis=1,
            tiled=True,
        ),
    )
    head_count = gate_fast.shape[0]
    wide_count = lax.axis_size("wide")
    narrow_count = lax.axis_size("narrow")
    piece_rows = tok_count // wide_count
    fast_tokens = query_fast.shape[1]
    rate_blocks = token_rates.reshape(token_rates.shape[0], narrow_count, wide_count, piece_rows)
    rates_here = lax.dynamic_slice(
        rate_blocks,
        (lax.axis_index("narrow") * head_count, 0, lax.axis_index("wide"), 0),
        (head_count, narrow_count, 1, piece_rows),
    ).reshape(head_count, fast_tokens)
    query_heads = query_fast.reshape(head_count, FD, fast_tokens)
    key_heads = key_fast.reshape(head_count, FD, fast_tokens)
    value_heads = value_fast.reshape(head_count, FD, fast_tokens)
    recall = fast_group(
        gate_fast, lift_fast, down_fast, query_heads, key_heads, value_heads, rates_here
    )
    recall = recall.reshape(head_count * FD, fast_tokens)
    recalled = lax.all_to_all(
        lax.all_to_all(recall, "narrow", split_axis=1, concat_axis=0, tiled=True),
        "wide",
        split_axis=0,
        concat_axis=1,
        tiled=True,
    )
    return (attended, recalled)


def solution(mesh):
    in_specs = (
        P("wide", "narrow"),
        P("wide", "narrow"),
        P("wide", "narrow"),
        P("wide", None),
        P("wide", None),
        P("narrow", None, None),
        P("narrow", None, None),
        P("narrow", None, None),
        P(),
    )
    out_specs = (P("wide", "narrow"), P("wide", "narrow"))
    return jax.shard_map(
        per_device, mesh=mesh, in_specs=in_specs, out_specs=out_specs, check_vma=False
    )
```

profile of v0, /device:TPU:0, one launch (start us, length us, event | category | flops | bytes accessed | tf_op | source)
XLA Modules:
  0.0 703.5 jit_solution(14772219572014750178)
XLA Ops:
  0.6 4.0 copy.48
  4.6 7.4 %all-to-all-start.4 = ((bf16[512,8,256]{0,2,1:T(8,128)(2,1)}), bf16[512,8,256]{0,2,1:T(8,128)(2,1)}, u32[]{:S(2)}, u32[]{:S(2)}) async-start(bf16[512,8,256]{0,2,1:T(8,128)(2,1)} %bitcast.129), calls=%async_computation.4 | async-start | bytes 4194304 | tf_op jit(solution)/shard_map/all_to_all | solution.py:227
  12.0 2.5 copy.39
  14.5 45.8 %all-to-all-done.4 = bf16[512,8,256]{0,2,1:T(8,128)(2,1)} async-done(((bf16[512,8,256]{0,2,1:T(8,128)(2,1)}), bf16[512,8,256]{0,2,1:T(8,128)(2,1)}, u32[]{:S(2)}, u32[]{:S(2)}) %all-to-all-start.4) | async-done | bytes 2097184 | tf_op jit(solution)/shard_map/all_to_all | solution.py:227
  60.4 4.5 all-to-all-start.2
  64.9 2.6 copy.36
  67.5 45.2 %all-to-all-done.2 = bf16[512,8,256]{0,2,1:T(8,128)(2,1)} async-done(((bf16[512,8,256]{0,2,1:T(8,128)(2,1)}), bf16[512,8,256]{0,2,1:T(8,128)(2,1)}, u32[]{:S(2)}, u32[]{:S(2)}) %all-to-all-start.2) | async-done | bytes 2097184 | tf_op jit(solution)/shard_map/all_to_all | solution.py:234
  112.7 4.4 all-to-all-start
  117.0 3.9 copy.40
  121.0 43.9 %all-to-all-done = bf16[512,8,256]{0,2,1:T(8,128)(2,1)} async-done(((bf16[512,8,256]{0,2,1:T(8,128)(2,1)}), bf16[512,8,256]{0,2,1:T(8,128)(2,1)}, u32[]{:S(2)}, u32[]{:S(2)}) %all-to-all-start) | async-done | bytes 2097184 | tf_op jit(solution)/shard_map/all_to_all | solution.py:241
  164.8 4.5 all-to-all-start.3
  169.3 3.9 copy.37
  173.2 21.8 %all-to-all-done.3 = bf16[4,1024,256]{2,1,0:T(8,128)(2,1)} async-done(((bf16[4,1024,256]{2,1,0:T(8,128)(2,1)}), bf16[4,1024,256]{2,1,0:T(8,128)(2,1)}, u32[]{:S(2)}, u32[]{:S(2)}) %all-to-all-start.3) | async-done | bytes 2097184 | tf_op jit(solution)/shard_map/all_to_all | solution.py:233
  195.0 4.5 all-to-all-start.1
  202.7 3.7 collective-permute-start
  206.4 3.9 copy.49
  210.3 4.6 copy.41
  214.9 3.2 reshape.143
  218.1 7.1 %all-to-all-done.1 = bf16[4,1024,256]{2,1,0:T(8,128)(2,1)} async-done(((bf16[4,1024,256]{2,1,0:T(8,128)(2,1)}), bf16[4,1024,256]{2,1,0:T(8,128)(2,1)}, u32[]{:S(2)}, u32[]{:S(2)}) %all-to-all-start.1) | async-done | bytes 2097184 | tf_op jit(solution)/shard_map/all_to_all | solution.py:240
  225.2 4.6 all-to-all-start.5
  231.9 4.6 copy.38
  236.5 5.8 reshape.145
  242.3 2.6 fusion.47
  248.7 2.9 fusion.28
  251.7 2.7 fusion.29
  254.4 3.3 fusion.31
  257.7 4.6 copy.50
  262.3 3.2 reshape.144
  265.5 250.7 %all-reduce.2 = (bf16[2,512,512]{2,1,0:T(8,128)(2,1)}, bf16[2,512,512]{2,1,0:T(8,128)(2,1)}, bf16[2,512,512]{2,1,0:T(8,128)(2,1)}) all-reduce(f32[2,512,512]{2,1,0:T(8,128)} %fusion.31, f32[2,512,512]{2,1,0:T(8,128)} %fusion.28, f32[2,512,512]{2,1,0:T(8,128)} %fusion.29), channel_id=1, replica_groups=mesh['wide'=8,'narrow'=4] {'wide'}, use_global_device_ids=true, to_apply=%region_8.9 | all-reduce | flops 1572864 | bytes 9437184 | tf_op jit(solution)/shard_map/psum | solution.py:146
  539.8 3.3 fusion.33
  543.1 7.7 %convolution_convert_fusion = bf16[2,512,1024]{2,1,0:T(8,128)(2,1)} fusion(f32[2,512,1024]{2,1,0:T(8,128)} %fusion.33, bf16[2,512,1024]{2,1,0:T(8,128)(2,1)S(1)} %reshape.144, bf16[2,512,512]{2,1,0:T(8,128)(2,1)} %copy-done.16, bf16[2,512,512]{2,1,0:T(8,128)(2,1)} %param.18, bf16[2,512,512]{2,1,0:T(8,128)(2,1)} %copy-done.17, ...), kind=kOutput, calls=%fused_computation.73 | convolution fusion | flops 2160066560 | bytes 12591104 | tf_op jit(solution)/shard_map/hfc,hct->hft/dot_general | solution.py:196
  550.8 3.3 all_to_all.113
  555.7 10.1 %all-to-all-start.6 = ((bf16[1024,4,256]{2,0,1:T(8,128)(2,1)}), bf16[1024,4,256]{2,0,1:T(8,128)(2,1)}, u32[]{:S(2)}, u32[]{:S(2)}) async-start(bf16[1024,4,256]{2,0,1:T(8,128)(2,1)} %copy.53), calls=%async_computation.6 | async-start | bytes 4194304 | tf_op jit(solution)/shard_map/all_to_all | solution.py:267
  572.1 20.6 %all-to-all-done.6 = bf16[1024,4,256]{2,0,1:T(8,128)(2,1)} async-done(((bf16[1024,4,256]{2,0,1:T(8,128)(2,1)}), bf16[1024,4,256]{2,0,1:T(8,128)(2,1)}, u32[]{:S(2)}, u32[]{:S(2)}) %all-to-all-start.6) | async-done | bytes 2097184 | tf_op jit(solution)/shard_map/all_to_all | solution.py:267
  592.7 4.5 all-to-all-start.7
  597.2 97.6 %while.11 = (s32[]{:T(128)}, bf16[4,512,512]{2,1,0:T(8,128)(2,1)}, s32[4]{0:T(128)S(1)}, bf16[512,3072]{1,0:T(8,128)(2,1)}, bf16[512,2048]{1,0:T(8,128)(2,1)}, /...) while((s32[]{:T(128)}, bf16[4,512,512]{2,1,0:T(8,128)(2,1)}, ...), condition=%wide.region_3.4_spmd.clone, body=%wide.region_0.3_spmd.clone.sunk | while | flops 1632110080 | bytes 39340252 | solution.py:77
  598.5 2.1 constant_dynamic-slice_fusion.6
  603.9 10.0 %fusion.108 = (f32[4,512]{1,0:T(4,128)S(1)}, f32[4,512,1536]{2,1,0:T(8,128)}) fusion(pred[512,1536]{1,0:T(8,128)(4,1)} %fusion.107, bf16[4,128,512]{2,1,0:T(8,128)(2,1)} %bitcast.122, bf16[4,128,1536]{2,1,0:T(8,128)(2,1)S(1)} %bitcast.121), kind=kOutput, calls=%fused_computation.107.clone.1 | convolution fusion | flops 817890816 | bytes 15474688 | tf_op jit(solution)/shard_map/while/body/eval_jaxpr/sub | solution.py:70
  613.9 6.9 fusion.109
  628.3 10.0 %fusion.108 = (f32[4,512]{1,0:T(4,128)S(1)}, f32[4,512,1536]{2,1,0:T(8,128)}) fusion(pred[512,1536]{1,0:T(8,128)(4,1)} %fusion.107, bf16[4,128,512]{2,1,0:T(8,128)(2,1)} %bitcast.122, bf16[4,128,1536]{2,1,0:T(8,128)(2,1)S(1)} %bitcast.121), kind=kOutput, calls=%fused_computation.107.clone.1 | convolution fusion | flops 817890816 | bytes 15474688 | tf_op jit(solution)/shard_map/while/body/eval_jaxpr/sub | solution.py:70
  638.3 6.9 fusion.109
  652.7 10.0 %fusion.108 = (f32[4,512]{1,0:T(4,128)S(1)}, f32[4,512,1536]{2,1,0:T(8,128)}) fusion(pred[512,1536]{1,0:T(8,128)(4,1)} %fusion.107, bf16[4,128,512]{2,1,0:T(8,128)(2,1)} %bitcast.122, bf16[4,128,1536]{2,1,0:T(8,128)(2,1)S(1)} %bitcast.121), kind=kOutput, calls=%fused_computation.107.clone.1 | convolution fusion | flops 817890816 | bytes 15474688 | tf_op jit(solution)/shard_map/while/body/eval_jaxpr/sub | solution.py:70
  662.7 6.9 fusion.109
  677.1 10.0 %fusion.108 = (f32[4,512]{1,0:T(4,128)S(1)}, f32[4,512,1536]{2,1,0:T(8,128)}) fusion(pred[512,1536]{1,0:T(8,128)(4,1)} %fusion.107, bf16[4,128,512]{2,1,0:T(8,128)(2,1)} %bitcast.122, bf16[4,128,1536]{2,1,0:T(8,128)(2,1)S(1)} %bitcast.121), kind=kOutput, calls=%fused_computation.107.clone.1 | convolution fusion | flops 817890816 | bytes 15474688 | tf_op jit(solution)/shard_map/while/body/eval_jaxpr/sub | solution.py:70
  687.1 6.9 fusion.109
  694.8 3.2 copy.65
  698.0 2.9 copy.54
  700.9 2.4 copy.55
  (105 shorter events, 65.3 us)
Async XLA Ops:
  0.6 205.8 %copy-start = (f32[8,8192]{1,0:T(8,128)S(1)}, f32[8,8192]{1,0:T(8,128)}, u32[]{:S(2)}) copy-start(f32[8,8192]{1,0:T(8,128)} %param.19) | copy-start | bytes 786436
  4.6 7.4 %copy-start.5 = (bf16[512,2048]{1,0:T(8,128)(2,1)S(1)}, bf16[512,2048]{1,0:T(8,128)(2,1)}, u32[]{:S(2)}) copy-start(bf16[512,2048]{1,0:T(8,128)(2,1)} %param.12) | copy-start | bytes 6291460
  4.6 55.8 %all-to-all-start.4 = ((bf16[512,8,256]{0,2,1:T(8,128)(2,1)}), bf16[512,8,256]{0,2,1:T(8,128)(2,1)}, u32[]{:S(2)}, u32[]{:S(2)}) async-start(bf16[512,8,256]{0,2,1:T(8,128)(2,1)} %bitcast.129), calls=%async_computation.4 | async-start | bytes 4194304 | tf_op jit(solution)/shard_map/all_to_all | solution.py:227
  60.4 4.5 copy-start.3
  60.4 52.3 %all-to-all-start.2 = ((bf16[512,8,256]{0,2,1:T(8,128)(2,1)}), bf16[512,8,256]{0,2,1:T(8,128)(2,1)}, u32[]{:S(2)}, u32[]{:S(2)}) async-start(bf16[512,8,256]{0,2,1:T(8,128)(2,1)} %bitcast.128), calls=%async_computation.2 | async-start | bytes 4194304 | tf_op jit(solution)/shard_map/all_to_all | solution.py:234
  112.7 52.2 %all-to-all-start = ((bf16[512,8,256]{0,2,1:T(8,128)(2,1)}), bf16[512,8,256]{0,2,1:T(8,128)(2,1)}, u32[]{:S(2)}, u32[]{:S(2)}) async-start(bf16[512,8,256]{0,2,1:T(8,128)(2,1)} %bitcast.127), calls=%async_computation | async-start | bytes 4194304 | tf_op jit(solution)/shard_map/all_to_all | solution.py:241
  164.8 30.2 %all-to-all-start.3 = ((bf16[4,1024,256]{2,1,0:T(8,128)(2,1)}), bf16[4,1024,256]{2,1,0:T(8,128)(2,1)}, u32[]{:S(2)}, u32[]{:S(2)}) async-start(bf16[4,1024,256]{2,1,0:T(8,128)(2,1)} %bitcast.126), calls=%async_computation.3 | async-start | bytes 4194304 | tf_op jit(solution)/shard_map/all_to_all | solution.py:233
  195.0 30.2 %all-to-all-start.1 = ((bf16[4,1024,256]{2,1,0:T(8,128)(2,1)}), bf16[4,1024,256]{2,1,0:T(8,128)(2,1)}, u32[]{:S(2)}, u32[]{:S(2)}) async-start(bf16[4,1024,256]{2,1,0:T(8,128)(2,1)} %bitcast.124), calls=%async_computation.1 | async-start | bytes 4194304 | tf_op jit(solution)/shard_map/all_to_all | solution.py:240
  199.5 1.6 copy-start.6
  202.7 363.1 %collective-permute-start = (bf16[2,512,1024]{2,1,0:T(8,128)(2,1)}, bf16[2,512,1024]{2,1,0:T(8,128)(2,1)}, u32[]{:S(2)}, u32[]{:S(2)}) collective-permute-start(bf16[2,512,1024]{2,1,0:T(8,128)(2,1)} %pad_maximum_fusion.2), channel_id=1, source_target_pairs={{0,1},{1,2},{2,3},{4,5},{5,6},{6,7},{8,9},{9,10},{10,11},{12,13},{... | collective-permute-start | bytes 6291464 | tf_op jit(solution)/shard_map/ppermute | solution.py:35
  225.2 32.5 %all-to-all-start.5 = ((bf16[4,1024,256]{2,1,0:T(8,128)(2,1)}), bf16[4,1024,256]{2,1,0:T(8,128)(2,1)}, u32[]{:S(2)}, u32[]{:S(2)}) async-start(bf16[4,1024,256]{2,1,0:T(8,128)(2,1)} %bitcast.125), calls=%async_computation.5 | async-start | bytes 4194304 | tf_op jit(solution)/shard_map/all_to_all | solution.py:226
  242.3 2.6 copy-start.8
  244.9 2.2 copy-start.2
  244.9 2.5 copy-start.12
  524.2 1.2 copy-start.11
  530.0 1.2 copy-start.10
  530.9 7.2 %copy-start.16 = (bf16[2,512,512]{2,1,0:T(8,128)(2,1)}, bf16[2,512,512]{2,1,0:T(8,128)(2,1)S(1)}, u32[]{:S(2)}) copy-start(bf16[2,512,512]{2,1,0:T(8,128)(2,1)S(1)} %add_convert_fusion.4) | copy-start | bytes 3145732
  536.3 1.2 copy-start.9
  537.5 2.2 copy-start.17
  537.5 1.6 copy-start.13
  555.7 10.1 %copy-start.14 = (bf16[512,1024]{1,0:T(8,128)(2,1)S(1)}, bf16[512,1024]{1,0:T(8,128)(2,1)}, u32[]{:S(2)}) copy-start(bf16[512,1024]{1,0:T(8,128)(2,1)} %param.15) | copy-start | bytes 3145732
  555.7 10.1 %copy-start.15 = (bf16[512,1024]{1,0:T(8,128)(2,1)S(1)}, bf16[512,1024]{1,0:T(8,128)(2,1)}, u32[]{:S(2)}) copy-start(bf16[512,1024]{1,0:T(8,128)(2,1)} %param.14) | copy-start | bytes 3145732
  555.7 37.0 %all-to-all-start.6 = ((bf16[1024,4,256]{2,0,1:T(8,128)(2,1)}), bf16[1024,4,256]{2,0,1:T(8,128)(2,1)}, u32[]{:S(2)}, u32[]{:S(2)}) async-start(bf16[1024,4,256]{2,0,1:T(8,128)(2,1)} %copy.53), calls=%async_computation.6 | async-start | bytes 4194304 | tf_op jit(solution)/shard_map/all_to_all | solution.py:267
  566.1 1.6 copy-start.4
  567.7 2.5 copy-start.7
  592.7 105.3 %all-to-all-start.7 = ((bf16[8,512,256]{2,1,0:T(8,128)(2,1)}), bf16[8,512,256]{2,1,0:T(8,128)(2,1)}, u32[]{:S(2)}, u32[]{:S(2)}) async-start(bf16[8,512,256]{2,1,0:T(8,128)(2,1)} %bitcast.23), calls=%async_computation.7 | async-start | bytes 4194304 | tf_op jit(solution)/shard_map/all_to_all | solution.py:266
  700.9 2.4 copy-start.1
where the time goes:
time: 710 us; the launch traced here: 703 us
  blocking collectives  251 us (35%)
  waiting for transfers between devices  184 us (26%)
  matrix products  107 us (15%)
  local copies, waits for them, and re-layouts  89.1 us (13%)
  starting transfers between devices  48.2 us (7%)
  other arithmetic  20 us (3%)
    psum x1, blocking collectives, starting(): lax.psum((grad_gate, grad_lift, grad_down), 'wide')  251 us
    all_to_all x1, waiting for transfers between devices, per_device(): lax.all_to_all(query_states, 'wide', split_axis=1, concat_axis=0, tiled=T...  45.8 us
    all_to_all x1, waiting for transfers between devices, per_device(): lax.all_to_all(key_states, 'wide', split_axis=1, concat_axis=0, tiled=True)  45.2 us
    all_to_all x1, waiting for transfers between devices, per_device(): lax.all_to_all(value_states, 'wide', split_axis=1, concat_axis=0, tiled=T...  43.9 us
    sub x4, matrix products, one_block(): raised = jnp.exp(scores - highest)  40.2 us
    dot_general x4, matrix products, one_block(): jnp.einsum('hdk,hqk->hdq', value_part, weights, preferred_element_type=jn...  27.4 us
    all_to_all x1, waiting for transfers between devices, per_device(): lax.all_to_all(lax.all_to_all(key_states, 'wide', split_axis=1, concat_ax...  21.8 us
    all_to_all x1, waiting for transfers between devices, per_device(): lax.all_to_all(recall, 'narrow', split_axis=1, concat_axis=0, tiled=True)  20.6 us
  transfers between devices with their start and end apart: 9, of which 6 were waited for; matrix products, arithmetic and copies ran while one was open for 28% of the time, Pallas kernels for 0%

commit v1 on v0

--- a/solution.py
+++ b/solution.py
@@ -1,8 +1,11 @@
+import functools
 import math
 
 import jax
 import jax.numpy as jnp
 from jax import lax
+from jax.experimental import pallas as pl
+from jax.experimental.pallas import tpu as pltpu
 from jax.sharding import PartitionSpec as P
 
 FD = 512
@@ -15,6 +18,7 @@
 COEF_A = 3.4445
 COEF_B = -4.775
 COEF_C = 2.0315
+LOG2E = math.log2(math.e)
 
 
 def swapped(array, axis, distance):
@@ -198,7 +202,362 @@
     ).astype(jnp.bfloat16)
 
 
-def per_device(
+def attend_body(flag_ref, q_ref, kp_ref, vp_ref, kc_ref, vc_ref, *rest, block, has_cache, hd, window):
+    if has_cache:
+        ck_ref, cv_ref, o_prev, o_ref, kt_ref, v_ref = rest
+    else:
+        o_ref, kt_ref, v_ref = rest
+    scale = LOG2E / math.sqrt(hd)
+    def place(k, v):
+        kt = k[...].T
+        kt_ref[:window, :hd] = kt
+        kt_ref[:window, hd:] = kt
+        v_ref[:hd, :window] = v[...]
+    if has_cache:
+        @pl.when(flag_ref[0] == 1)
+        def _(): place(ck_ref, cv_ref)
+        @pl.when(flag_ref[0] != 1)
+        def _(): place(kp_ref, vp_ref)
+    else:
+        place(kp_ref, vp_ref)
+    kt = kc_ref[...].T
+    kt_ref[window:, :hd] = kt
+    kt_ref[window:, hd:] = kt
+    v_ref[:hd, window:] = vc_ref[...]
+    v_ref[hd:, :] = jnp.ones((v_ref.shape[0]-hd, 2*window), jnp.bfloat16)
+    rows = lax.broadcasted_iota(jnp.int32, (block, block), 0)
+    cols = lax.broadcasted_iota(jnp.int32, (block, block), 1)
+    first = rows > cols
+    inner = window // block
+    for b in range(window // block):
+        q = q_ref[:, b*block:(b+1)*block].astype(jnp.float32) * scale
+        hi = q.astype(jnp.bfloat16)
+        lo = (q - hi.astype(jnp.float32)).astype(jnp.bfloat16)
+        q2 = jnp.concatenate([hi, lo], axis=0)
+        s = []
+        for j in range(inner + 1):
+            lo_row = (b + j) * block
+            s.append(jnp.dot(kt_ref[lo_row:lo_row+block, :], q2, preferred_element_type=jnp.float32))
+        s[0] = jnp.where(first, s[0], s[inner])
+        top = s[0]
+        for j in range(1, inner): top = jnp.maximum(top, s[j])
+        top = jnp.max(top, axis=0, keepdims=True)
+        p = [jnp.exp2(s[j] - top).astype(jnp.bfloat16) for j in range(inner)]
+        zero = jnp.zeros_like(p[0])
+        parts = [jnp.where(first, p[0], zero)] + p[1:] + [jnp.where(first, zero, p[0])]
+        w = jnp.concatenate(parts, axis=0)
+        o = jnp.dot(v_ref[:, b*block:(b+inner+1)*block], w, preferred_element_type=jnp.float32)
+        o_ref[:, b*block:(b+1)*block] = (o[:hd] * (1.0 / o[hd:hd+1])).astype(jnp.bfloat16)
+
+def attend_late(q, k, v, block=256):
+    f, T = q.shape
+    hd, W = HEAD_SIZE, WINDOW
+    heads, chunks = f//hd, T//W - 1
+    cur = pl.BlockSpec((hd, W), lambda h, c: (h, c+1))
+    prev = pl.BlockSpec((hd, W), lambda h, c: (h, c))
+    return pl.pallas_call(
+        functools.partial(attend_body, block=block, has_cache=False, hd=hd, window=W),
+        out_shape=jax.ShapeDtypeStruct((f, T), jnp.bfloat16),
+        grid=(heads, chunks),
+        in_specs=[pl.BlockSpec(memory_space=pltpu.SMEM), cur, prev, prev, cur, cur],
+        out_specs=cur,
+        scratch_shapes=[pltpu.VMEM((2*W, 2*hd), jnp.bfloat16), pltpu.VMEM((hd+16, 2*W), jnp.bfloat16)],
+        cost_estimate=pl.CostEstimate(flops=heads*chunks*W*W*hd*5, bytes_accessed=5*f*W*2, transcendentals=heads*chunks*W*W),
+        name="attend_late",
+    )(jnp.zeros((1,), jnp.int32), q, k, v, k, v)
+
+def attend_early(flag, q, k, v, prior, ck, cv, out, block=256):
+    f, T = q.shape
+    hd, W = HEAD_SIZE, WINDOW
+    heads = f//hd
+    cur = pl.BlockSpec((hd, W), lambda h: (h, 0))
+    prior_k = pl.BlockSpec((None, hd, W), lambda h: (0, h, 0))
+    prior_v = pl.BlockSpec((None, hd, W), lambda h: (1, h, 0))
+    return pl.pallas_call(
+        functools.partial(attend_body, block=block, has_cache=True, hd=hd, window=W),
+        out_shape=jax.ShapeDtypeStruct((f, T), jnp.bfloat16),
+        grid=(heads,),
+        in_specs=[pl.BlockSpec(memory_space=pltpu.SMEM), cur, prior_k, prior_v, cur, cur, cur, cur, pl.BlockSpec(memory_space=pl.ANY)],
+        out_specs=cur,
+        scratch_shapes=[pltpu.VMEM((2*W, 2*hd), jnp.bfloat16), pltpu.VMEM((hd+16, 2*W), jnp.bfloat16)],
+        input_output_aliases={8: 0},
+        cost_estimate=pl.CostEstimate(flops=heads*W*W*hd*5, bytes_accessed=7*f*W*2, transcendentals=heads*W*W),
+        name="attend_early",
+    )(flag, q, prior, prior, k, v, ck, cv, out)
+
+
+def pick_weights(role, sources, target, sem):
+    for place, source in enumerate(sources):
+
+        @pl.when(role == place)
+        def _(source=source):
+            pltpu.sync_copy(source, target)
+
+
+def terms_body(where_ref, *refs):
+    sources = refs[:-12]
+    (
+        key_ref, value_ref, rate_ref, keep_ref, send_ref,
+        w_ref, turned_ref, hidden_ref, target_ref, back_ref, sem, _,
+    ) = refs[-12:]
+    features, tokens = key_ref.shape
+    hidden_rows = w_ref.shape[1]
+    half = hidden_rows // 2
+    block = min(256, tokens)
+    side = where_ref[1]
+    pick_weights(where_ref[0], sources, w_ref, sem)
+    turned_ref[...] = w_ref[2].T
+    gate_lift = w_ref[0:2].reshape(2 * hidden_rows, features)
+
+    def step(index, carry):
+        at = pl.ds(pl.multiple_of(index * block, block), block)
+        keys = key_ref[:, at]
+        pre = jnp.dot(gate_lift, keys, preferred_element_type=jnp.float32)
+        pre_gate = pre[:hidden_rows]
+        pre_lift = pre[hidden_rows:]
+        rates = rate_ref[pl.ds(where_ref[2], 1), at]
+        target = (-(value_ref[:, at].astype(jnp.float32) * rates)).astype(jnp.bfloat16)
+        back_hidden = jnp.dot(turned_ref[...], target, preferred_element_type=jnp.float32)
+        sigmoid_gate = 0.5 * jnp.tanh(0.5 * pre_gate) + 0.5
+        silu_gate = pre_gate * sigmoid_gate
+        hidden_ref[:, at] = (silu_gate * pre_lift).astype(jnp.bfloat16)
+        target_ref[:, at] = target
+        back_lift = (back_hidden * silu_gate).astype(jnp.bfloat16)
+        slope = sigmoid_gate + silu_gate * (1.0 - sigmoid_gate)
+        back_gate = (back_hidden * pre_lift * slope).astype(jnp.bfloat16)
+        for part in range(2):
+            back_ref[part, :half, at] = back_gate[part * half : (part + 1) * half]
+            back_ref[part, half:, at] = back_lift[part * half : (part + 1) * half]
+        return carry
+
+    lax.fori_loop(0, tokens // block, step, 0, unroll=2)
+    contract = (((1,), (1,)), ((), ()))
+    for part, out_ref in ((1 - side, send_ref), (side, keep_ref)):
+        sums = lax.dot_general(
+            back_ref[part], key_ref[...], contract, preferred_element_type=jnp.float32
+        )
+        out_ref[0] = sums[:half].astype(out_ref.dtype)
+        out_ref[1] = sums[half:].astype(out_ref.dtype)
+        rows = pl.ds(pl.multiple_of(part * half, half), half)
+        out_ref[2] = lax.dot_general(
+            target_ref[rows, :], hidden_ref[...], contract, preferred_element_type=jnp.float32
+        ).astype(out_ref.dtype)
+
+
+def fast_sums(where, sources, keys, values, rates):
+    features, tokens = keys.shape
+    _, hidden_rows, _ = sources[0].shape
+    half = hidden_rows // 2
+    whole = lambda i, where: (0, 0)
+    parts = lambda i, where: (0, 0, 0)
+    return pl.pallas_call(
+        terms_body,
+        out_shape=(
+            jax.ShapeDtypeStruct((3, half, features), jnp.float32),
+            jax.ShapeDtypeStruct((3, half, features), jnp.bfloat16),
+        ),
+        grid_spec=pltpu.PrefetchScalarGridSpec(
+            num_scalar_prefetch=1,
+            grid=(1,),
+            in_specs=[pl.BlockSpec(memory_space=pl.ANY)] * len(sources)
+            + [
+                pl.BlockSpec((features, tokens), whole),
+                pl.BlockSpec((features, tokens), whole),
+                pl.BlockSpec((rates.shape[0], tokens), lambda i, where: (0, where[3])),
+            ],
+            out_specs=(
+                pl.BlockSpec((3, half, features), parts),
+                pl.BlockSpec((3, half, features), parts),
+            ),
+            scratch_shapes=[
+                pltpu.VMEM((3, hidden_rows, features), jnp.bfloat16),
+                pltpu.VMEM((hidden_rows, features), jnp.bfloat16),
+                pltpu.VMEM((hidden_rows, tokens), jnp.bfloat16),
+                pltpu.VMEM((features, tokens), jnp.bfloat16),
+                pltpu.VMEM((2, hidden_rows, tokens), jnp.bfloat16),
+                pltpu.SemaphoreType.DMA(()),
+                pltpu.SMEM((1,), jnp.int32),
+            ],
+        ),
+        cost_estimate=pl.CostEstimate(
+            flops=12 * hidden_rows * features * tokens,
+            bytes_accessed=4 * features * tokens + 6 * hidden_rows * features,
+            transcendentals=hidden_rows * tokens,
+        ),
+        name="fast_sums",
+    )(where, *sources, keys, values, rates)
+
+
+def recall_body(where_ref, *refs):
+    sources = refs[:-7]
+    mine_ref, other_ref, query_ref, out_ref, w_ref, fresh_ref, sem = refs[-7:]
+    half = mine_ref.shape[1]
+
+    @pl.when(pl.program_id(0) == 0)
+    def _():
+        side = where_ref[1]
+        pick_weights(where_ref[0], sources, w_ref, sem)
+        rows_mine = pl.ds(pl.multiple_of(side * half, half), half)
+        rows_other = pl.ds(pl.multiple_of((1 - side) * half, half), half)
+        fresh_ref[:, rows_mine, :] = mine_ref[...]
+        fresh_ref[:, rows_other, :] = other_ref[...]
+        current = []
+        for i in range(3):
+            widened = fresh_ref[i].astype(jnp.float32)
+            total = jnp.sum(jnp.sum(widened * widened, axis=0, keepdims=True), axis=1, keepdims=True)
+            current.append((widened / jnp.sqrt(total + EPS)).astype(jnp.bfloat16))
+        for _ in range(NS_ITERS):
+            gram = [
+                lax.dot_general(
+                    x, x, (((0,), (0,)), ((), ())), preferred_element_type=jnp.float32
+                ).astype(jnp.bfloat16)
+                for x in current
+            ]
+            lifted = [
+                jnp.dot(x, g, preferred_element_type=jnp.float32).astype(jnp.bfloat16)
+                for x, g in zip(current, gram)
+            ]
+            current = [
+                (
+                    COEF_A * x.astype(jnp.float32)
+                    + COEF_B * y.astype(jnp.float32)
+                    + COEF_C * jnp.dot(y, g, preferred_element_type=jnp.float32)
+                ).astype(jnp.bfloat16)
+                for x, y, g in zip(current, lifted, gram)
+            ]
+        for i in range(3):
+            initial = w_ref[i].astype(jnp.float32)
+            moved = initial - current[i].astype(jnp.float32)
+            wanted = jnp.mean(jnp.square(initial), axis=-1, keepdims=True) + EPS
+            present = jnp.mean(jnp.square(moved), axis=-1, keepdims=True) + EPS
+            fresh_ref[i] = (moved * (jnp.sqrt(wanted) / jnp.sqrt(present))).astype(jnp.bfloat16)
+
+    hidden_rows, features = fresh_ref.shape[1:]
+    pre = jnp.dot(
+        fresh_ref[0:2].reshape(2 * hidden_rows, features),
+        query_ref[...],
+        preferred_element_type=jnp.float32,
+    )
+    gate = pre[:hidden_rows]
+    hidden = (gate * (0.5 * jnp.tanh(0.5 * gate) + 0.5) * pre[hidden_rows:]).astype(jnp.bfloat16)
+    out_ref[...] = jnp.dot(fresh_ref[2], hidden, preferred_element_type=jnp.float32).astype(
+        jnp.bfloat16
+    )
+
+
+def fast_recall(where, sources, mine, other, queries):
+    features, tokens = queries.shape
+    _, hidden_rows, _ = sources[0].shape
+    block = min(512, tokens)
+    half = hidden_rows // 2
+    parts = lambda i, where: (0, 0, 0)
+    piece = pl.BlockSpec((features, block), lambda i, where: (0, i))
+    return pl.pallas_call(
+        recall_body,
+        out_shape=jax.ShapeDtypeStruct((features, tokens), jnp.bfloat16),
+        grid_spec=pltpu.PrefetchScalarGridSpec(
+            num_scalar_prefetch=1,
+            grid=(tokens // block,),
+            in_specs=[pl.BlockSpec(memory_space=pl.ANY)] * len(sources)
+            + [
+                pl.BlockSpec((3, half, features), parts),
+                pl.BlockSpec((3, half, features), parts),
+                piece,
+            ],
+            out_specs=piece,
+            scratch_shapes=[
+                pltpu.VMEM((3, hidden_rows, features), jnp.bfloat16),
+                pltpu.VMEM((3, hidden_rows, features), jnp.bfloat16),
+                pltpu.SemaphoreType.DMA(()),
+            ],
+        ),
+        cost_estimate=pl.CostEstimate(
+            flops=6 * hidden_rows * features * tokens + 36 * NS_ITERS * hidden_rows * features**2 // 2,
+            bytes_accessed=4 * features * tokens + 12 * hidden_rows * features,
+            transcendentals=hidden_rows * tokens,
+        ),
+        name="fast_recall",
+    )(where, *sources, mine, other, queries)
+
+
+def in_place(query_states, key_states, value_states, cache_keys, cache_values, gate_fast, *rest):
+    features, tok_count = query_states.shape
+    narrow_count = lax.axis_size("narrow")
+    return (
+        features == FD
+        and gate_fast.shape[1:] == (FD, FD)
+        and features % HEAD_SIZE == 0
+        and tok_count % WINDOW == 0
+        and tok_count >= 2 * WINDOW
+        and narrow_count >= 2
+        and narrow_count & (narrow_count - 1) == 0
+    )
+
+
+def in_place_plan(
+    query_states,
+    key_states,
+    value_states,
+    cache_keys,
+    cache_values,
+    gate_fast,
+    lift_fast,
+    down_fast,
+    token_rates,
+):
+    tok_count = query_states.shape[1]
+    wide_count = lax.axis_size("wide")
+    narrow_count = lax.axis_size("narrow")
+    owned = gate_fast.shape[0]
+    wide_at = lax.axis_index("wide")
+    narrow_at = lax.axis_index("narrow")
+    role = narrow_at ^ (wide_at // owned)
+    where = jnp.stack([role, narrow_at % 2, wide_at, narrow_at]).astype(jnp.int32)
+
+    def sent(value, step):
+        source = step & (step - 1)
+        pairs = []
+        for wide in range(wide_count):
+            owner = wide // owned
+            pairs.append(
+                (wide * narrow_count + (owner ^ source), wide * narrow_count + (owner ^ step))
+            )
+        return lax.ppermute(value, ("wide", "narrow"), pairs)
+
+    local = wide_at % owned
+    sources = [
+        jnp.stack(
+            [
+                lax.dynamic_index_in_dim(weight, local, 0, keepdims=False)
+                for weight in (gate_fast, lift_fast, down_fast)
+            ]
+        )
+    ]
+    for step in range(1, narrow_count):
+        sources.append(sent(sources[step & (step - 1)], step))
+    edge_cols = jnp.stack(
+        [key_states[:, tok_count - WINDOW :], value_states[:, tok_count - WINDOW :]]
+    )
+    arrived = from_behind(edge_cols, "narrow", 1)
+    late = attend_late(query_states, key_states, value_states)
+    keep, send = fast_sums(where, sources, key_states, value_states, token_rates)
+    total = keep + swapped(send, "narrow", 0).astype(jnp.float32)
+    distance = 1
+    while 1 << distance < narrow_count:
+        other = swapped(total.astype(jnp.bfloat16), "narrow", distance)
+        total = total + other.astype(jnp.float32)
+        distance += 1
+    mine = stored(total)
+    theirs = swapped(mine, "narrow", 0)
+    leading = (narrow_at == 0).astype(jnp.int32).reshape(1)
+    attended = attend_early(
+        leading, query_states, key_states, value_states, arrived, cache_keys, cache_values, late
+    )
+    recalled = fast_recall(where, sources, mine, theirs, query_states)
+    return (attended, recalled)
+
+
+def spread_plan(
     query_states,
     key_states,
     value_states,
@@ -273,6 +632,12 @@
     return (attended, recalled)
 
 
+def per_device(*arrays):
+    if in_place(*arrays):
+        return in_place_plan(*arrays)
+    return spread_plan(*arrays)
+
+
 def solution(mesh):
     in_specs = (
         P("wide", "narrow"),

time: 710 us -> 138 us (0.19)
  blocking collectives: 251 us -> 0 us
  waiting for transfers between devices: 184 us -> 32.6 us
  matrix products: 107 us -> 0 us
  local copies, waits for them, and re-layouts: 89.1 us -> 5.24 us
  Pallas kernels: 0 us -> 55.1 us
  other arithmetic: 20 us -> 4.97 us
  starting transfers between devices: 48.2 us -> 39.1 us
    psum x1 -> x0, blocking collectives: 251 us -> none  [starting(): lax.psum((grad_gate, grad_lift, grad_down), 'wide')]
    all_to_all x8 -> x0, waiting for transfers between devices: 184 us -> none  [the longest x1 45.8 us: per_device(): lax.all_to_all(query_states, 'wide', split_axis=1, concat_axis=0, tiled=T...]
    dot_general x30 -> x0, matrix products: 66.9 us -> none  [the longest x4 27.4 us: one_block(): jnp.einsum('hdk,hqk->hdq', value_part, weights, preferred_element_type=jn...]
    pallas_call x0 -> x4, Pallas kernels: none -> 55.1 us  [the longest x1 15.5 us: fast_recall(): pl.pallas_call(recall_body, out_shape=jax.ShapeDtypeStruct((features, tok...]
    all_to_all x8 -> x0, starting transfers between devices: 44.4 us -> none  [the longest x1 10.1 us: per_device(): lax.all_to_all(recall, 'narrow', split_axis=1, concat_axis=0, tiled=True)]
    sub x4 -> x0, matrix products: 40.2 us -> none  [one_block(): raised = jnp.exp(scores - highest)]
    ppermute x0 -> x6, starting transfers between devices: none -> 36.6 us  [the longest x3 26.3 us: swapped(): lax.ppermute(array, axis, [(i, i ^ 1 << distance) for i in range(lax.axis...]
    ppermute x0 -> x6, waiting for transfers between devices: none -> 32.6 us  [the longest x3 17.9 us: swapped(): lax.ppermute(array, axis, [(i, i ^ 1 << distance) for i in range(lax.axis...]
  transfers between devices with their start and end apart: 9 -> 7, of which waited for: 6 -> 2; matrix products, arithmetic and copies ran while one was open for 28% -> 4% of each run, Pallas kernels for 0% -> 19%
where the time goes in v1:
time: 138 us
  Pallas kernels  55.1 us (40%)
  starting transfers between devices  39.1 us (28%)
  waiting for transfers between devices  32.6 us (24%)
  local copies, waits for them, and re-layouts  5.24 us (4%)
  other arithmetic  4.97 us (4%)
    ppermute x3, starting transfers between devices, swapped(): lax.ppermute(array, axis, [(i, i ^ 1 << distance) for i in range(lax.axis...  26.3 us
    ppermute x3, waiting for transfers between devices, swapped(): lax.ppermute(array, axis, [(i, i ^ 1 << distance) for i in range(lax.axis...  17.9 us
    pallas_call x1, Pallas kernels, fast_recall(): pl.pallas_call(recall_body, out_shape=jax.ShapeDtypeStruct((features, tok...  15.5 us
    ppermute x3, waiting for transfers between devices, sent(): return lax.ppermute(value, ('wide', 'narrow'), pairs)  14.6 us
    pallas_call x1, Pallas kernels, fast_sums(): pl.pallas_call(terms_body, out_shape=(jax.ShapeDtypeStruct((3, half, feat...  13.4 us
    pallas_call x1, Pallas kernels, attend_early(): pl.pallas_call(functools.partial(attend_body, block=block, has_cache=True...  13.4 us
    pallas_call x1, Pallas kernels, attend_late(): pl.pallas_call(functools.partial(attend_body, block=block, has_cache=Fals...  12.8 us
    ppermute x3, starting transfers between devices, sent(): return lax.ppermute(value, ('wide', 'narrow'), pairs)  10.3 us
  transfers between devices with their start and end apart: 7, of which 2 were waited for; matrix products, arithmetic and copies ran while one was open for 4% of the time, Pallas kernels for 19%

profile of v1, /device:TPU:0, one launch (start us, length us, event | category | flops | bytes accessed | tf_op | source)
XLA Modules:
  0.0 137.9 jit_solution(12541119347524830867)
XLA Ops:
  0.6 0.0 copy-start
  0.7 1.2 copy-done
  1.9 1.3 constant_dynamic-slice_fusion
  3.2 1.3 pad_maximum_fusion.1.refs_0_
  4.5 6.1 %collective-permute-start.2 = (bf16[3,512,512]{2,1,0:T(8,128)(2,1)}, bf16[3,512,512]{2,1,0:T(8,128)(2,1)}, u32[]{:S(2)}, u32[]{:S(2)}) collective-permute-start(bf16[3,512,512]{2,1,0:T(8,128)(2,1)} %pad_maximum_fusion.1.refs_0_), channel_id=1, source_target_pairs={{0,2},{4,6},{9,11},{13,15},{18,16},{22,20},{27,25},{31,29}} | collective-permute-start | bytes 4718600 | tf_op jit(solution)/shard_map/ppermute | solution.py:525
  10.6 2.4 %collective-permute-start.1 = (bf16[3,512,512]{2,1,0:T(8,128)(2,1)}, bf16[3,512,512]{2,1,0:T(8,128)(2,1)}, u32[]{:S(2)}, u32[]{:S(2)}) collective-permute-start(bf16[3,512,512]{2,1,0:T(8,128)(2,1)} %pad_maximum_fusion.1.refs_0_), channel_id=1, source_target_pairs={{0,1},{4,5},{9,8},{13,12},{18,19},{22,23},{27,26},{31,30}} | collective-permute-start | bytes 4718600 | tf_op jit(solution)/shard_map/ppermute | solution.py:525
  13.0 14.6 %collective-permute-done.2.refs_2_ = bf16[3,512,512]{2,1,0:T(8,128)(2,1)} collective-permute-done((bf16[3,512,512]{2,1,0:T(8,128)(2,1)}, bf16[3,512,512]{2,1,0:T(8,128)(2,1)}, u32[]{:S(2)}, u32[]{:S(2)}) %collective-permute-start.2) | collective-permute-done | bytes 1572896 | tf_op jit(solution)/shard_map/ppermute | solution.py:525
  27.6 1.8 %collective-permute-start.3 = (bf16[3,512,512]{2,1,0:T(8,128)(2,1)}, bf16[3,512,512]{2,1,0:T(8,128)(2,1)}, u32[]{:S(2)}, u32[]{:S(2)}) collective-permute-start(bf16[3,512,512]{2,1,0:T(8,128)(2,1)} %collective-permute-done.2.refs_2_), channel_id=1, source_target_pairs={{2,3},{6,7},{11,10},{15,14},{16,17},{20,21},{25,24},{29,28}} | collective-permute-start | bytes 4718600 | tf_op jit(solution)/shard_map/ppermute | solution.py:525
  29.5 0.6 pad_add_fusion.where_ref
  30.1 0.0 copy-start.1
  30.1 0.0 collective-permute-done.1.refs_1_
  30.1 0.0 collective-permute-done.3.refs_3_
  30.1 13.4 %fast_sums.1 = (f32[3,256,512]{2,1,0:T(8,128)}, bf16[3,256,512]{2,1,0:T(8,128)(2,1)}) custom-call(s32[4]{0:T(128)} %pad_add_fusion.where_ref, bf16[3,512,512]{2,1,0:T(8,128)(2,1)} %pad_maximum_fusion.1.refs_0_, bf16[3,512,512]{2,1,0:T(8,128)(2,1)} %collective-permute-done.1.refs_1_, bf16[3,512,512]{2,1,0:T(8,128)(2,1)} %collective-permute-done.2.refs_2_, ...), custom_call_target="tpu_custom_call" | custom-call | flops 6442450944 | bytes 5767168 | tf_op jit(solution)/shard_map/fast_sums/pallas_call | solution.py:353
  43.5 0.1 collective-permute-start.4
  43.6 0.0 copy-done.1
  43.6 1.4 %slice_bitcast_fusion = (bf16[1,512,1024]{2,1,0:T(8,128)(2,1)S(1)}, bf16[1,512,1024]{2,1,0:T(8,128)(2,1)S(1)}) fusion(bf16[512,2048]{1,0:T(8,128)(2,1)S(1)} %copy-done.1, bf16[512,2048]{1,0:T(8,128)(2,1)} %refs_4_.1), kind=kLoop, calls=%fused_computation.5 | loop fusion | bytes 4194304 | tf_op jit(solution)/shard_map/stack | solution.py:538
  45.0 0.0 copy-start.3
  45.0 1.5 %pad_maximum_fusion = bf16[2,512,1024]{2,1,0:T(8,128)(2,1)} fusion(bf16[1,512,1024]{2,1,0:T(8,128)(2,1)S(1)} %get-tuple-element.6, bf16[1,512,1024]{2,1,0:T(8,128)(2,1)S(1)} %get-tuple-element.7), kind=kLoop, calls=%fused_computation | loop fusion | flops 1048576 | bytes 4194304 | tf_op jit(solution)/shard_map/stack | solution.py:538
  46.5 2.5 %collective-permute-start = (bf16[2,512,1024]{2,1,0:T(8,128)(2,1)}, bf16[2,512,1024]{2,1,0:T(8,128)(2,1)S(1)}, u32[]{:S(2)}, u32[]{:S(2)}) collective-permute-start(bf16[2,512,1024]{2,1,0:T(8,128)(2,1)} %pad_maximum_fusion), channel_id=1, source_target_pairs={{0,1},{1,2},{2,3},{4,5},{5,6},{6,7},{8,9},{9,10},{10,11},{12,13},{... | collective-permute-start | bytes 6291464 | tf_op jit(solution)/shard_map/ppermute | solution.py:39
  49.0 0.0 collective-permute-done.4
  49.0 0.0 copy-done.3
  49.0 0.3 fusion
  49.3 4.5 %collective-permute-start.5 = (bf16[3,256,512]{2,1,0:T(8,128)(2,1)S(1)}, bf16[3,256,512]{2,1,0:T(8,128)(2,1)S(1)}, u32[]{:S(2)}, u32[]{:S(2)}) collective-permute-start(bf16[3,256,512]{2,1,0:T(8,128)(2,1)S(1)} %fusion), channel_id=1, source_target_pairs={{0,2},{1,3},{2,0},{3,1},{4,6},{5,7},{6,4},{7,5},{8,10},{9,11},{10,... | collective-permute-start | bytes 2359304 | tf_op jit(solution)/shard_map/ppermute | solution.py:25
  53.8 17.9 %collective-permute-done.5 = bf16[3,256,512]{2,1,0:T(8,128)(2,1)S(1)} collective-permute-done((bf16[3,256,512]{2,1,0:T(8,128)(2,1)S(1)}, bf16[3,256,512]{2,1,0:T(8,128)(2,1)S(1)}, u32[]{:S(2)}, u32[]{:S(2)}) %collective-permute-start.5) | collective-permute-done | bytes 786464 | tf_op jit(solution)/shard_map/ppermute | solution.py:25
  71.8 1.3 add_convert_fusion.refs_4_
  73.0 21.7 %collective-permute-start.6 = (bf16[3,256,512]{2,1,0:T(8,128)(2,1)}, bf16[3,256,512]{2,1,0:T(8,128)(2,1)}, u32[]{:S(2)}, u32[]{:S(2)}) collective-permute-start(bf16[3,256,512]{2,1,0:T(8,128)(2,1)} %add_convert_fusion.refs_4_), channel_id=1, source_target_pairs={{0,1},{1,0},{2,3},{3,2},{4,5},{5,4},{6,7},{7,6},{8,9},{9,8},{10,11... | collective-permute-start | bytes 2359304 | tf_op jit(solution)/shard_map/ppermute | solution.py:25
  94.7 12.8 %attend_late.1.rest_2_ = bf16[512,2048]{1,0:T(8,128)(2,1)} custom-call(s32[1]{0:T(128)} %constant.42.clone.1.flag_ref, bf16[512,2048]{1,0:T(8,128)(2,1)} %refs_6_.3, bf16[512,2048]{1,0:T(8,128)(2,1)} %refs_4_.1, bf16[512,2048]{1,0:T(8,128)(2,1)} %refs_5_.1, bf16[512,2048]{1,0:T(8,128)(2,1)} %refs_4_.1, bf16[512,2048]{1,0:T(8,128)(2,1)} %refs_5_.1), custom_call_target="tpu_custom_call" | custom-call | flops 2684354560 | bytes 5242880 | tf_op jit(solution)/shard_map/attend_late/pallas_call | solution.py:258
  107.5 0.0 collective-permute-done.kp_ref.vp_ref
  107.5 0.0 copy-start.2
  107.5 1.3 copy-done.2
  108.8 13.4 %attend_early.1 = bf16[512,2048]{1,0:T(8,128)(2,1)} custom-call(s32[1]{0:T(128)} %bitcast.flag_ref, bf16[512,2048]{1,0:T(8,128)(2,1)} %refs_6_.3, bf16[2,512,1024]{2,1,0:T(8,128)(2,1)} %copy-done.2, bf16[2,512,1024]{2,1,0:T(8,128)(2,1)} %copy-done.2, bf16[512,2048]{1,0:T(8,128)(2,1)} %refs_4_.1, ...), custom_call_target="tpu_custom_call", output_to_operand_aliasing={{}: (8, {})} | custom-call | flops 2684354560 | bytes 7340032 | tf_op jit(solution)/shard_map/attend_early/pallas_call | solution.py:276
  122.2 0.0 collective-permute-done.6.refs_5_
  122.2 15.5 %fast_recall.1 = bf16[512,2048]{1,0:T(8,128)(2,1)} custom-call(s32[4]{0:T(128)} %pad_add_fusion.where_ref, bf16[3,512,512]{2,1,0:T(8,128)(2,1)} %pad_maximum_fusion.1.refs_0_, bf16[3,512,512]{2,1,0:T(8,128)(2,1)} %collective-permute-done.1.refs_1_, bf16[3,512,512]{2,1,0:T(8,128)(2,1)} %collective-permute-done.2.refs_2_, ...), custom_call_target="tpu_custom_call" | custom-call | flops 8053063680 | bytes 7340032 | tf_op jit(solution)/shard_map/fast_recall/pallas_call | solution.py:455
  (1 shorter events, 0.0 us)
Async XLA Ops:
  0.6 1.2 copy-start
  4.5 23.1 %collective-permute-start.2 = (bf16[3,512,512]{2,1,0:T(8,128)(2,1)}, bf16[3,512,512]{2,1,0:T(8,128)(2,1)}, u32[]{:S(2)}, u32[]{:S(2)}) collective-permute-start(bf16[3,512,512]{2,1,0:T(8,128)(2,1)} %pad_maximum_fusion.1.refs_0_), channel_id=1, source_target_pairs={{0,2},{4,6},{9,11},{13,15},{18,16},{22,20},{27,25},{31,29}} | collective-permute-start | bytes 4718600 | tf_op jit(solution)/shard_map/ppermute | solution.py:525
  10.6 19.5 %collective-permute-start.1 = (bf16[3,512,512]{2,1,0:T(8,128)(2,1)}, bf16[3,512,512]{2,1,0:T(8,128)(2,1)}, u32[]{:S(2)}, u32[]{:S(2)}) collective-permute-start(bf16[3,512,512]{2,1,0:T(8,128)(2,1)} %pad_maximum_fusion.1.refs_0_), channel_id=1, source_target_pairs={{0,1},{4,5},{9,8},{13,12},{18,19},{22,23},{27,26},{31,30}} | collective-permute-start | bytes 4718600 | tf_op jit(solution)/shard_map/ppermute | solution.py:525
  27.6 2.4 %collective-permute-start.3 = (bf16[3,512,512]{2,1,0:T(8,128)(2,1)}, bf16[3,512,512]{2,1,0:T(8,128)(2,1)}, u32[]{:S(2)}, u32[]{:S(2)}) collective-permute-start(bf16[3,512,512]{2,1,0:T(8,128)(2,1)} %collective-permute-done.2.refs_2_), channel_id=1, source_target_pairs={{2,3},{6,7},{11,10},{15,14},{16,17},{20,21},{25,24},{29,28}} | collective-permute-start | bytes 4718600 | tf_op jit(solution)/shard_map/ppermute | solution.py:525
  30.1 13.5 %copy-start.1 = (bf16[512,2048]{1,0:T(8,128)(2,1)S(1)}, bf16[512,2048]{1,0:T(8,128)(2,1)}, u32[]{:S(2)}) copy-start(bf16[512,2048]{1,0:T(8,128)(2,1)} %refs_5_.1) | copy-start | bytes 6291460
  43.5 5.5 %collective-permute-start.4 = (bf16[3,256,512]{2,1,0:T(8,128)(2,1)}, bf16[3,256,512]{2,1,0:T(8,128)(2,1)S(1)}, u32[]{:S(2)}, u32[]{:S(2)}) collective-permute-start(bf16[3,256,512]{2,1,0:T(8,128)(2,1)} %get-tuple-element.5), channel_id=1, source_target_pairs={{0,1},{1,0},{2,3},{3,2},{4,5},{5,4},{6,7},{7,6},{8,9},{9,8},{10,11... | collective-permute-start | bytes 2359304 | tf_op jit(solution)/shard_map/ppermute | solution.py:25
  45.0 4.0 %copy-start.3 = (f32[3,256,512]{2,1,0:T(8,128)S(1)}, f32[3,256,512]{2,1,0:T(8,128)}, u32[]{:S(2)}) copy-start(f32[3,256,512]{2,1,0:T(8,128)} %get-tuple-element.4) | copy-start | bytes 4718596
  46.5 61.0 %collective-permute-start = (bf16[2,512,1024]{2,1,0:T(8,128)(2,1)}, bf16[2,512,1024]{2,1,0:T(8,128)(2,1)S(1)}, u32[]{:S(2)}, u32[]{:S(2)}) collective-permute-start(bf16[2,512,1024]{2,1,0:T(8,128)(2,1)} %pad_maximum_fusion), channel_id=1, source_target_pairs={{0,1},{1,2},{2,3},{4,5},{5,6},{6,7},{8,9},{9,10},{10,11},{12,13},{... | collective-permute-start | bytes 6291464 | tf_op jit(solution)/shard_map/ppermute | solution.py:39
  49.3 22.4 %collective-permute-start.5 = (bf16[3,256,512]{2,1,0:T(8,128)(2,1)S(1)}, bf16[3,256,512]{2,1,0:T(8,128)(2,1)S(1)}, u32[]{:S(2)}, u32[]{:S(2)}) collective-permute-start(bf16[3,256,512]{2,1,0:T(8,128)(2,1)S(1)} %fusion), channel_id=1, source_target_pairs={{0,2},{1,3},{2,0},{3,1},{4,6},{5,7},{6,4},{7,5},{8,10},{9,11},{10,... | collective-permute-start | bytes 2359304 | tf_op jit(solution)/shard_map/ppermute | solution.py:25
  73.0 49.2 %collective-permute-start.6 = (bf16[3,256,512]{2,1,0:T(8,128)(2,1)}, bf16[3,256,512]{2,1,0:T(8,128)(2,1)}, u32[]{:S(2)}, u32[]{:S(2)}) collective-permute-start(bf16[3,256,512]{2,1,0:T(8,128)(2,1)} %add_convert_fusion.refs_4_), channel_id=1, source_target_pairs={{0,1},{1,0},{2,3},{3,2},{4,5},{5,4},{6,7},{7,6},{8,9},{9,8},{10,11... | collective-permute-start | bytes 2359304 | tf_op jit(solution)/shard_map/ppermute | solution.py:25
  107.5 1.3 copy-start.2

commit v2 on v1

--- a/solution.py
+++ b/solution.py
@@ -7,6 +7,7 @@
 from jax.experimental import pallas as pl
 from jax.experimental.pallas import tpu as pltpu
 from jax.sharding import PartitionSpec as P
+
 
 FD = 512
 HEAD_SIZE = 128
@@ -156,7 +157,7 @@
 
 
 def orthogonal(current):
-    for sweep_index in range(NS_ITERS):
+    for _ in range(NS_ITERS):
         gram_mat = jnp.einsum(
             "hrc,hrd->hcd", current, current, preferred_element_type=jnp.float32
         ).astype(jnp.bfloat16)
@@ -204,18 +205,21 @@
 
 def attend_body(flag_ref, q_ref, kp_ref, vp_ref, kc_ref, vc_ref, *rest, block, has_cache, hd, window):
     if has_cache:
-        ck_ref, cv_ref, o_prev, o_ref, kt_ref, v_ref = rest
+        ck_ref, cv_ref, _, o_ref, kt_ref, v_ref = rest
     else:
         o_ref, kt_ref, v_ref = rest
     scale = LOG2E / math.sqrt(hd)
+
     def place(k, v):
         kt = k[...].T
         kt_ref[:window, :hd] = kt
         kt_ref[:window, hd:] = kt
         v_ref[:hd, :window] = v[...]
+
     if has_cache:
         @pl.when(flag_ref[0] == 1)
         def _(): place(ck_ref, cv_ref)
+
         @pl.when(flag_ref[0] != 1)
         def _(): place(kp_ref, vp_ref)
     else:
@@ -249,6 +253,7 @@
         o = jnp.dot(v_ref[:, b*block:(b+inner+1)*block], w, preferred_element_type=jnp.float32)
         o_ref[:, b*block:(b+1)*block] = (o[:hd] * (1.0 / o[hd:hd+1])).astype(jnp.bfloat16)
 
+
 def attend_late(q, k, v, block=256):
     f, T = q.shape
     hd, W = HEAD_SIZE, WINDOW
@@ -265,6 +270,7 @@
         cost_estimate=pl.CostEstimate(flops=heads*chunks*W*W*hd*5, bytes_accessed=5*f*W*2, transcendentals=heads*chunks*W*W),
         name="attend_late",
     )(jnp.zeros((1,), jnp.int32), q, k, v, k, v)
+
 
 def attend_early(flag, q, k, v, prior, ck, cv, out, block=256):
     f, T = q.shape
@@ -286,124 +292,198 @@
     )(flag, q, prior, prior, k, v, ck, cv, out)
 
 
-def pick_weights(role, sources, target, sem):
+def in_hbm(array):
+    return pltpu.with_memory_space_constraint(array, pltpu.HBM)
+
+
+def prepare_body(where_ref, gate_ref, lift_ref, down_ref, own_ref, other_ref, w_ref, sem):
+    local = where_ref[4]
+    copies = [
+        pltpu.make_async_copy(source.at[local], w_ref.at[place], sem.at[place])
+        for place, source in enumerate((down_ref, gate_ref, lift_ref))
+    ]
+    for copy in copies:
+        copy.start()
+    half = own_ref.shape[1]
+    side = where_ref[1]
+    copies[0].wait()
+    w_ref[0] = w_ref[0].T
+    copies[1].wait()
+    copies[2].wait()
+    for out_ref, part in ((own_ref, side), (other_ref, 1 - side)):
+        rows = pl.ds(pl.multiple_of(part * half, half), half)
+        out_ref[0] = w_ref[1, rows, :]
+        out_ref[1] = w_ref[2, rows, :]
+        out_ref[2] = w_ref[0, rows, :]
+
+
+def prepare(where, gate_fast, lift_fast, down_fast):
+    _, hidden_rows, features = gate_fast.shape
+    shape = (3, hidden_rows // 2, features)
+    return pl.pallas_call(
+        prepare_body,
+        out_shape=(jax.ShapeDtypeStruct(shape, jnp.bfloat16),) * 2,
+        in_specs=[pl.BlockSpec(memory_space=pltpu.SMEM)] + [pl.BlockSpec(memory_space=pl.ANY)] * 3,
+        out_specs=(pl.BlockSpec(memory_space=pltpu.VMEM),) * 2,
+        scratch_shapes=[
+            pltpu.VMEM((3, hidden_rows, features), jnp.bfloat16),
+            pltpu.SemaphoreType.DMA((3,)),
+        ],
+        cost_estimate=pl.CostEstimate(
+            flops=0, bytes_accessed=12 * hidden_rows * features, transcendentals=0
+        ),
+        name="prepare",
+    )(where, gate_fast, lift_fast, down_fast)
+
+
+def edges_body(key_ref, value_ref, out_ref):
+    out_ref[0] = key_ref[...]
+    out_ref[1] = value_ref[...]
+
+
+def edges(keys, values):
+    features, tokens = keys.shape
+    last = tokens // WINDOW - 1
+    rows = HEAD_SIZE
+    piece = pl.BlockSpec((rows, WINDOW), lambda i: (i, last))
+    return pl.pallas_call(
+        edges_body,
+        out_shape=jax.ShapeDtypeStruct((2, features, WINDOW), jnp.bfloat16),
+        grid=(features // rows,),
+        in_specs=[piece, piece],
+        out_specs=pl.BlockSpec((2, rows, WINDOW), lambda i: (0, i, 0)),
+        cost_estimate=pl.CostEstimate(
+            flops=0, bytes_accessed=8 * features * WINDOW, transcendentals=0
+        ),
+        name="edges",
+    )(keys, values)
+
+
+def sums_body(where_ref, *refs):
+    sources = refs[:-15]
+    (
+        key_ref, value_ref, pair_key_ref, pair_value_ref, rate_ref,
+        keep_ref, send_ref, pack_ref,
+        keys_ref, values_ref, hidden_ref, target_ref, back_ref, sem, sem_in,
+    ) = refs[-15:]
+    features, tokens = key_ref.shape
+    half = pack_ref.shape[1]
+    block = min(512, tokens)
+    count = tokens // block
+
+    def moved(keys, values, index, slot):
+        source = pl.ds(pl.multiple_of(index * block, block), block)
+        target = pl.ds(pl.multiple_of(slot * block, block), block)
+        return (
+            pltpu.make_async_copy(keys.at[:, source], keys_ref.at[:, target], sem_in.at[0, slot]),
+            pltpu.make_async_copy(
+                values.at[:, source], values_ref.at[:, target], sem_in.at[1, slot]
+            ),
+        )
+
+    for index in range(count):
+        for copy in moved(key_ref, value_ref, index, index):
+            copy.start()
     for place, source in enumerate(sources):
 
-        @pl.when(role == place)
+        @pl.when(where_ref[0] == place)
         def _(source=source):
-            pltpu.sync_copy(source, target)
-
-
-def terms_body(where_ref, *refs):
-    sources = refs[:-12]
-    (
-        key_ref, value_ref, rate_ref, keep_ref, send_ref,
-        w_ref, turned_ref, hidden_ref, target_ref, back_ref, sem, _,
-    ) = refs[-12:]
-    features, tokens = key_ref.shape
-    hidden_rows = w_ref.shape[1]
-    half = hidden_rows // 2
-    block = min(256, tokens)
-    side = where_ref[1]
-    pick_weights(where_ref[0], sources, w_ref, sem)
-    turned_ref[...] = w_ref[2].T
-    gate_lift = w_ref[0:2].reshape(2 * hidden_rows, features)
-
-    def step(index, carry):
-        at = pl.ds(pl.multiple_of(index * block, block), block)
-        keys = key_ref[:, at]
+            pltpu.make_async_copy(source, pack_ref, sem).start()
+
+    for index in range(count):
+        for copy in moved(pair_key_ref, pair_value_ref, index, count + index):
+            copy.start()
+    pltpu.make_async_copy(sources[0], pack_ref, sem).wait()
+    gate_lift = pack_ref[0:2].reshape(2 * half, features)
+    row = where_ref[2]
+
+    def step(slot, carry):
+        for copy in moved(key_ref, value_ref, 0, slot):
+            copy.wait()
+        at = pl.ds(pl.multiple_of(slot * block, block), block)
+        mirrored = where_ref[3] ^ (slot // count)
+        rate_at = pl.ds(pl.multiple_of(mirrored * tokens + (slot % count) * block, block), block)
+        keys = keys_ref[:, at]
         pre = jnp.dot(gate_lift, keys, preferred_element_type=jnp.float32)
-        pre_gate = pre[:hidden_rows]
-        pre_lift = pre[hidden_rows:]
-        rates = rate_ref[pl.ds(where_ref[2], 1), at]
-        target = (-(value_ref[:, at].astype(jnp.float32) * rates)).astype(jnp.bfloat16)
-        back_hidden = jnp.dot(turned_ref[...], target, preferred_element_type=jnp.float32)
+        pre_gate = pre[:half]
+        pre_lift = pre[half:]
+        rates = rate_ref[pl.ds(row, 1), rate_at]
+        target = (-(values_ref[:, at].astype(jnp.float32) * rates)).astype(jnp.bfloat16)
+        back_hidden = jnp.dot(pack_ref[2], target, preferred_element_type=jnp.float32)
         sigmoid_gate = 0.5 * jnp.tanh(0.5 * pre_gate) + 0.5
         silu_gate = pre_gate * sigmoid_gate
         hidden_ref[:, at] = (silu_gate * pre_lift).astype(jnp.bfloat16)
         target_ref[:, at] = target
-        back_lift = (back_hidden * silu_gate).astype(jnp.bfloat16)
         slope = sigmoid_gate + silu_gate * (1.0 - sigmoid_gate)
-        back_gate = (back_hidden * pre_lift * slope).astype(jnp.bfloat16)
-        for part in range(2):
-            back_ref[part, :half, at] = back_gate[part * half : (part + 1) * half]
-            back_ref[part, half:, at] = back_lift[part * half : (part + 1) * half]
+        back_ref[:half, at] = (back_hidden * pre_lift * slope).astype(jnp.bfloat16)
+        back_ref[half:, at] = (back_hidden * silu_gate).astype(jnp.bfloat16)
         return carry
 
-    lax.fori_loop(0, tokens // block, step, 0, unroll=2)
+    lax.fori_loop(0, 2 * count, step, 0, unroll=2)
     contract = (((1,), (1,)), ((), ()))
-    for part, out_ref in ((1 - side, send_ref), (side, keep_ref)):
-        sums = lax.dot_general(
-            back_ref[part], key_ref[...], contract, preferred_element_type=jnp.float32
-        )
-        out_ref[0] = sums[:half].astype(out_ref.dtype)
-        out_ref[1] = sums[half:].astype(out_ref.dtype)
-        rows = pl.ds(pl.multiple_of(part * half, half), half)
-        out_ref[2] = lax.dot_general(
-            target_ref[rows, :], hidden_ref[...], contract, preferred_element_type=jnp.float32
-        ).astype(out_ref.dtype)
-
-
-def fast_sums(where, sources, keys, values, rates):
+    sums = lax.dot_general(
+        back_ref[...], keys_ref[...], contract, preferred_element_type=jnp.float32
+    )
+    down = lax.dot_general(
+        hidden_ref[...], target_ref[...], contract, preferred_element_type=jnp.float32
+    )
+    for place, value in enumerate((sums[:half], sums[half:], down)):
+        keep_ref[place] = value
+        send_ref[place] = value.astype(jnp.bfloat16)
+
+
+def fast_sums(where, sources, keys, values, pair_keys, pair_values, rates):
     features, tokens = keys.shape
-    _, hidden_rows, _ = sources[0].shape
-    half = hidden_rows // 2
-    whole = lambda i, where: (0, 0)
-    parts = lambda i, where: (0, 0, 0)
+    shape = sources[0].shape
+    half = shape[1]
+    block = min(512, tokens)
+    anywhere = pl.BlockSpec(memory_space=pl.ANY)
+    resident = pl.BlockSpec(memory_space=pltpu.VMEM)
     return pl.pallas_call(
-        terms_body,
+        sums_body,
         out_shape=(
-            jax.ShapeDtypeStruct((3, half, features), jnp.float32),
-            jax.ShapeDtypeStruct((3, half, features), jnp.bfloat16),
+            jax.ShapeDtypeStruct(shape, jnp.float32),
+            jax.ShapeDtypeStruct(shape, jnp.bfloat16),
+            jax.ShapeDtypeStruct(shape, jnp.bfloat16),
         ),
-        grid_spec=pltpu.PrefetchScalarGridSpec(
-            num_scalar_prefetch=1,
-            grid=(1,),
-            in_specs=[pl.BlockSpec(memory_space=pl.ANY)] * len(sources)
-            + [
-                pl.BlockSpec((features, tokens), whole),
-                pl.BlockSpec((features, tokens), whole),
-                pl.BlockSpec((rates.shape[0], tokens), lambda i, where: (0, where[3])),
-            ],
-            out_specs=(
-                pl.BlockSpec((3, half, features), parts),
-                pl.BlockSpec((3, half, features), parts),
-            ),
-            scratch_shapes=[
-                pltpu.VMEM((3, hidden_rows, features), jnp.bfloat16),
-                pltpu.VMEM((hidden_rows, features), jnp.bfloat16),
-                pltpu.VMEM((hidden_rows, tokens), jnp.bfloat16),
-                pltpu.VMEM((features, tokens), jnp.bfloat16),
-                pltpu.VMEM((2, hidden_rows, tokens), jnp.bfloat16),
-                pltpu.SemaphoreType.DMA(()),
-                pltpu.SMEM((1,), jnp.int32),
-            ],
-        ),
+        in_specs=[pl.BlockSpec(memory_space=pltpu.SMEM)]
+        + [anywhere] * (len(sources) + 4)
+        + [resident],
+        out_specs=(resident,) * 3,
+        scratch_shapes=[
+            pltpu.VMEM((features, 2 * tokens), jnp.bfloat16),
+            pltpu.VMEM((features, 2 * tokens), jnp.bfloat16),
+            pltpu.VMEM((half, 2 * tokens), jnp.bfloat16),
+            pltpu.VMEM((features, 2 * tokens), jnp.bfloat16),
+            pltpu.VMEM((2 * half, 2 * tokens), jnp.bfloat16),
+            pltpu.SemaphoreType.DMA(()),
+            pltpu.SemaphoreType.DMA((2, 2 * tokens // block)),
+        ],
         cost_estimate=pl.CostEstimate(
-            flops=12 * hidden_rows * features * tokens,
-            bytes_accessed=4 * features * tokens + 6 * hidden_rows * features,
-            transcendentals=hidden_rows * tokens,
+            flops=24 * half * features * tokens,
+            bytes_accessed=8 * features * tokens + 8 * 3 * half * features,
+            transcendentals=2 * half * tokens,
         ),
         name="fast_sums",
-    )(where, *sources, keys, values, rates)
-
-
-def recall_body(where_ref, *refs):
-    sources = refs[:-7]
-    mine_ref, other_ref, query_ref, out_ref, w_ref, fresh_ref, sem = refs[-7:]
+    )(where, *sources, keys, values, pair_keys, pair_values, rates)
+
+
+def recall_body(where_ref, mine_ref, other_ref, pack_ref, pair_pack_ref, query_ref, out_ref, w_ref, fresh_ref):
     half = mine_ref.shape[1]
 
     @pl.when(pl.program_id(0) == 0)
     def _():
         side = where_ref[1]
-        pick_weights(where_ref[0], sources, w_ref, sem)
         rows_mine = pl.ds(pl.multiple_of(side * half, half), half)
         rows_other = pl.ds(pl.multiple_of((1 - side) * half, half), half)
         fresh_ref[:, rows_mine, :] = mine_ref[...]
         fresh_ref[:, rows_other, :] = other_ref[...]
+        w_ref[:, rows_mine, :] = pack_ref[...]
+        w_ref[:, rows_other, :] = pair_pack_ref[...]
         current = []
         for i in range(3):
-            widened = fresh_ref[i].astype(jnp.float32)
+            rounded = fresh_ref[i].T if i == 2 else fresh_ref[i]
+            widened = rounded.astype(jnp.float32)
             total = jnp.sum(jnp.sum(widened * widened, axis=0, keepdims=True), axis=1, keepdims=True)
             current.append((widened / jnp.sqrt(total + EPS)).astype(jnp.bfloat16))
         for _ in range(NS_ITERS):
@@ -426,7 +506,8 @@
                 for x, y, g in zip(current, lifted, gram)
             ]
         for i in range(3):
-            initial = w_ref[i].astype(jnp.float32)
+            weight = w_ref[i].T if i == 2 else w_ref[i]
+            initial = weight.astype(jnp.float32)
             moved = initial - current[i].astype(jnp.float32)
             wanted = jnp.mean(jnp.square(initial), axis=-1, keepdims=True) + EPS
             present = jnp.mean(jnp.square(moved), axis=-1, keepdims=True) + EPS
@@ -445,39 +526,30 @@
     )
 
 
-def fast_recall(where, sources, mine, other, queries):
+def fast_recall(where, mine, other, pack, pair_pack, queries):
     features, tokens = queries.shape
-    _, hidden_rows, _ = sources[0].shape
+    half = mine.shape[1]
+    hidden_rows = 2 * half
     block = min(512, tokens)
-    half = hidden_rows // 2
-    parts = lambda i, where: (0, 0, 0)
-    piece = pl.BlockSpec((features, block), lambda i, where: (0, i))
+    parts = pl.BlockSpec((3, half, features), lambda i: (0, 0, 0))
+    piece = pl.BlockSpec((features, block), lambda i: (0, i))
     return pl.pallas_call(
         recall_body,
         out_shape=jax.ShapeDtypeStruct((features, tokens), jnp.bfloat16),
-        grid_spec=pltpu.PrefetchScalarGridSpec(
-            num_scalar_prefetch=1,
-            grid=(tokens // block,),
-            in_specs=[pl.BlockSpec(memory_space=pl.ANY)] * len(sources)
-            + [
-                pl.BlockSpec((3, half, features), parts),
-                pl.BlockSpec((3, half, features), parts),
-                piece,
-            ],
-            out_specs=piece,
-            scratch_shapes=[
-                pltpu.VMEM((3, hidden_rows, features), jnp.bfloat16),
-                pltpu.VMEM((3, hidden_rows, features), jnp.bfloat16),
-                pltpu.SemaphoreType.DMA(()),
-            ],
-        ),
+        grid=(tokens // block,),
+        in_specs=[pl.BlockSpec(memory_space=pltpu.SMEM)] + [parts] * 4 + [piece],
+        out_specs=piece,
+        scratch_shapes=[
+            pltpu.VMEM((3, hidden_rows, features), jnp.bfloat16),
+            pltpu.VMEM((3, hidden_rows, features), jnp.bfloat16),
+        ],
         cost_estimate=pl.CostEstimate(
-            flops=6 * hidden_rows * features * tokens + 36 * NS_ITERS * hidden_rows * features**2 // 2,
+            flops=6 * hidden_rows * features * tokens + 18 * NS_ITERS * hidden_rows * features**2,
             bytes_accessed=4 * features * tokens + 12 * hidden_rows * features,
             transcendentals=hidden_rows * tokens,
         ),
         name="fast_recall",
-    )(where, *sources, mine, other, queries)
+    )(where, mine, other, pack, pair_pack, queries)
 
 
 def in_place(query_states, key_states, value_states, cache_keys, cache_values, gate_fast, *rest):
@@ -505,55 +577,50 @@
     down_fast,
     token_rates,
 ):
-    tok_count = query_states.shape[1]
     wide_count = lax.axis_size("wide")
     narrow_count = lax.axis_size("narrow")
     owned = gate_fast.shape[0]
     wide_at = lax.axis_index("wide")
     narrow_at = lax.axis_index("narrow")
     role = narrow_at ^ (wide_at // owned)
-    where = jnp.stack([role, narrow_at % 2, wide_at, narrow_at]).astype(jnp.int32)
-
-    def sent(value, step):
-        source = step & (step - 1)
+    where = jnp.stack([role, narrow_at % 2, wide_at, narrow_at, wide_at % owned]).astype(jnp.int32)
+
+    def from_owner(value, step):
         pairs = []
         for wide in range(wide_count):
+            start = wide * narrow_count
             owner = wide // owned
-            pairs.append(
-                (wide * narrow_count + (owner ^ source), wide * narrow_count + (owner ^ step))
-            )
+            pairs.append((start + owner, start + (owner ^ step)))
         return lax.ppermute(value, ("wide", "narrow"), pairs)
 
-    local = wide_at % owned
-    sources = [
-        jnp.stack(
-            [
-                lax.dynamic_index_in_dim(weight, local, 0, keepdims=False)
-                for weight in (gate_fast, lift_fast, down_fast)
-            ]
-        )
-    ]
-    for step in range(1, narrow_count):
-        sources.append(sent(sources[step & (step - 1)], step))
-    edge_cols = jnp.stack(
-        [key_states[:, tok_count - WINDOW :], value_states[:, tok_count - WINDOW :]]
-    )
-    arrived = from_behind(edge_cols, "narrow", 1)
+    own, other = prepare(where, gate_fast, lift_fast, down_fast)
+    arrivals = {}
+    for step in reversed(range(1, narrow_count)):
+        arrivals[step] = from_owner((own, other)[step % 2], step)
+    pair_keys = swapped(key_states, "narrow", 0)
+    pair_values = swapped(value_states, "narrow", 0)
+    prior = from_behind(edges(key_states, value_states), "narrow", 1)
     late = attend_late(query_states, key_states, value_states)
-    keep, send = fast_sums(where, sources, key_states, value_states, token_rates)
-    total = keep + swapped(send, "narrow", 0).astype(jnp.float32)
-    distance = 1
-    while 1 << distance < narrow_count:
-        other = swapped(total.astype(jnp.bfloat16), "narrow", distance)
-        total = total + other.astype(jnp.float32)
-        distance += 1
+    sources = [own] + [arrivals[step] for step in range(1, narrow_count)]
+    sources, late = lax.optimization_barrier((sources, late))
+    keep, send, pack = fast_sums(
+        where, sources, key_states, value_states, pair_keys, pair_values, token_rates
+    )
+    pair_pack = swapped(pack, "narrow", 0)
+    total = keep
+    rounded = send
+    for distance in range(1, narrow_count.bit_length() - 1):
+        if distance > 1:
+            rounded = total.astype(jnp.bfloat16)
+        partner = swapped(rounded, "narrow", distance)
+        total = total + partner.astype(jnp.float32)
     mine = stored(total)
     theirs = swapped(mine, "narrow", 0)
     leading = (narrow_at == 0).astype(jnp.int32).reshape(1)
     attended = attend_early(
-        leading, query_states, key_states, value_states, arrived, cache_keys, cache_values, late
-    )
-    recalled = fast_recall(where, sources, mine, theirs, query_states)
+        leading, query_states, key_states, value_states, in_hbm(prior), cache_keys, cache_values, late
+    )
+    recalled = fast_recall(where, mine, theirs, pack, pair_pack, query_states)
     return (attended, recalled)
 
 

time: 138 us -> 104 us (0.75)
  the two profiles are of different devices: /device:TPU:0 before, /device:TPU:21 now
where the time goes in v2:
time: 104 us
  Pallas kernels  63.2 us (61%)
  waiting for transfers between devices  24.4 us (23%)
  starting transfers between devices  11.8 us (11%)
  local copies, waits for them, and re-layouts  2.02 us (2%)
  other arithmetic  1.72 us (2%)
    ppermute x5, waiting for transfers between devices, swapped(): lax.ppermute(array, axis, [(i, i ^ 1 << distance) for i in range(lax.axis...  24.4 us
    pallas_call x1, Pallas kernels, fast_sums(): pl.pallas_call(sums_body, out_shape=(jax.ShapeDtypeStruct(shape, jnp.floa...  15.7 us
    pallas_call x1, Pallas kernels, fast_recall(): pl.pallas_call(recall_body, out_shape=jax.ShapeDtypeStruct((features, tok...  14.3 us
    pallas_call x1, Pallas kernels, attend_early(): pl.pallas_call(functools.partial(attend_body, block=block, has_cache=True...  13.4 us
    pallas_call x1, Pallas kernels, attend_late(): pl.pallas_call(functools.partial(attend_body, block=block, has_cache=Fals...  12.8 us
    ppermute x5, starting transfers between devices, swapped(): lax.ppermute(array, axis, [(i, i ^ 1 << distance) for i in range(lax.axis...  6.92 us
    pallas_call x1, Pallas kernels, edges(): pl.pallas_call(edges_body, out_shape=jax.ShapeDtypeStruct((2, features, W...  3.76 us
    ppermute x3, starting transfers between devices, from_owner(): return lax.ppermute(value, ('wide', 'narrow'), pairs)  3.56 us
  transfers between devices with their start and end apart: 9, of which 1 were waited for; matrix products, arithmetic and copies ran while one was open for 2% of the time, Pallas kernels for 47%

profile of v2, /device:TPU:21, one launch (start us, length us, event | category | flops | bytes accessed | tf_op | source)
XLA Modules:
  0.0 103.9 jit_solution(12259323013398023920)
XLA Ops:
  0.6 0.7 collective-permute-start.4
  1.4 0.1 collective-permute-start.5
  1.5 0.6 stack.23.where_ref
  2.1 3.3 %prepare.1 = (bf16[3,256,512]{2,1,0:T(8,128)(2,1)}, bf16[3,256,512]{2,1,0:T(8,128)(2,1)}) custom-call(s32[5]{0:T(128)} %stack.23.where_ref, bf16[2,512,512]{2,1,0:T(8,128)(2,1)} %gate_ref.1, bf16[2,512,512]{2,1,0:T(8,128)(2,1)} %lift_ref.1, bf16[2,512,512]{2,1,0:T(8,128)(2,1)} %down_ref.1), custom_call_target="tpu_custom_call" | custom-call | bytes 3145728 | tf_op jit(solution)/shard_map/prepare/pallas_call | solution.py:323
  5.4 0.7 collective-permute-start.2
  6.1 1.6 %collective-permute-start.3 = (bf16[3,256,512]{2,1,0:T(8,128)(2,1)}, bf16[3,256,512]{2,1,0:T(8,128)(2,1)}, u32[]{:S(2)}, u32[]{:S(2)}) collective-permute-start(bf16[3,256,512]{2,1,0:T(8,128)(2,1)} %get-tuple-element.13), channel_id=1, source_target_pairs={{0,3},{4,7},{9,10},{13,14},{18,17},{22,21},{27,24},{31,28}} | collective-permute-start | bytes 2359304 | tf_op jit(solution)/shard_map/ppermute | solution.py:594
  7.7 1.3 %collective-permute-start.1 = (bf16[3,256,512]{2,1,0:T(8,128)(2,1)}, bf16[3,256,512]{2,1,0:T(8,128)(2,1)}, u32[]{:S(2)}, u32[]{:S(2)}) collective-permute-start(bf16[3,256,512]{2,1,0:T(8,128)(2,1)} %get-tuple-element.13), channel_id=1, source_target_pairs={{0,1},{4,5},{9,8},{13,12},{18,19},{22,23},{27,26},{31,30}} | collective-permute-start | bytes 2359304 | tf_op jit(solution)/shard_map/ppermute | solution.py:594
  9.0 3.8 %edges.1 = bf16[2,512,1024]{2,1,0:T(8,128)(2,1)} custom-call(bf16[512,2048]{1,0:T(8,128)(2,1)} %refs_4_.1, bf16[512,2048]{1,0:T(8,128)(2,1)} %refs_5_.1), custom_call_target="tpu_custom_call" | custom-call | bytes 4194304 | tf_op jit(solution)/shard_map/edges/pallas_call | solution.py:349
  12.7 12.8 %attend_late.1.rest_2_ = bf16[512,2048]{1,0:T(8,128)(2,1)} custom-call(s32[1]{0:T(128)} %constant.39.clone.1.flag_ref, bf16[512,2048]{1,0:T(8,128)(2,1)} %query_ref.1, bf16[512,2048]{1,0:T(8,128)(2,1)} %refs_4_.1, bf16[512,2048]{1,0:T(8,128)(2,1)} %refs_5_.1, bf16[512,2048]{1,0:T(8,128)(2,1)} %refs_4_.1, bf16[512,2048]{1,0:T(8,128)(2,1)} %refs_5_.1), custom_call_target="tpu_custom_call" | custom-call | flops 2684354560 | bytes 5242880 | tf_op jit(solution)/shard_map/attend_late/pallas_call | solution.py:263
  25.5 0.0 collective-permute-done.2.refs_2_
  25.5 0.0 copy-start.2
  25.5 1.3 %collective-permute-start = (bf16[2,512,1024]{2,1,0:T(8,128)(2,1)}, bf16[2,512,1024]{2,1,0:T(8,128)(2,1)S(1)}, u32[]{:S(2)}, u32[]{:S(2)}) collective-permute-start(bf16[2,512,1024]{2,1,0:T(8,128)(2,1)} %edges.1), channel_id=1, source_target_pairs={{0,1},{1,2},{2,3},{4,5},{5,6},{6,7},{8,9},{9,10},{10,11},{12,13},{... | collective-permute-start | bytes 6291464 | tf_op jit(solution)/shard_map/ppermute | solution.py:40
  26.8 0.0 collective-permute-done.3.refs_3_
  26.8 0.0 collective-permute-done.1.refs_1_
  26.8 0.0 collective-permute-done.4.refs_6_
  26.8 0.0 collective-permute-done.5.refs_7_
  26.8 0.0 copy-done.2
  26.8 15.7 %fast_sums.1 = (f32[3,256,512]{2,1,0:T(8,128)}, bf16[3,256,512]{2,1,0:T(8,128)(2,1)}, bf16[3,256,512]{2,1,0:T(8,128)(2,1)}) custom-call(s32[5]{0:T(128)} %stack.23.where_ref, bf16[3,256,512]{2,1,0:T(8,128)(2,1)} %get-tuple-element.15.refs_0_, bf16[3,256,512]{2,1,0:T(8,128)(2,1)} %collective-permute-done.1.refs_1_, bf16[3,256,512]{2,1,0:T(8,128)(2,1)} %copy-done.2, ...), custom_call_target="tpu_custom_call" | custom-call | flops 6442450944 | bytes 11534336 | tf_op jit(solution)/shard_map/fast_sums/pallas_call | solution.py:442
  42.5 6.0 %collective-permute-start.6 = (bf16[3,256,512]{2,1,0:T(8,128)(2,1)}, bf16[3,256,512]{2,1,0:T(8,128)(2,1)S(1)}, u32[]{:S(2)}, u32[]{:S(2)}) collective-permute-start(bf16[3,256,512]{2,1,0:T(8,128)(2,1)} %get-tuple-element.20), channel_id=1, source_target_pairs={{0,2},{1,3},{2,0},{3,1},{4,6},{5,7},{6,4},{7,5},{8,10},{9,11},{10,... | collective-permute-start | bytes 2359304 | tf_op jit(solution)/shard_map/ppermute | solution.py:26
  48.5 0.0 collective-permute-start.8
  48.5 24.3 %collective-permute-done.6 = bf16[3,256,512]{2,1,0:T(8,128)(2,1)S(1)} collective-permute-done((bf16[3,256,512]{2,1,0:T(8,128)(2,1)}, bf16[3,256,512]{2,1,0:T(8,128)(2,1)S(1)}, u32[]{:S(2)}, u32[]{:S(2)}) %collective-permute-start.6) | collective-permute-done | bytes 786464 | tf_op jit(solution)/shard_map/ppermute | solution.py:26
  72.9 1.7 %add_convert_fusion.mine_ref = bf16[3,256,512]{2,1,0:T(8,128)(2,1)S(1)} fusion(f32[3,256,512]{2,1,0:T(8,128)} %get-tuple-element.19, bf16[3,256,512]{2,1,0:T(8,128)(2,1)S(1)} %collective-permute-done.6), kind=kLoop, calls=%fused_computation | loop fusion | flops 1179648 | bytes 3145728 | tf_op jit(solution)/shard_map/convert_element_type | solution.py:44
  74.6 0.0 copy-start.1
  74.6 0.1 collective-permute-start.7
  74.7 0.0 collective-permute-done.kp_ref.vp_ref
  74.7 0.0 copy-start
  74.7 1.4 %copy-done = bf16[2,512,1024]{2,1,0:T(8,128)(2,1)} copy-done((bf16[2,512,1024]{2,1,0:T(8,128)(2,1)}, bf16[2,512,1024]{2,1,0:T(8,128)(2,1)S(1)}, u32[]{:S(2)}) %copy-start) | copy-done | bytes 2097176
  76.1 13.4 %attend_early.1 = bf16[512,2048]{1,0:T(8,128)(2,1)} custom-call(s32[1]{0:T(128)} %bitcast.flag_ref, bf16[512,2048]{1,0:T(8,128)(2,1)} %query_ref.1, bf16[2,512,1024]{2,1,0:T(8,128)(2,1)} %copy-done, bf16[2,512,1024]{2,1,0:T(8,128)(2,1)} %copy-done, bf16[512,2048]{1,0:T(8,128)(2,1)} %refs_4_.1, ...), custom_call_target="tpu_custom_call", output_to_operand_aliasing={{}: (8, {})} | custom-call | flops 2684354560 | bytes 7340032 | tf_op jit(solution)/shard_map/attend_early/pallas_call | solution.py:282
  89.5 0.0 copy-done.1
  89.6 0.0 collective-permute-done.8.pair_pack_ref
  89.6 0.0 collective-permute-done.7.other_ref
  89.6 14.3 %fast_recall.1 = bf16[512,2048]{1,0:T(8,128)(2,1)} custom-call(s32[5]{0:T(128)} %stack.23.where_ref, bf16[3,256,512]{2,1,0:T(8,128)(2,1)} %copy-done.1, bf16[3,256,512]{2,1,0:T(8,128)(2,1)} %collective-permute-done.7.other_ref, bf16[3,256,512]{2,1,0:T(8,128)(2,1)} %get-tuple-element.21.pack_ref, bf16[3,256,512]{2,1,0:T(8,128)(2,1)} %collective-permute-done.8.pair_pack_ref, ...), custom_call_target="tpu_custom_call" | custom-call | flops 8053063680 | bytes 7340032 | tf_op jit(solution)/shard_map/fast_recall/pallas_call | solution.py:536
Async XLA Ops:
  0.6 26.2 %collective-permute-start.4 = (bf16[512,2048]{1,0:T(8,128)(2,1)}, bf16[512,2048]{1,0:T(8,128)(2,1)}, u32[]{:S(2)}, u32[]{:S(2)}) collective-permute-start(bf16[512,2048]{1,0:T(8,128)(2,1)} %refs_4_.1), channel_id=1, source_target_pairs={{0,1},{1,0},{2,3},{3,2},{4,5},{5,4},{6,7},{7,6},{8,9},{9,8},{10,11... | collective-permute-start | bytes 6291464 | tf_op jit(solution)/shard_map/ppermute | solution.py:26
  1.4 25.4 %collective-permute-start.5 = (bf16[512,2048]{1,0:T(8,128)(2,1)}, bf16[512,2048]{1,0:T(8,128)(2,1)}, u32[]{:S(2)}, u32[]{:S(2)}) collective-permute-start(bf16[512,2048]{1,0:T(8,128)(2,1)} %refs_5_.1), channel_id=1, source_target_pairs={{0,1},{1,0},{2,3},{3,2},{4,5},{5,4},{6,7},{7,6},{8,9},{9,8},{10,11... | collective-permute-start | bytes 6291464 | tf_op jit(solution)/shard_map/ppermute | solution.py:26
  5.4 20.1 %collective-permute-start.2 = (bf16[3,256,512]{2,1,0:T(8,128)(2,1)}, bf16[3,256,512]{2,1,0:T(8,128)(2,1)S(1)}, u32[]{:S(2)}, u32[]{:S(2)}) collective-permute-start(bf16[3,256,512]{2,1,0:T(8,128)(2,1)} %get-tuple-element.15.refs_0_), channel_id=1, source_target_pairs={{0,2},{4,6},{9,11},{13,15},{18,16},{22,20},{27,25},{31,29}} | collective-permute-start | bytes 2359304 | tf_op jit(solution)/shard_map/ppermute | solution.py:594
  6.1 20.7 %collective-permute-start.3 = (bf16[3,256,512]{2,1,0:T(8,128)(2,1)}, bf16[3,256,512]{2,1,0:T(8,128)(2,1)}, u32[]{:S(2)}, u32[]{:S(2)}) collective-permute-start(bf16[3,256,512]{2,1,0:T(8,128)(2,1)} %get-tuple-element.13), channel_id=1, source_target_pairs={{0,3},{4,7},{9,10},{13,14},{18,17},{22,21},{27,24},{31,28}} | collective-permute-start | bytes 2359304 | tf_op jit(solution)/shard_map/ppermute | solution.py:594
  7.7 19.1 %collective-permute-start.1 = (bf16[3,256,512]{2,1,0:T(8,128)(2,1)}, bf16[3,256,512]{2,1,0:T(8,128)(2,1)}, u32[]{:S(2)}, u32[]{:S(2)}) collective-permute-start(bf16[3,256,512]{2,1,0:T(8,128)(2,1)} %get-tuple-element.13), channel_id=1, source_target_pairs={{0,1},{4,5},{9,8},{13,12},{18,19},{22,23},{27,26},{31,30}} | collective-permute-start | bytes 2359304 | tf_op jit(solution)/shard_map/ppermute | solution.py:594
  25.5 1.3 %copy-start.2 = (bf16[3,256,512]{2,1,0:T(8,128)(2,1)}, bf16[3,256,512]{2,1,0:T(8,128)(2,1)S(1)}, u32[]{:S(2)}) copy-start(bf16[3,256,512]{2,1,0:T(8,128)(2,1)S(1)} %collective-permute-done.2.refs_2_) | copy-start | bytes 2359300
  25.5 49.2 %collective-permute-start = (bf16[2,512,1024]{2,1,0:T(8,128)(2,1)}, bf16[2,512,1024]{2,1,0:T(8,128)(2,1)S(1)}, u32[]{:S(2)}, u32[]{:S(2)}) collective-permute-start(bf16[2,512,1024]{2,1,0:T(8,128)(2,1)} %edges.1), channel_id=1, source_target_pairs={{0,1},{1,2},{2,3},{4,5},{5,6},{6,7},{8,9},{9,10},{10,11},{12,13},{... | collective-permute-start | bytes 6291464 | tf_op jit(solution)/shard_map/ppermute | solution.py:40
  42.5 30.4 %collective-permute-start.6 = (bf16[3,256,512]{2,1,0:T(8,128)(2,1)}, bf16[3,256,512]{2,1,0:T(8,128)(2,1)S(1)}, u32[]{:S(2)}, u32[]{:S(2)}) collective-permute-start(bf16[3,256,512]{2,1,0:T(8,128)(2,1)} %get-tuple-element.20), channel_id=1, source_target_pairs={{0,2},{1,3},{2,0},{3,1},{4,6},{5,7},{6,4},{7,5},{8,10},{9,11},{10,... | collective-permute-start | bytes 2359304 | tf_op jit(solution)/shard_map/ppermute | solution.py:26
  48.5 41.0 %collective-permute-start.8 = (bf16[3,256,512]{2,1,0:T(8,128)(2,1)}, bf16[3,256,512]{2,1,0:T(8,128)(2,1)}, u32[]{:S(2)}, u32[]{:S(2)}) collective-permute-start(bf16[3,256,512]{2,1,0:T(8,128)(2,1)} %get-tuple-element.21.pack_ref), channel_id=1, source_target_pairs={{0,1},{1,0},{2,3},{3,2},{4,5},{5,4},{6,7},{7,6},{8,9},{9,8},{10,11... | collective-permute-start | bytes 2359304 | tf_op jit(solution)/shard_map/ppermute | solution.py:26
  74.6 14.9 %copy-start.1 = (bf16[3,256,512]{2,1,0:T(8,128)(2,1)}, bf16[3,256,512]{2,1,0:T(8,128)(2,1)S(1)}, u32[]{:S(2)}) copy-start(bf16[3,256,512]{2,1,0:T(8,128)(2,1)S(1)} %add_convert_fusion.mine_ref) | copy-start | bytes 2359300
  74.6 14.9 %collective-permute-start.7 = (bf16[3,256,512]{2,1,0:T(8,128)(2,1)S(1)}, bf16[3,256,512]{2,1,0:T(8,128)(2,1)}, u32[]{:S(2)}, u32[]{:S(2)}) collective-permute-start(bf16[3,256,512]{2,1,0:T(8,128)(2,1)S(1)} %add_convert_fusion.mine_ref), channel_id=1, source_target_pairs={{0,1},{1,0},{2,3},{3,2},{4,5},{5,4},{6,7},{7,6},{8,9},{9,8},{10,11... | collective-permute-start | bytes 2359304 | tf_op jit(solution)/shard_map/ppermute | solution.py:26
  74.7 1.4 %copy-start = (bf16[2,512,1024]{2,1,0:T(8,128)(2,1)}, bf16[2,512,1024]{2,1,0:T(8,128)(2,1)S(1)}, u32[]{:S(2)}) copy-start(bf16[2,512,1024]{2,1,0:T(8,128)(2,1)S(1)} %collective-permute-done.kp_ref.vp_ref) | copy-start | bytes 6291460

commit v3 on v0

--- a/solution.py
+++ b/solution.py
@@ -1,9 +1,13 @@
+import functools
 import math
 
 import jax
 import jax.numpy as jnp
 from jax import lax
+from jax.experimental import pallas as pl
+from jax.experimental.pallas import tpu as pltpu
 from jax.sharding import PartitionSpec as P
+
 
 FD = 512
 HEAD_SIZE = 128
@@ -15,6 +19,8 @@
 COEF_A = 3.4445
 COEF_B = -4.775
 COEF_C = 2.0315
+LOG2E = math.log2(math.e)
+VMEM_GRANT = 67043328
 
 
 def swapped(array, axis, distance):
@@ -152,7 +158,7 @@
 
 
 def orthogonal(current):
-    for sweep_index in range(NS_ITERS):
+    for _ in range(NS_ITERS):
         gram_mat = jnp.einsum(
             "hrc,hrd->hcd", current, current, preferred_element_type=jnp.float32
         ).astype(jnp.bfloat16)
@@ -198,7 +204,493 @@
     ).astype(jnp.bfloat16)
 
 
-def per_device(
+def attend_body(q_ref, kp_ref, vp_ref, kc_ref, vc_ref, *rest, block, window):
+    cached = len(rest) > 3
+    o_ref, kt_ref, v_ref = rest[-3:]
+    hd = q_ref.shape[0]
+    scale = LOG2E / math.sqrt(hd)
+
+    def place(k, v, at):
+        turned = k[...].T
+        kt_ref[at : at + window, :hd] = turned
+        kt_ref[at : at + window, hd:] = turned
+        v_ref[:hd, at : at + window] = v[...]
+
+    if cached:
+        leading = lax.axis_index("narrow") == 0
+
+        @pl.when(leading)
+        def _():
+            place(*rest[:2], 0)
+
+        @pl.when(jnp.logical_not(leading))
+        def _():
+            place(kp_ref, vp_ref, 0)
+
+    else:
+        place(kp_ref, vp_ref, 0)
+    place(kc_ref, vc_ref, window)
+    v_ref[hd:, :] = jnp.ones((v_ref.shape[0] - hd, 2 * window), jnp.bfloat16)
+    rows = lax.broadcasted_iota(jnp.int32, (block, block), 0)
+    cols = lax.broadcasted_iota(jnp.int32, (block, block), 1)
+    first = rows > cols
+    inner = window // block
+
+    def scores(b):
+        q = q_ref[:, b * block : (b + 1) * block].astype(jnp.float32) * scale
+        high = q.astype(jnp.bfloat16)
+        low = (q - high.astype(jnp.float32)).astype(jnp.bfloat16)
+        pair = jnp.concatenate([high, low], axis=0)
+        parts = [
+            jnp.dot(
+                kt_ref[(b + j) * block : (b + j + 1) * block, :],
+                pair,
+                preferred_element_type=jnp.float32,
+            )
+            for j in range(inner + 1)
+        ]
+        return [jnp.where(first, parts[0], parts[inner])] + parts[1:inner]
+
+    def blend(b, parts):
+        top = functools.reduce(jnp.maximum, parts)
+        top = jnp.max(top, axis=0, keepdims=True)
+        raised = [jnp.exp2(part - top).astype(jnp.bfloat16) for part in parts]
+        zero = jnp.zeros_like(raised[0])
+        ends = jnp.where(first, raised[0], zero), jnp.where(first, zero, raised[0])
+        weights = jnp.concatenate([ends[0]] + raised[1:] + [ends[1]], axis=0)
+        span = v_ref[:, b * block : (b + inner + 1) * block]
+        out = jnp.dot(span, weights, preferred_element_type=jnp.float32)
+        o_ref[:, b * block : (b + 1) * block] = (out[:hd] * (1.0 / out[hd : hd + 1])).astype(
+            jnp.bfloat16
+        )
+
+    ready = scores(0)
+    for b in range(1, inner):
+        following = scores(b)
+        blend(b - 1, ready)
+        ready = following
+    blend(inner - 1, ready)
+
+
+def attend_scratch():
+    return [
+        pltpu.VMEM((2 * WINDOW, 2 * HEAD_SIZE), jnp.bfloat16),
+        pltpu.VMEM((HEAD_SIZE + 16, 2 * WINDOW), jnp.bfloat16),
+    ]
+
+
+def attend_late(queries, keys, values):
+    features, tokens = queries.shape
+    heads, chunks = features // HEAD_SIZE, tokens // WINDOW - 1
+    here = pl.BlockSpec((HEAD_SIZE, WINDOW), lambda h, c: (h, c + 1))
+    before = pl.BlockSpec((HEAD_SIZE, WINDOW), lambda h, c: (h, c))
+    return pl.pallas_call(
+        functools.partial(attend_body, block=min(256, WINDOW), window=WINDOW),
+        out_shape=jax.ShapeDtypeStruct((features, tokens), jnp.bfloat16),
+        grid=(heads, chunks),
+        in_specs=[here, before, before, here, here],
+        out_specs=here,
+        scratch_shapes=attend_scratch(),
+        cost_estimate=pl.CostEstimate(
+            flops=5 * features * chunks * WINDOW**2,
+            bytes_accessed=10 * features * chunks * WINDOW,
+            transcendentals=heads * chunks * WINDOW**2,
+        ),
+        name="attend_late",
+    )(queries, keys, values, keys, values)
+
+
+def attend_early(queries, keys, values, prior, cache_keys, cache_values, late):
+    features, tokens = queries.shape
+    heads = features // HEAD_SIZE
+    here = pl.BlockSpec((HEAD_SIZE, WINDOW), lambda h: (h, 0))
+    prior_keys = pl.BlockSpec((None, HEAD_SIZE, WINDOW), lambda h: (0, h, 0))
+    prior_values = pl.BlockSpec((None, HEAD_SIZE, WINDOW), lambda h: (1, h, 0))
+    body = functools.partial(attend_body, block=min(256, WINDOW), window=WINDOW)
+
+    def early_body(*refs):
+        body(*refs[:7], *refs[8:])
+
+    return pl.pallas_call(
+        early_body,
+        out_shape=jax.ShapeDtypeStruct((features, tokens), jnp.bfloat16),
+        grid=(heads,),
+        in_specs=[here, prior_keys, prior_values, here, here, here, here]
+        + [pl.BlockSpec(memory_space=pl.ANY)],
+        out_specs=here,
+        scratch_shapes=attend_scratch(),
+        input_output_aliases={7: 0},
+        cost_estimate=pl.CostEstimate(
+            flops=5 * features * WINDOW**2,
+            bytes_accessed=14 * features * WINDOW,
+            transcendentals=heads * WINDOW**2,
+        ),
+        name="attend_early",
+        compiler_params=pltpu.CompilerParams(vmem_limit_bytes=VMEM_GRANT),
+    )(queries, prior, prior, keys, values, cache_keys, cache_values, late)
+
+
+def anywhere(count):
+    return [pl.BlockSpec(memory_space=pl.ANY)] * count
+
+
+def half_rows(part, half):
+    return pl.ds(pl.multiple_of(part * half, half), half)
+
+
+def prepare_body(gate_ref, lift_ref, down_ref, own_ref, other_ref, w_ref, out_ref, sem):
+    owned = gate_ref.shape[0]
+    local = lax.axis_index("wide") % owned
+    side = lax.axis_index("narrow") % 2
+    half = own_ref.shape[1]
+    copies = [
+        pltpu.make_async_copy(source.at[local], w_ref.at[place], sem.at[0, place])
+        for place, source in enumerate((down_ref, gate_ref, lift_ref))
+    ]
+    for copy in copies:
+        copy.start()
+    leaving = []
+    copies[0].wait()
+    out_ref[...] = w_ref[0].T
+    for order, (place, source) in enumerate(((2, out_ref), (0, w_ref.at[1]), (1, w_ref.at[2]))):
+        if order:
+            copies[order].wait()
+        for turn, (target, part) in enumerate(((own_ref, side), (other_ref, 1 - side))):
+            leaving.append(
+                pltpu.make_async_copy(
+                    source.at[half_rows(part, half)], target.at[place], sem.at[1 + turn, place]
+                )
+            )
+            leaving[-1].start()
+    for copy in leaving:
+        copy.wait()
+
+
+def prepare(gate_fast, lift_fast, down_fast):
+    _, hidden_rows, features = gate_fast.shape
+    shape = (3, hidden_rows // 2, features)
+    return pl.pallas_call(
+        prepare_body,
+        out_shape=(jax.ShapeDtypeStruct(shape, jnp.bfloat16),) * 2,
+        in_specs=anywhere(3),
+        out_specs=tuple(anywhere(2)),
+        scratch_shapes=[
+            pltpu.VMEM((3, hidden_rows, features), jnp.bfloat16),
+            pltpu.VMEM((hidden_rows, features), jnp.bfloat16),
+            pltpu.SemaphoreType.DMA((3, 3)),
+        ],
+        cost_estimate=pl.CostEstimate(
+            flops=0, bytes_accessed=12 * hidden_rows * features, transcendentals=0
+        ),
+        name="prepare",
+    )(gate_fast, lift_fast, down_fast)
+
+
+def edges_body(key_ref, value_ref, out_ref, held_ref, sem):
+    features, tokens = key_ref.shape
+    rows = min(HEAD_SIZE, features)
+    window = out_ref.shape[2]
+    moves = []
+    for place, source in enumerate((key_ref, value_ref)):
+        for part in range(features // rows):
+            at = slice(part * rows, (part + 1) * rows)
+            arriving = pltpu.make_async_copy(
+                source.at[at, tokens - window :], held_ref.at[place, at], sem.at[0, place, part]
+            )
+            leaving = pltpu.make_async_copy(
+                held_ref.at[place, at], out_ref.at[place, at], sem.at[1, place, part]
+            )
+            arriving.start()
+            moves.append((arriving, leaving))
+    for arriving, leaving in moves:
+        arriving.wait()
+        leaving.start()
+    for _, leaving in moves:
+        leaving.wait()
+
+
+def edges(keys, values):
+    features = keys.shape[0]
+    shape = (2, features, WINDOW)
+    return pl.pallas_call(
+        edges_body,
+        out_shape=jax.ShapeDtypeStruct(shape, jnp.bfloat16),
+        in_specs=anywhere(2),
+        out_specs=pl.BlockSpec(memory_space=pl.ANY),
+        scratch_shapes=[
+            pltpu.VMEM(shape, jnp.bfloat16),
+            pltpu.SemaphoreType.DMA((2, 2, features // min(HEAD_SIZE, features))),
+        ],
+        cost_estimate=pl.CostEstimate(
+            flops=0, bytes_accessed=8 * features * WINDOW, transcendentals=0
+        ),
+        name="edges",
+    )(keys, values)
+
+
+def sums_body(*refs, owned):
+    sources = refs[:-14]
+    (
+        key_ref, value_ref, pair_key_ref, pair_value_ref, rate_ref,
+        send_ref, pack_ref,
+        keys_ref, values_ref, hidden_ref, target_ref, back_ref, sem, sem_in,
+    ) = refs[-14:]
+    _, tokens = key_ref.shape
+    half = pack_ref.shape[1]
+    block = min(1024, tokens)
+    count = tokens // block
+    wide_at = lax.axis_index("wide")
+    narrow_at = lax.axis_index("narrow")
+    role = narrow_at ^ (wide_at // owned)
+
+    def moved(keys, values, index, slot):
+        source = slice(index * block, (index + 1) * block)
+        target = slice(slot * block, (slot + 1) * block)
+        return (
+            pltpu.make_async_copy(keys.at[:, source], keys_ref.at[:, target], sem_in.at[0, slot]),
+            pltpu.make_async_copy(
+                values.at[:, source], values_ref.at[:, target], sem_in.at[1, slot]
+            ),
+        )
+
+    for place, source in enumerate(sources):
+
+        @pl.when(role == place)
+        def _(source=source):
+            pltpu.make_async_copy(source, pack_ref, sem).start()
+
+    arrivals = [moved(key_ref, value_ref, index, index) for index in range(count)]
+    arrivals += [moved(pair_key_ref, pair_value_ref, index, count + index) for index in range(count)]
+    for copies in arrivals:
+        for copy in copies:
+            copy.start()
+    pltpu.make_async_copy(sources[0], pack_ref, sem).wait()
+    gate_lift = jnp.concatenate([pack_ref[0] * jnp.bfloat16(0.5), pack_ref[1]], axis=0)
+    down = pack_ref[2]
+    for slot, copies in enumerate(arrivals):
+        for copy in copies:
+            copy.wait()
+        at = slice(slot * block, (slot + 1) * block)
+        begin = (narrow_at ^ (slot // count)) * tokens + (slot % count) * block
+        rates = rate_ref[pl.ds(wide_at, 1), pl.ds(pl.multiple_of(begin, block), block)]
+        pre = jnp.dot(gate_lift, keys_ref[:, at], preferred_element_type=jnp.float32)
+        target = (values_ref[:, at].astype(jnp.float32) * -rates).astype(jnp.bfloat16)
+        target_ref[:, at] = target
+        back_hidden = jnp.dot(down, target, preferred_element_type=jnp.float32)
+        half_gate = pre[:half]
+        pre_lift = pre[half:]
+        twice = jnp.tanh(half_gate) + 1.0
+        silu_gate = half_gate * twice
+        hidden_ref[:, at] = (silu_gate * pre_lift).astype(jnp.bfloat16)
+        slope = twice + silu_gate * (2.0 - twice)
+        back_ref[:half, at] = (back_hidden * pre_lift * slope).astype(jnp.bfloat16)
+        back_ref[half:, at] = (back_hidden * silu_gate).astype(jnp.bfloat16)
+    contract = (((1,), (1,)), ((), ()))
+    sums = lax.dot_general(
+        back_ref[...], keys_ref[...], contract, preferred_element_type=jnp.float32
+    )
+    down_sums = lax.dot_general(
+        hidden_ref[...], target_ref[...], contract, preferred_element_type=jnp.float32
+    )
+    for place, value in enumerate((sums[:half] * 0.5, sums[half:], down_sums)):
+        send_ref[place] = value.astype(jnp.bfloat16)
+
+
+def fast_sums(sources, keys, values, pair_keys, pair_values, rates, owned):
+    features, tokens = keys.shape
+    shape = sources[0].shape
+    half = shape[1]
+    block = min(1024, tokens)
+    resident = pl.BlockSpec(memory_space=pltpu.VMEM)
+    return pl.pallas_call(
+        functools.partial(sums_body, owned=owned),
+        out_shape=(jax.ShapeDtypeStruct(shape, jnp.bfloat16),) * 2,
+        in_specs=anywhere(len(sources) + 4) + [resident],
+        out_specs=(resident,) * 2,
+        scratch_shapes=[
+            pltpu.VMEM((features, 2 * tokens), jnp.bfloat16),
+            pltpu.VMEM((features, 2 * tokens), jnp.bfloat16),
+            pltpu.VMEM((half, 2 * tokens), jnp.bfloat16),
+            pltpu.VMEM((features, 2 * tokens), jnp.bfloat16),
+            pltpu.VMEM((2 * half, 2 * tokens), jnp.bfloat16),
+            pltpu.SemaphoreType.DMA(()),
+            pltpu.SemaphoreType.DMA((2, 2 * tokens // block)),
+        ],
+        cost_estimate=pl.CostEstimate(
+            flops=24 * half * features * tokens,
+            bytes_accessed=8 * features * tokens + 6 * 3 * half * features,
+            transcendentals=2 * half * tokens,
+        ),
+        name="fast_sums",
+        compiler_params=pltpu.CompilerParams(vmem_limit_bytes=VMEM_GRANT),
+    )(*sources, keys, values, pair_keys, pair_values, rates)
+
+
+def recall_body(mine_ref, other_ref, pack_ref, pair_pack_ref, query_ref, out_ref, w_ref, fresh_ref, turned_ref, sem):
+    half = mine_ref.shape[1]
+    nt = (((1,), (1,)), ((), ()))
+
+    @pl.when(pl.program_id(0) == 0)
+    def _():
+        side = lax.axis_index("narrow") % 2
+        copies = [
+            pltpu.make_async_copy(
+                source, target.at[:, half_rows(part, half)], sem.at[place]
+            )
+            for place, (source, target, part) in enumerate(
+                (
+                    (mine_ref, fresh_ref, side),
+                    (other_ref, fresh_ref, 1 - side),
+                    (pack_ref, w_ref, side),
+                    (pair_pack_ref, w_ref, 1 - side),
+                )
+            )
+        ]
+        for copy in copies:
+            copy.start()
+        copies[0].wait()
+        copies[1].wait()
+        current = []
+        for i in range(3):
+            widened = fresh_ref[i].astype(jnp.float32)
+            total = jnp.sum(jnp.sum(widened * widened, axis=0, keepdims=True), axis=1, keepdims=True)
+            current.append((widened * lax.rsqrt(total + EPS)).astype(jnp.bfloat16))
+        for _ in range(NS_ITERS):
+            gram = [
+                lax.dot_general(x, x, nt, preferred_element_type=jnp.float32).astype(jnp.bfloat16)
+                for x in current
+            ]
+            lifted = [
+                jnp.dot(g, x, preferred_element_type=jnp.float32).astype(jnp.bfloat16)
+                for x, g in zip(current, gram)
+            ]
+            current = [
+                (
+                    COEF_A * x.astype(jnp.float32)
+                    + COEF_B * y.astype(jnp.float32)
+                    + COEF_C * jnp.dot(g, y, preferred_element_type=jnp.float32)
+                ).astype(jnp.bfloat16)
+                for x, y, g in zip(current, lifted, gram)
+            ]
+        copies[2].wait()
+        copies[3].wait()
+        for i in range(3):
+            axis = 0 if i == 2 else 1
+            initial = w_ref[i].astype(jnp.float32)
+            moved = initial - current[i].astype(jnp.float32)
+            wanted = jnp.mean(jnp.square(initial), axis=axis, keepdims=True) + EPS
+            present = jnp.mean(jnp.square(moved), axis=axis, keepdims=True) + EPS
+            fresh = (moved * (wanted * lax.rsqrt(wanted * present))).astype(jnp.bfloat16)
+            if i == 2:
+                turned_ref[...] = fresh.T
+            else:
+                fresh_ref[i] = fresh
+
+    hidden_rows, features = fresh_ref.shape[1:]
+    pre = jnp.dot(
+        fresh_ref[0:2].reshape(2 * hidden_rows, features),
+        query_ref[...],
+        preferred_element_type=jnp.float32,
+    )
+    gate = 0.5 * pre[:hidden_rows]
+    hidden = (gate * (jnp.tanh(gate) + 1.0) * pre[hidden_rows:]).astype(jnp.bfloat16)
+    out_ref[...] = jnp.dot(turned_ref[...], hidden, preferred_element_type=jnp.float32).astype(
+        jnp.bfloat16
+    )
+
+
+def fast_recall(mine, other, pack, pair_pack, queries):
+    features, tokens = queries.shape
+    half = mine.shape[1]
+    hidden_rows = 2 * half
+    block = min(512, tokens)
+    piece = pl.BlockSpec((features, block), lambda i: (0, i))
+    return pl.pallas_call(
+        recall_body,
+        out_shape=jax.ShapeDtypeStruct((features, tokens), jnp.bfloat16),
+        grid=(tokens // block,),
+        in_specs=anywhere(4) + [piece],
+        out_specs=piece,
+        scratch_shapes=[
+            pltpu.VMEM((3, hidden_rows, features), jnp.bfloat16),
+            pltpu.VMEM((3, hidden_rows, features), jnp.bfloat16),
+            pltpu.VMEM((features, hidden_rows), jnp.bfloat16),
+            pltpu.SemaphoreType.DMA((4,)),
+        ],
+        cost_estimate=pl.CostEstimate(
+            flops=6 * hidden_rows * features * tokens + 18 * NS_ITERS * hidden_rows * features**2,
+            bytes_accessed=4 * features * tokens + 12 * hidden_rows * features,
+            transcendentals=hidden_rows * tokens,
+        ),
+        name="fast_recall",
+        compiler_params=pltpu.CompilerParams(vmem_limit_bytes=VMEM_GRANT),
+    )(mine, other, pack, pair_pack, queries)
+
+
+def in_place(query_states, key_states, value_states, cache_keys, cache_values, gate_fast, *rest):
+    features, tok_count = query_states.shape
+    narrow_count = lax.axis_size("narrow")
+    return (
+        features == FD
+        and gate_fast.shape[1:] == (FD, FD)
+        and features % HEAD_SIZE == 0
+        and tok_count % WINDOW == 0
+        and tok_count >= 2 * WINDOW
+        and narrow_count >= 2
+        and narrow_count & (narrow_count - 1) == 0
+    )
+
+
+def in_place_plan(
+    query_states,
+    key_states,
+    value_states,
+    cache_keys,
+    cache_values,
+    gate_fast,
+    lift_fast,
+    down_fast,
+    token_rates,
+):
+    wide_count = lax.axis_size("wide")
+    narrow_count = lax.axis_size("narrow")
+    owned = gate_fast.shape[0]
+
+    def from_owner(value, step):
+        pairs = []
+        for wide in range(wide_count):
+            start = wide * narrow_count
+            owner = wide // owned
+            pairs.append((start + owner, start + (owner ^ step)))
+        return lax.ppermute(value, ("wide", "narrow"), pairs)
+
+    own, other = prepare(gate_fast, lift_fast, down_fast)
+    arrivals = {}
+    for step in reversed(range(1, narrow_count)):
+        arrivals[step] = from_owner((own, other)[step % 2], step)
+    pair_keys = swapped(key_states, "narrow", 0)
+    pair_values = swapped(value_states, "narrow", 0)
+    ends = edges(key_states, value_states)
+    late = attend_late(query_states, key_states, value_states)
+    sources = [own] + [arrivals[step] for step in range(1, narrow_count)]
+    sources, late, ends = lax.optimization_barrier((sources, late, ends))
+    prior = from_behind(ends, "narrow", 1)
+    total, pack = fast_sums(
+        sources, key_states, value_states, pair_keys, pair_values, token_rates, owned
+    )
+    pair_pack = swapped(pack, "narrow", 0)
+    for distance in range(1, narrow_count.bit_length() - 1):
+        partner = swapped(total, "narrow", distance)
+        total = stored(total.astype(jnp.float32) + partner.astype(jnp.float32))
+    theirs = swapped(total, "narrow", 0)
+    attended = attend_early(
+        query_states, key_states, value_states, prior, cache_keys, cache_values, late
+    )
+    recalled = fast_recall(total, theirs, pack, pair_pack, query_states)
+    return (attended, recalled)
+
+
+def spread_plan(
     query_states,
     key_states,
     value_states,
@@ -273,6 +765,12 @@
     return (attended, recalled)
 
 
+def per_device(*arrays):
+    if in_place(*arrays):
+        return in_place_plan(*arrays)
+    return spread_plan(*arrays)
+
+
 def solution(mesh):
     in_specs = (
         P("wide", "narrow"),

time: 710 us -> 97.7 us (0.14)
  the two profiles are of different devices: /device:TPU:0 before, /device:TPU:13 now
where the time goes in v3:
time: 97.7 us; the launch traced here: 97.3 us
  Pallas kernels  53.1 us (54%)
  waiting for transfers between devices  26.9 us (28%)
  starting transfers between devices  14.2 us (15%)
  other arithmetic  2.24 us (2%)
    ppermute x5, waiting for transfers between devices, swapped(): lax.ppermute(array, axis, [(i, i ^ 1 << distance) for i in range(lax.axis...  26.8 us
    pallas_call x1, Pallas kernels, fast_recall(): pl.pallas_call(recall_body, out_shape=jax.ShapeDtypeStruct((features, tok...  14.5 us
    pallas_call x1, Pallas kernels, fast_sums(): pl.pallas_call(functools.partial(sums_body, owned=owned), out_shape=(jax....  13.5 us
    pallas_call x1, Pallas kernels, attend_early(): pl.pallas_call(early_body, out_shape=jax.ShapeDtypeStruct((features, toke...  10.5 us
    pallas_call x1, Pallas kernels, attend_late(): pl.pallas_call(functools.partial(attend_body, block=min(256, WINDOW), win...  9.72 us
    ppermute x5, starting transfers between devices, swapped(): lax.ppermute(array, axis, [(i, i ^ 1 << distance) for i in range(lax.axis...  8.37 us
    ppermute x3, starting transfers between devices, from_owner(): return lax.ppermute(value, ('wide', 'narrow'), pairs)  4.5 us
    pallas_call x1, Pallas kernels, prepare(): pl.pallas_call(prepare_body, out_shape=(jax.ShapeDtypeStruct(shape, jnp.b...  2.47 us
  transfers between devices with their start and end apart: 9, of which 1 were waited for; matrix products, arithmetic and copies ran while one was open for 2% of the time, Pallas kernels for 40%

profile of v3, /device:TPU:13, one launch (start us, length us, event | category | flops | bytes accessed | tf_op | source)
XLA Modules:
  0.0 97.3 jit_solution(5254062726931192270)
XLA Ops:
  0.6 0.7 collective-permute-start.4
  1.4 0.1 collective-permute-start.5
  1.5 2.5 %prepare.1 = (bf16[3,256,512]{2,1,0:T(8,128)(2,1)}, bf16[3,256,512]{2,1,0:T(8,128)(2,1)}) custom-call(bf16[2,512,512]{2,1,0:T(8,128)(2,1)} %gate_ref.1, bf16[2,512,512]{2,1,0:T(8,128)(2,1)} %lift_ref.1, bf16[2,512,512]{2,1,0:T(8,128)(2,1)} %down_ref.1), custom_call_target="tpu_custom_call" | custom-call | bytes 3145728 | tf_op jit(solution)/shard_map/prepare/pallas_call | solution.py:372
  3.9 1.3 %collective-permute-start.1 = (bf16[3,256,512]{2,1,0:T(8,128)(2,1)}, bf16[3,256,512]{2,1,0:T(8,128)(2,1)}, u32[]{:S(2)}, u32[]{:S(2)}) collective-permute-start(bf16[3,256,512]{2,1,0:T(8,128)(2,1)} %get-tuple-element.16.refs_0_), channel_id=1, source_target_pairs={{0,2},{4,6},{9,11},{13,15},{18,16},{22,20},{27,25},{31,29}} | collective-permute-start | bytes 2359304 | tf_op jit(solution)/shard_map/ppermute | solution.py:665
  5.2 1.6 %collective-permute-start.2 = (bf16[3,256,512]{2,1,0:T(8,128)(2,1)}, bf16[3,256,512]{2,1,0:T(8,128)(2,1)}, u32[]{:S(2)}, u32[]{:S(2)}) collective-permute-start(bf16[3,256,512]{2,1,0:T(8,128)(2,1)} %get-tuple-element.13), channel_id=1, source_target_pairs={{0,3},{4,7},{9,10},{13,14},{18,17},{22,21},{27,24},{31,28}} | collective-permute-start | bytes 2359304 | tf_op jit(solution)/shard_map/ppermute | solution.py:665
  6.8 1.7 %collective-permute-start = (bf16[3,256,512]{2,1,0:T(8,128)(2,1)}, bf16[3,256,512]{2,1,0:T(8,128)(2,1)}, u32[]{:S(2)}, u32[]{:S(2)}) collective-permute-start(bf16[3,256,512]{2,1,0:T(8,128)(2,1)} %get-tuple-element.13), channel_id=1, source_target_pairs={{0,1},{4,5},{9,8},{13,12},{18,19},{22,23},{27,26},{31,30}} | collective-permute-start | bytes 2359304 | tf_op jit(solution)/shard_map/ppermute | solution.py:665
  8.4 2.4 %edges.1 = bf16[2,512,1024]{2,1,0:T(8,128)(2,1)} custom-call(bf16[512,2048]{1,0:T(8,128)(2,1)} %refs_4_.3, bf16[512,2048]{1,0:T(8,128)(2,1)} %refs_5_.3), custom_call_target="tpu_custom_call" | custom-call | bytes 4194304 | tf_op jit(solution)/shard_map/edges/pallas_call | solution.py:415
  10.8 9.7 %attend_late.1.refs_7_ = bf16[512,2048]{1,0:T(8,128)(2,1)} custom-call(bf16[512,2048]{1,0:T(8,128)(2,1)} %query_ref.1, bf16[512,2048]{1,0:T(8,128)(2,1)} %refs_4_.3, bf16[512,2048]{1,0:T(8,128)(2,1)} %refs_5_.3, bf16[512,2048]{1,0:T(8,128)(2,1)} %refs_4_.3, bf16[512,2048]{1,0:T(8,128)(2,1)} %refs_5_.3), custom_call_target="tpu_custom_call" | custom-call | flops 2684354560 | bytes 5242880 | tf_op jit(solution)/shard_map/attend_late/pallas_call | solution.py:287
  20.6 0.0 collective-permute-done.1.refs_2_
  20.6 0.0 collective-permute-done.2.refs_3_
  20.6 0.0 collective-permute-done.refs_1_
  20.6 1.3 %collective-permute-start.3 = (bf16[2,512,1024]{2,1,0:T(8,128)(2,1)}, bf16[2,512,1024]{2,1,0:T(8,128)(2,1)}, u32[]{:S(2)}, u32[]{:S(2)}) collective-permute-start(bf16[2,512,1024]{2,1,0:T(8,128)(2,1)} %edges.1), channel_id=1, source_target_pairs={{0,1},{1,2},{2,3},{4,5},{5,6},{6,7},{8,9},{9,10},{10,11},{12,13},{... | collective-permute-start | bytes 6291464 | tf_op jit(solution)/shard_map/ppermute | solution.py:41
  21.9 0.0 collective-permute-done.4.refs_6_
  21.9 0.0 collective-permute-done.5.refs_7_
  21.9 13.5 %fast_sums.1 = (bf16[3,256,512]{2,1,0:T(8,128)(2,1)}, bf16[3,256,512]{2,1,0:T(8,128)(2,1)}) custom-call(bf16[3,256,512]{2,1,0:T(8,128)(2,1)} %get-tuple-element.16.refs_0_, bf16[3,256,512]{2,1,0:T(8,128)(2,1)} %collective-permute-done.refs_1_, bf16[3,256,512]{2,1,0:T(8,128)(2,1)} %collective-permute-done.1.refs_2_, ...), custom_call_target="tpu_custom_call" | custom-call | flops 6442450944 | bytes 10747904 | tf_op jit(solution)/shard_map/fast_sums/pallas_call | solution.py:505
  35.4 7.5 %collective-permute-start.6 = (bf16[3,256,512]{2,1,0:T(8,128)(2,1)}, bf16[3,256,512]{2,1,0:T(8,128)(2,1)S(1)}, u32[]{:S(2)}, u32[]{:S(2)}) collective-permute-start(bf16[3,256,512]{2,1,0:T(8,128)(2,1)} %get-tuple-element.20), channel_id=1, source_target_pairs={{0,2},{1,3},{2,0},{3,1},{4,6},{5,7},{6,4},{7,5},{8,10},{9,11},{10,... | collective-permute-start | bytes 2359304 | tf_op jit(solution)/shard_map/ppermute | solution.py:27
  43.0 0.0 collective-permute-start.8
  43.0 26.8 %collective-permute-done.6 = bf16[3,256,512]{2,1,0:T(8,128)(2,1)S(1)} collective-permute-done((bf16[3,256,512]{2,1,0:T(8,128)(2,1)}, bf16[3,256,512]{2,1,0:T(8,128)(2,1)S(1)}, u32[]{:S(2)}, u32[]{:S(2)}) %collective-permute-start.6) | collective-permute-done | bytes 786464 | tf_op jit(solution)/shard_map/ppermute | solution.py:27
  69.8 2.2 %add_convert_fusion.mine_ref = bf16[3,256,512]{2,1,0:T(8,128)(2,1)} fusion(bf16[3,256,512]{2,1,0:T(8,128)(2,1)S(1)} %collective-permute-done.6, bf16[3,256,512]{2,1,0:T(8,128)(2,1)} %get-tuple-element.20), kind=kLoop, calls=%fused_computation | loop fusion | flops 1572864 | bytes 2359296 | tf_op jit(solution)/shard_map/convert_element_type | solution.py:45
  72.1 0.0 collective-permute-start.7
  72.1 0.0 collective-permute-done.3.refs_1_.refs_2_
  72.1 10.5 %attend_early.1 = bf16[512,2048]{1,0:T(8,128)(2,1)} custom-call(bf16[512,2048]{1,0:T(8,128)(2,1)} %query_ref.1, bf16[2,512,1024]{2,1,0:T(8,128)(2,1)} %collective-permute-done.3.refs_1_.refs_2_, bf16[2,512,1024]{2,1,0:T(8,128)(2,1)} %collective-permute-done.3.refs_1_.refs_2_, bf16[512,2048]{1,0:T(8,128)(2,1)} %refs_4_.3, ...), custom_call_target="tpu_custom_call", output_to_operand_aliasing={{}: (7, {})} | custom-call | flops 2684354560 | bytes 7340032 | tf_op jit(solution)/shard_map/attend_early/pallas_call | solution.py:314
  82.5 0.0 collective-permute-done.8.pair_pack_ref
  82.6 0.0 collective-permute-done.7.other_ref
  82.6 14.5 %fast_recall.1 = bf16[512,2048]{1,0:T(8,128)(2,1)} custom-call(bf16[3,256,512]{2,1,0:T(8,128)(2,1)} %add_convert_fusion.mine_ref, bf16[3,256,512]{2,1,0:T(8,128)(2,1)} %collective-permute-done.7.other_ref, bf16[3,256,512]{2,1,0:T(8,128)(2,1)} %get-tuple-element.21.pack_ref, bf16[3,256,512]{2,1,0:T(8,128)(2,1)} %collective-permute-done.8.pair_pack_ref, ...), custom_call_target="tpu_custom_call" | custom-call | flops 8053063680 | bytes 7340032 | tf_op jit(solution)/shard_map/fast_recall/pallas_call | solution.py:608
Async XLA Ops:
  0.6 21.3 %collective-permute-start.4 = (bf16[512,2048]{1,0:T(8,128)(2,1)}, bf16[512,2048]{1,0:T(8,128)(2,1)}, u32[]{:S(2)}, u32[]{:S(2)}) collective-permute-start(bf16[512,2048]{1,0:T(8,128)(2,1)} %refs_4_.3), channel_id=1, source_target_pairs={{0,1},{1,0},{2,3},{3,2},{4,5},{5,4},{6,7},{7,6},{8,9},{9,8},{10,11... | collective-permute-start | bytes 6291464 | tf_op jit(solution)/shard_map/ppermute | solution.py:27
  1.4 20.5 %collective-permute-start.5 = (bf16[512,2048]{1,0:T(8,128)(2,1)}, bf16[512,2048]{1,0:T(8,128)(2,1)}, u32[]{:S(2)}, u32[]{:S(2)}) collective-permute-start(bf16[512,2048]{1,0:T(8,128)(2,1)} %refs_5_.3), channel_id=1, source_target_pairs={{0,1},{1,0},{2,3},{3,2},{4,5},{5,4},{6,7},{7,6},{8,9},{9,8},{10,11... | collective-permute-start | bytes 6291464 | tf_op jit(solution)/shard_map/ppermute | solution.py:27
  3.9 16.6 %collective-permute-start.1 = (bf16[3,256,512]{2,1,0:T(8,128)(2,1)}, bf16[3,256,512]{2,1,0:T(8,128)(2,1)}, u32[]{:S(2)}, u32[]{:S(2)}) collective-permute-start(bf16[3,256,512]{2,1,0:T(8,128)(2,1)} %get-tuple-element.16.refs_0_), channel_id=1, source_target_pairs={{0,2},{4,6},{9,11},{13,15},{18,16},{22,20},{27,25},{31,29}} | collective-permute-start | bytes 2359304 | tf_op jit(solution)/shard_map/ppermute | solution.py:665
  5.2 15.3 %collective-permute-start.2 = (bf16[3,256,512]{2,1,0:T(8,128)(2,1)}, bf16[3,256,512]{2,1,0:T(8,128)(2,1)}, u32[]{:S(2)}, u32[]{:S(2)}) collective-permute-start(bf16[3,256,512]{2,1,0:T(8,128)(2,1)} %get-tuple-element.13), channel_id=1, source_target_pairs={{0,3},{4,7},{9,10},{13,14},{18,17},{22,21},{27,24},{31,28}} | collective-permute-start | bytes 2359304 | tf_op jit(solution)/shard_map/ppermute | solution.py:665
  6.8 13.8 %collective-permute-start = (bf16[3,256,512]{2,1,0:T(8,128)(2,1)}, bf16[3,256,512]{2,1,0:T(8,128)(2,1)}, u32[]{:S(2)}, u32[]{:S(2)}) collective-permute-start(bf16[3,256,512]{2,1,0:T(8,128)(2,1)} %get-tuple-element.13), channel_id=1, source_target_pairs={{0,1},{4,5},{9,8},{13,12},{18,19},{22,23},{27,26},{31,30}} | collective-permute-start | bytes 2359304 | tf_op jit(solution)/shard_map/ppermute | solution.py:665
  20.6 51.5 %collective-permute-start.3 = (bf16[2,512,1024]{2,1,0:T(8,128)(2,1)}, bf16[2,512,1024]{2,1,0:T(8,128)(2,1)}, u32[]{:S(2)}, u32[]{:S(2)}) collective-permute-start(bf16[2,512,1024]{2,1,0:T(8,128)(2,1)} %edges.1), channel_id=1, source_target_pairs={{0,1},{1,2},{2,3},{4,5},{5,6},{6,7},{8,9},{9,10},{10,11},{12,13},{... | collective-permute-start | bytes 6291464 | tf_op jit(solution)/shard_map/ppermute | solution.py:41
  35.4 34.4 %collective-permute-start.6 = (bf16[3,256,512]{2,1,0:T(8,128)(2,1)}, bf16[3,256,512]{2,1,0:T(8,128)(2,1)S(1)}, u32[]{:S(2)}, u32[]{:S(2)}) collective-permute-start(bf16[3,256,512]{2,1,0:T(8,128)(2,1)} %get-tuple-element.20), channel_id=1, source_target_pairs={{0,2},{1,3},{2,0},{3,1},{4,6},{5,7},{6,4},{7,5},{8,10},{9,11},{10,... | collective-permute-start | bytes 2359304 | tf_op jit(solution)/shard_map/ppermute | solution.py:27
  43.0 39.6 %collective-permute-start.8 = (bf16[3,256,512]{2,1,0:T(8,128)(2,1)}, bf16[3,256,512]{2,1,0:T(8,128)(2,1)}, u32[]{:S(2)}, u32[]{:S(2)}) collective-permute-start(bf16[3,256,512]{2,1,0:T(8,128)(2,1)} %get-tuple-element.21.pack_ref), channel_id=1, source_target_pairs={{0,1},{1,0},{2,3},{3,2},{4,5},{5,4},{6,7},{7,6},{8,9},{9,8},{10,11... | collective-permute-start | bytes 2359304 | tf_op jit(solution)/shard_map/ppermute | solution.py:27
  72.1 10.5 %collective-permute-start.7 = (bf16[3,256,512]{2,1,0:T(8,128)(2,1)}, bf16[3,256,512]{2,1,0:T(8,128)(2,1)}, u32[]{:S(2)}, u32[]{:S(2)}) collective-permute-start(bf16[3,256,512]{2,1,0:T(8,128)(2,1)} %add_convert_fusion.mine_ref), channel_id=1, source_target_pairs={{0,1},{1,0},{2,3},{3,2},{4,5},{5,4},{6,7},{7,6},{8,9},{9,8},{10,11... | collective-permute-start | bytes 2359304 | tf_op jit(solution)/shard_map/ppermute | solution.py:27

commit v4 on v3

--- a/solution.py
+++ b/solution.py
@@ -300,10 +300,10 @@
     )(queries, keys, values, keys, values)
 
 
-def attend_early(queries, keys, values, prior, cache_keys, cache_values, late):
+def attend_early(queries, keys, values, prior, cache_keys, cache_values, late, part):
     features, tokens = queries.shape
-    heads = features // HEAD_SIZE
-    here = pl.BlockSpec((HEAD_SIZE, WINDOW), lambda h: (h, 0))
+    heads = prior.shape[1] // HEAD_SIZE
+    here = pl.BlockSpec((HEAD_SIZE, WINDOW), lambda h: (h + part * heads, 0))
     prior_keys = pl.BlockSpec((None, HEAD_SIZE, WINDOW), lambda h: (0, h, 0))
     prior_values = pl.BlockSpec((None, HEAD_SIZE, WINDOW), lambda h: (1, h, 0))
     body = functools.partial(attend_body, block=min(256, WINDOW), window=WINDOW)
@@ -321,8 +321,8 @@
         scratch_shapes=attend_scratch(),
         input_output_aliases={7: 0},
         cost_estimate=pl.CostEstimate(
-            flops=5 * features * WINDOW**2,
-            bytes_accessed=14 * features * WINDOW,
+            flops=5 * heads * HEAD_SIZE * WINDOW**2,
+            bytes_accessed=14 * heads * HEAD_SIZE * WINDOW,
             transcendentals=heads * WINDOW**2,
         ),
         name="attend_early",
@@ -386,19 +386,19 @@
     )(gate_fast, lift_fast, down_fast)
 
 
-def edges_body(key_ref, value_ref, out_ref, held_ref, sem):
-    features, tokens = key_ref.shape
-    rows = min(HEAD_SIZE, features)
-    window = out_ref.shape[2]
+def edges_body(key_ref, value_ref, *refs):
+    out_refs, (held_ref, sem) = refs[:-2], refs[-2:]
+    _, tokens = key_ref.shape
+    rows, window = out_refs[0].shape[1:]
     moves = []
-    for place, source in enumerate((key_ref, value_ref)):
-        for part in range(features // rows):
-            at = slice(part * rows, (part + 1) * rows)
+    for part, out_ref in enumerate(out_refs):
+        at = slice(part * rows, (part + 1) * rows)
+        for place, source in enumerate((key_ref, value_ref)):
             arriving = pltpu.make_async_copy(
                 source.at[at, tokens - window :], held_ref.at[place, at], sem.at[0, place, part]
             )
             leaving = pltpu.make_async_copy(
-                held_ref.at[place, at], out_ref.at[place, at], sem.at[1, place, part]
+                held_ref.at[place, at], out_ref.at[place], sem.at[1, place, part]
             )
             arriving.start()
             moves.append((arriving, leaving))
@@ -409,17 +409,16 @@
         leaving.wait()
 
 
-def edges(keys, values):
+def edges(keys, values, parts):
     features = keys.shape[0]
-    shape = (2, features, WINDOW)
     return pl.pallas_call(
         edges_body,
-        out_shape=jax.ShapeDtypeStruct(shape, jnp.bfloat16),
+        out_shape=(jax.ShapeDtypeStruct((2, features // parts, WINDOW), jnp.bfloat16),) * parts,
         in_specs=anywhere(2),
-        out_specs=pl.BlockSpec(memory_space=pl.ANY),
+        out_specs=tuple(anywhere(parts)),
         scratch_shapes=[
-            pltpu.VMEM(shape, jnp.bfloat16),
-            pltpu.SemaphoreType.DMA((2, 2, features // min(HEAD_SIZE, features))),
+            pltpu.VMEM((2, features, WINDOW), jnp.bfloat16),
+            pltpu.SemaphoreType.DMA((2, 2, parts)),
         ],
         cost_estimate=pl.CostEstimate(
             flops=0, bytes_accessed=8 * features * WINDOW, transcendentals=0
@@ -526,7 +525,10 @@
     )(*sources, keys, values, pair_keys, pair_values, rates)
 
 
-def recall_body(mine_ref, other_ref, pack_ref, pair_pack_ref, query_ref, out_ref, w_ref, fresh_ref, turned_ref, sem):
+def recall_body(
+    mine_ref, other_ref, far_ref, other_far_ref, pack_ref, pair_pack_ref, query_ref, out_ref,
+    w_ref, fresh_ref, far_sums_ref, turned_ref, sem,
+):
     half = mine_ref.shape[1]
     nt = (((1,), (1,)), ((), ()))
 
@@ -541,6 +543,8 @@
                 (
                     (mine_ref, fresh_ref, side),
                     (other_ref, fresh_ref, 1 - side),
+                    (far_ref, far_sums_ref, side),
+                    (other_far_ref, far_sums_ref, 1 - side),
                     (pack_ref, w_ref, side),
                     (pair_pack_ref, w_ref, 1 - side),
                 )
@@ -548,11 +552,12 @@
         ]
         for copy in copies:
             copy.start()
-        copies[0].wait()
-        copies[1].wait()
+        for copy in copies[:4]:
+            copy.wait()
         current = []
         for i in range(3):
-            widened = fresh_ref[i].astype(jnp.float32)
+            summed = fresh_ref[i].astype(jnp.float32) + far_sums_ref[i].astype(jnp.float32)
+            widened = summed.astype(jnp.bfloat16).astype(jnp.float32)
             total = jnp.sum(jnp.sum(widened * widened, axis=0, keepdims=True), axis=1, keepdims=True)
             current.append((widened * lax.rsqrt(total + EPS)).astype(jnp.bfloat16))
         for _ in range(NS_ITERS):
@@ -572,8 +577,8 @@
                 ).astype(jnp.bfloat16)
                 for x, y, g in zip(current, lifted, gram)
             ]
-        copies[2].wait()
-        copies[3].wait()
+        for copy in copies[4:]:
+            copy.wait()
         for i in range(3):
             axis = 0 if i == 2 else 1
             initial = w_ref[i].astype(jnp.float32)
@@ -599,9 +604,9 @@
     )
 
 
-def fast_recall(mine, other, pack, pair_pack, queries):
+def fast_recall(sums, packs, queries):
     features, tokens = queries.shape
-    half = mine.shape[1]
+    half = packs[0].shape[1]
     hidden_rows = 2 * half
     block = min(512, tokens)
     piece = pl.BlockSpec((features, block), lambda i: (0, i))
@@ -609,13 +614,14 @@
         recall_body,
         out_shape=jax.ShapeDtypeStruct((features, tokens), jnp.bfloat16),
         grid=(tokens // block,),
-        in_specs=anywhere(4) + [piece],
+        in_specs=anywhere(6) + [piece],
         out_specs=piece,
         scratch_shapes=[
             pltpu.VMEM((3, hidden_rows, features), jnp.bfloat16),
             pltpu.VMEM((3, hidden_rows, features), jnp.bfloat16),
+            pltpu.VMEM((3, hidden_rows, features), jnp.bfloat16),
             pltpu.VMEM((features, hidden_rows), jnp.bfloat16),
-            pltpu.SemaphoreType.DMA((4,)),
+            pltpu.SemaphoreType.DMA((6,)),
         ],
         cost_estimate=pl.CostEstimate(
             flops=6 * hidden_rows * features * tokens + 18 * NS_ITERS * hidden_rows * features**2,
@@ -624,7 +630,7 @@
         ),
         name="fast_recall",
         compiler_params=pltpu.CompilerParams(vmem_limit_bytes=VMEM_GRANT),
-    )(mine, other, pack, pair_pack, queries)
+    )(*sums, *packs, queries)
 
 
 def in_place(query_states, key_states, value_states, cache_keys, cache_values, gate_fast, *rest):
@@ -636,7 +642,7 @@
         and features % HEAD_SIZE == 0
         and tok_count % WINDOW == 0
         and tok_count >= 2 * WINDOW
-        and narrow_count >= 2
+        and narrow_count >= 4
         and narrow_count & (narrow_count - 1) == 0
     )
 
@@ -670,23 +676,30 @@
         arrivals[step] = from_owner((own, other)[step % 2], step)
     pair_keys = swapped(key_states, "narrow", 0)
     pair_values = swapped(value_states, "narrow", 0)
-    ends = edges(key_states, value_states)
-    late = attend_late(query_states, key_states, value_states)
+    parts = 2
+    ends = edges(key_states, value_states, parts)
+    attended = attend_late(query_states, key_states, value_states)
     sources = [own] + [arrivals[step] for step in range(1, narrow_count)]
-    sources, late, ends = lax.optimization_barrier((sources, late, ends))
-    prior = from_behind(ends, "narrow", 1)
-    total, pack = fast_sums(
+    sources, attended, ends = lax.optimization_barrier((sources, attended, ends))
+    prior = []
+    for end in ends:
+        prior.append(from_behind(end, "narrow", 1))
+    near, pack = fast_sums(
         sources, key_states, value_states, pair_keys, pair_values, token_rates, owned
     )
+    distances = range(1, narrow_count.bit_length() - 1)
+    for distance in distances:
+        far = swapped(near, "narrow", distance)
+        if distance != distances[-1]:
+            near = stored(near.astype(jnp.float32) + far.astype(jnp.float32))
     pair_pack = swapped(pack, "narrow", 0)
-    for distance in range(1, narrow_count.bit_length() - 1):
-        partner = swapped(total, "narrow", distance)
-        total = stored(total.astype(jnp.float32) + partner.astype(jnp.float32))
-    theirs = swapped(total, "narrow", 0)
-    attended = attend_early(
-        query_states, key_states, value_states, prior, cache_keys, cache_values, late
-    )
-    recalled = fast_recall(total, theirs, pack, pair_pack, query_states)
+    pair_near = swapped(near, "narrow", 0)
+    pair_far = swapped(far, "narrow", 0)
+    for part, before in enumerate(prior):
+        attended = attend_early(
+            query_states, key_states, value_states, before, cache_keys, cache_values, attended, part
+        )
+    recalled = fast_recall((near, pair_near, far, pair_far), (pack, pair_pack), query_states)
     return (attended, recalled)
 
 

time: 97.7 us -> 104 us (1.064)
  the two profiles are of different devices: /device:TPU:13 before, /device:TPU:1 now
where the time goes in v4:
time: 104 us; the launch traced here: 103 us
  Pallas kernels  56.5 us (54%)
  waiting for transfers between devices  26.2 us (25%)
  starting transfers between devices  19.6 us (19%)
    pallas_call x1, Pallas kernels, fast_recall(): pl.pallas_call(recall_body, out_shape=jax.ShapeDtypeStruct((features, tok...  15.9 us
    ppermute x2, waiting for transfers between devices, from_behind(): lax.ppermute(value, axis, [(source, source + steps) for source in range(i...  13.8 us
    pallas_call x1, Pallas kernels, fast_sums(): pl.pallas_call(functools.partial(sums_body, owned=owned), out_shape=(jax....  13.5 us
    pallas_call x2, Pallas kernels, attend_early(): pl.pallas_call(early_body, out_shape=jax.ShapeDtypeStruct((features, toke...  12.4 us
    ppermute x6, waiting for transfers between devices, swapped(): lax.ppermute(array, axis, [(i, i ^ 1 << distance) for i in range(lax.axis...  12.3 us
    ppermute x6, starting transfers between devices, swapped(): lax.ppermute(array, axis, [(i, i ^ 1 << distance) for i in range(lax.axis...  10.7 us
    pallas_call x1, Pallas kernels, attend_late(): pl.pallas_call(functools.partial(attend_body, block=min(256, WINDOW), win...  9.72 us
    ppermute x3, starting transfers between devices, from_owner(): return lax.ppermute(value, ('wide', 'narrow'), pairs)  4.46 us
  transfers between devices with their start and end apart: 11, of which 3 were waited for; matrix products, arithmetic and copies ran while one was open for 0% of the time, Pallas kernels for 26%

profile of v4, /device:TPU:1, one launch (start us, length us, event | category | flops | bytes accessed | tf_op | source)
XLA Modules:
  0.0 103.1 jit_solution(105957140983763548)
XLA Ops:
  0.6 0.1 collective-permute-start.5
  0.7 0.5 collective-permute-start.6
  1.2 2.5 %prepare.1 = (bf16[3,256,512]{2,1,0:T(8,128)(2,1)}, bf16[3,256,512]{2,1,0:T(8,128)(2,1)}) custom-call(bf16[2,512,512]{2,1,0:T(8,128)(2,1)} %gate_ref.1, bf16[2,512,512]{2,1,0:T(8,128)(2,1)} %lift_ref.1, bf16[2,512,512]{2,1,0:T(8,128)(2,1)} %down_ref.1), custom_call_target="tpu_custom_call" | custom-call | bytes 3145728 | tf_op jit(solution)/shard_map/prepare/pallas_call | solution.py:372
  3.7 1.6 %collective-permute-start.1 = (bf16[3,256,512]{2,1,0:T(8,128)(2,1)}, bf16[3,256,512]{2,1,0:T(8,128)(2,1)}, u32[]{:S(2)}, u32[]{:S(2)}) collective-permute-start(bf16[3,256,512]{2,1,0:T(8,128)(2,1)} %get-tuple-element.22.refs_0_), channel_id=1, source_target_pairs={{0,2},{4,6},{9,11},{13,15},{18,16},{22,20},{27,25},{31,29}} | collective-permute-start | bytes 2359304 | tf_op jit(solution)/shard_map/ppermute | solution.py:671
  5.3 1.6 %collective-permute-start.2 = (bf16[3,256,512]{2,1,0:T(8,128)(2,1)}, bf16[3,256,512]{2,1,0:T(8,128)(2,1)}, u32[]{:S(2)}, u32[]{:S(2)}) collective-permute-start(bf16[3,256,512]{2,1,0:T(8,128)(2,1)} %get-tuple-element.16), channel_id=1, source_target_pairs={{0,3},{4,7},{9,10},{13,14},{18,17},{22,21},{27,24},{31,28}} | collective-permute-start | bytes 2359304 | tf_op jit(solution)/shard_map/ppermute | solution.py:671
  6.9 1.3 %collective-permute-start = (bf16[3,256,512]{2,1,0:T(8,128)(2,1)}, bf16[3,256,512]{2,1,0:T(8,128)(2,1)}, u32[]{:S(2)}, u32[]{:S(2)}) collective-permute-start(bf16[3,256,512]{2,1,0:T(8,128)(2,1)} %get-tuple-element.16), channel_id=1, source_target_pairs={{0,1},{4,5},{9,8},{13,12},{18,19},{22,23},{27,26},{31,30}} | collective-permute-start | bytes 2359304 | tf_op jit(solution)/shard_map/ppermute | solution.py:671
  8.2 2.4 %edges.1 = (bf16[2,256,1024]{2,1,0:T(8,128)(2,1)}, bf16[2,256,1024]{2,1,0:T(8,128)(2,1)}) custom-call(bf16[512,2048]{1,0:T(8,128)(2,1)} %refs_4_.5, bf16[512,2048]{1,0:T(8,128)(2,1)} %refs_5_.5), custom_call_target="tpu_custom_call" | custom-call | bytes 4194304 | tf_op jit(solution)/shard_map/edges/pallas_call | solution.py:414
  10.6 9.7 %attend_late.1.refs_7_ = bf16[512,2048]{1,0:T(8,128)(2,1)} custom-call(bf16[512,2048]{1,0:T(8,128)(2,1)} %query_ref.1, bf16[512,2048]{1,0:T(8,128)(2,1)} %refs_4_.5, bf16[512,2048]{1,0:T(8,128)(2,1)} %refs_5_.5, bf16[512,2048]{1,0:T(8,128)(2,1)} %refs_4_.5, bf16[512,2048]{1,0:T(8,128)(2,1)} %refs_5_.5), custom_call_target="tpu_custom_call" | custom-call | flops 2684354560 | bytes 5242880 | tf_op jit(solution)/shard_map/attend_late/pallas_call | solution.py:287
  20.3 0.0 collective-permute-done.1.refs_2_
  20.3 0.0 collective-permute-done.2.refs_3_
  20.3 0.0 collective-permute-done.refs_1_
  20.3 0.0 collective-permute-done.5.refs_6_
  20.4 0.0 collective-permute-done.6.refs_7_
  20.4 13.5 %fast_sums.1 = (bf16[3,256,512]{2,1,0:T(8,128)(2,1)}, bf16[3,256,512]{2,1,0:T(8,128)(2,1)}) custom-call(bf16[3,256,512]{2,1,0:T(8,128)(2,1)} %get-tuple-element.22.refs_0_, bf16[3,256,512]{2,1,0:T(8,128)(2,1)} %collective-permute-done.refs_1_, bf16[3,256,512]{2,1,0:T(8,128)(2,1)} %collective-permute-done.1.refs_2_, ...), custom_call_target="tpu_custom_call" | custom-call | flops 6442450944 | bytes 10747904 | tf_op jit(solution)/shard_map/fast_sums/pallas_call | solution.py:504
  33.9 8.1 %collective-permute-start.8 = (bf16[3,256,512]{2,1,0:T(8,128)(2,1)}, bf16[3,256,512]{2,1,0:T(8,128)(2,1)}, u32[]{:S(2)}, u32[]{:S(2)}) collective-permute-start(bf16[3,256,512]{2,1,0:T(8,128)(2,1)} %get-tuple-element.26.mine_ref), channel_id=1, source_target_pairs={{0,2},{1,3},{2,0},{3,1},{4,6},{5,7},{6,4},{7,5},{8,10},{9,11},{10,... | collective-permute-start | bytes 2359304 | tf_op jit(solution)/shard_map/ppermute | solution.py:27
  42.0 2.0 %collective-permute-start.4 = (bf16[2,256,1024]{2,1,0:T(8,128)(2,1)}, bf16[2,256,1024]{2,1,0:T(8,128)(2,1)}, u32[]{:S(2)}, u32[]{:S(2)}) collective-permute-start(bf16[2,256,1024]{2,1,0:T(8,128)(2,1)} %get-tuple-element.20), channel_id=1, source_target_pairs={{0,1},{1,2},{2,3},{4,5},{5,6},{6,7},{8,9},{9,10},{10,11},{12,13},{... | collective-permute-start | bytes 3145736 | tf_op jit(solution)/shard_map/ppermute | solution.py:41
  44.0 2.4 %collective-permute-start.3 = (bf16[2,256,1024]{2,1,0:T(8,128)(2,1)}, bf16[2,256,1024]{2,1,0:T(8,128)(2,1)}, u32[]{:S(2)}, u32[]{:S(2)}) collective-permute-start(bf16[2,256,1024]{2,1,0:T(8,128)(2,1)} %get-tuple-element.19), channel_id=1, source_target_pairs={{0,1},{1,2},{2,3},{4,5},{5,6},{6,7},{8,9},{9,10},{10,11},{12,13},{... | collective-permute-start | bytes 3145736 | tf_op jit(solution)/shard_map/ppermute | solution.py:41
  46.4 1.2 %collective-permute-start.7 = (bf16[3,256,512]{2,1,0:T(8,128)(2,1)}, bf16[3,256,512]{2,1,0:T(8,128)(2,1)}, u32[]{:S(2)}, u32[]{:S(2)}) collective-permute-start(bf16[3,256,512]{2,1,0:T(8,128)(2,1)} %get-tuple-element.26.mine_ref), channel_id=1, source_target_pairs={{0,1},{1,0},{2,3},{3,2},{4,5},{5,4},{6,7},{7,6},{8,9},{9,8},{10,11... | collective-permute-start | bytes 2359304 | tf_op jit(solution)/shard_map/ppermute | solution.py:27
  47.7 0.0 collective-permute-start.10
  47.7 12.3 %collective-permute-done.8.far_ref = bf16[3,256,512]{2,1,0:T(8,128)(2,1)} collective-permute-done((bf16[3,256,512]{2,1,0:T(8,128)(2,1)}, bf16[3,256,512]{2,1,0:T(8,128)(2,1)}, u32[]{:S(2)}, u32[]{:S(2)}) %collective-permute-start.8) | collective-permute-done | bytes 786464 | tf_op jit(solution)/shard_map/ppermute | solution.py:27
  60.0 0.8 collective-permute-start.9
  60.8 8.8 %collective-permute-done.4.refs_1_.refs_2_ = bf16[2,256,1024]{2,1,0:T(8,128)(2,1)} collective-permute-done((bf16[2,256,1024]{2,1,0:T(8,128)(2,1)}, bf16[2,256,1024]{2,1,0:T(8,128)(2,1)}, u32[]{:S(2)}, u32[]{:S(2)}) %collective-permute-start.4) | collective-permute-done | bytes 1048608 | tf_op jit(solution)/shard_map/ppermute | solution.py:41
  69.6 6.2 %attend_early.2.refs_7_ = bf16[512,2048]{1,0:T(8,128)(2,1)} custom-call(bf16[512,2048]{1,0:T(8,128)(2,1)} %query_ref.1, bf16[2,256,1024]{2,1,0:T(8,128)(2,1)} %collective-permute-done.4.refs_1_.refs_2_, bf16[2,256,1024]{2,1,0:T(8,128)(2,1)} %collective-permute-done.4.refs_1_.refs_2_, bf16[512,2048]{1,0:T(8,128)(2,1)} %refs_4_.5, ...), custom_call_target="tpu_custom_call", output_to_operand_aliasing={{}: (7, {})} | custom-call | flops 1342177280 | bytes 3670016 | tf_op jit(solution)/shard_map/attend_early/pallas_call | solution.py:314
  75.8 5.1 %collective-permute-done.3.refs_1_.refs_2_ = bf16[2,256,1024]{2,1,0:T(8,128)(2,1)} collective-permute-done((bf16[2,256,1024]{2,1,0:T(8,128)(2,1)}, bf16[2,256,1024]{2,1,0:T(8,128)(2,1)}, u32[]{:S(2)}, u32[]{:S(2)}) %collective-permute-start.3) | collective-permute-done | bytes 1048608 | tf_op jit(solution)/shard_map/ppermute | solution.py:41
  80.8 6.2 %attend_early.3 = bf16[512,2048]{1,0:T(8,128)(2,1)} custom-call(bf16[512,2048]{1,0:T(8,128)(2,1)} %query_ref.1, bf16[2,256,1024]{2,1,0:T(8,128)(2,1)} %collective-permute-done.3.refs_1_.refs_2_, bf16[2,256,1024]{2,1,0:T(8,128)(2,1)} %collective-permute-done.3.refs_1_.refs_2_, bf16[512,2048]{1,0:T(8,128)(2,1)} %refs_4_.5, ...), custom_call_target="tpu_custom_call", output_to_operand_aliasing={{}: (7, {})} | custom-call | flops 1342177280 | bytes 3670016 | tf_op jit(solution)/shard_map/attend_early/pallas_call | solution.py:314
  87.0 0.0 collective-permute-done.10.pair_pack_ref
  87.0 0.0 collective-permute-done.7.other_ref
  87.0 0.0 collective-permute-done.9.other_far_ref
  87.0 15.9 %fast_recall.1 = bf16[512,2048]{1,0:T(8,128)(2,1)} custom-call(bf16[3,256,512]{2,1,0:T(8,128)(2,1)} %get-tuple-element.26.mine_ref, bf16[3,256,512]{2,1,0:T(8,128)(2,1)} %collective-permute-done.7.other_ref, bf16[3,256,512]{2,1,0:T(8,128)(2,1)} %collective-permute-done.8.far_ref, bf16[3,256,512]{2,1,0:T(8,128)(2,1)} %collective-permute-done.9.other_far_ref, ...), custom_call_target="tpu_custom_call" | custom-call | flops 8053063680 | bytes 7340032 | tf_op jit(solution)/shard_map/fast_recall/pallas_call | solution.py:613
Async XLA Ops:
  0.6 19.7 %collective-permute-start.5 = (bf16[512,2048]{1,0:T(8,128)(2,1)}, bf16[512,2048]{1,0:T(8,128)(2,1)}, u32[]{:S(2)}, u32[]{:S(2)}) collective-permute-start(bf16[512,2048]{1,0:T(8,128)(2,1)} %refs_4_.5), channel_id=1, source_target_pairs={{0,1},{1,0},{2,3},{3,2},{4,5},{5,4},{6,7},{7,6},{8,9},{9,8},{10,11... | collective-permute-start | bytes 6291464 | tf_op jit(solution)/shard_map/ppermute | solution.py:27
  0.7 19.6 %collective-permute-start.6 = (bf16[512,2048]{1,0:T(8,128)(2,1)}, bf16[512,2048]{1,0:T(8,128)(2,1)}, u32[]{:S(2)}, u32[]{:S(2)}) collective-permute-start(bf16[512,2048]{1,0:T(8,128)(2,1)} %refs_5_.5), channel_id=1, source_target_pairs={{0,1},{1,0},{2,3},{3,2},{4,5},{5,4},{6,7},{7,6},{8,9},{9,8},{10,11... | collective-permute-start | bytes 6291464 | tf_op jit(solution)/shard_map/ppermute | solution.py:27
  3.7 16.6 %collective-permute-start.1 = (bf16[3,256,512]{2,1,0:T(8,128)(2,1)}, bf16[3,256,512]{2,1,0:T(8,128)(2,1)}, u32[]{:S(2)}, u32[]{:S(2)}) collective-permute-start(bf16[3,256,512]{2,1,0:T(8,128)(2,1)} %get-tuple-element.22.refs_0_), channel_id=1, source_target_pairs={{0,2},{4,6},{9,11},{13,15},{18,16},{22,20},{27,25},{31,29}} | collective-permute-start | bytes 2359304 | tf_op jit(solution)/shard_map/ppermute | solution.py:671
  5.3 15.0 %collective-permute-start.2 = (bf16[3,256,512]{2,1,0:T(8,128)(2,1)}, bf16[3,256,512]{2,1,0:T(8,128)(2,1)}, u32[]{:S(2)}, u32[]{:S(2)}) collective-permute-start(bf16[3,256,512]{2,1,0:T(8,128)(2,1)} %get-tuple-element.16), channel_id=1, source_target_pairs={{0,3},{4,7},{9,10},{13,14},{18,17},{22,21},{27,24},{31,28}} | collective-permute-start | bytes 2359304 | tf_op jit(solution)/shard_map/ppermute | solution.py:671
  6.9 13.5 %collective-permute-start = (bf16[3,256,512]{2,1,0:T(8,128)(2,1)}, bf16[3,256,512]{2,1,0:T(8,128)(2,1)}, u32[]{:S(2)}, u32[]{:S(2)}) collective-permute-start(bf16[3,256,512]{2,1,0:T(8,128)(2,1)} %get-tuple-element.16), channel_id=1, source_target_pairs={{0,1},{4,5},{9,8},{13,12},{18,19},{22,23},{27,26},{31,30}} | collective-permute-start | bytes 2359304 | tf_op jit(solution)/shard_map/ppermute | solution.py:671
  33.9 26.1 %collective-permute-start.8 = (bf16[3,256,512]{2,1,0:T(8,128)(2,1)}, bf16[3,256,512]{2,1,0:T(8,128)(2,1)}, u32[]{:S(2)}, u32[]{:S(2)}) collective-permute-start(bf16[3,256,512]{2,1,0:T(8,128)(2,1)} %get-tuple-element.26.mine_ref), channel_id=1, source_target_pairs={{0,2},{1,3},{2,0},{3,1},{4,6},{5,7},{6,4},{7,5},{8,10},{9,11},{10,... | collective-permute-start | bytes 2359304 | tf_op jit(solution)/shard_map/ppermute | solution.py:27
  42.0 27.6 %collective-permute-start.4 = (bf16[2,256,1024]{2,1,0:T(8,128)(2,1)}, bf16[2,256,1024]{2,1,0:T(8,128)(2,1)}, u32[]{:S(2)}, u32[]{:S(2)}) collective-permute-start(bf16[2,256,1024]{2,1,0:T(8,128)(2,1)} %get-tuple-element.20), channel_id=1, source_target_pairs={{0,1},{1,2},{2,3},{4,5},{5,6},{6,7},{8,9},{9,10},{10,11},{12,13},{... | collective-permute-start | bytes 3145736 | tf_op jit(solution)/shard_map/ppermute | solution.py:41
  44.0 36.8 %collective-permute-start.3 = (bf16[2,256,1024]{2,1,0:T(8,128)(2,1)}, bf16[2,256,1024]{2,1,0:T(8,128)(2,1)}, u32[]{:S(2)}, u32[]{:S(2)}) collective-permute-start(bf16[2,256,1024]{2,1,0:T(8,128)(2,1)} %get-tuple-element.19), channel_id=1, source_target_pairs={{0,1},{1,2},{2,3},{4,5},{5,6},{6,7},{8,9},{9,10},{10,11},{12,13},{... | collective-permute-start | bytes 3145736 | tf_op jit(solution)/shard_map/ppermute | solution.py:41
  46.4 40.6 %collective-permute-start.7 = (bf16[3,256,512]{2,1,0:T(8,128)(2,1)}, bf16[3,256,512]{2,1,0:T(8,128)(2,1)}, u32[]{:S(2)}, u32[]{:S(2)}) collective-permute-start(bf16[3,256,512]{2,1,0:T(8,128)(2,1)} %get-tuple-element.26.mine_ref), channel_id=1, source_target_pairs={{0,1},{1,0},{2,3},{3,2},{4,5},{5,4},{6,7},{7,6},{8,9},{9,8},{10,11... | collective-permute-start | bytes 2359304 | tf_op jit(solution)/shard_map/ppermute | solution.py:27
  47.7 39.4 %collective-permute-start.10 = (bf16[3,256,512]{2,1,0:T(8,128)(2,1)}, bf16[3,256,512]{2,1,0:T(8,128)(2,1)}, u32[]{:S(2)}, u32[]{:S(2)}) collective-permute-start(bf16[3,256,512]{2,1,0:T(8,128)(2,1)} %get-tuple-element.27.pack_ref), channel_id=1, source_target_pairs={{0,1},{1,0},{2,3},{3,2},{4,5},{5,4},{6,7},{7,6},{8,9},{9,8},{10,11... | collective-permute-start | bytes 2359304 | tf_op jit(solution)/shard_map/ppermute | solution.py:27
  60.0 27.0 %collective-permute-start.9 = (bf16[3,256,512]{2,1,0:T(8,128)(2,1)}, bf16[3,256,512]{2,1,0:T(8,128)(2,1)}, u32[]{:S(2)}, u32[]{:S(2)}) collective-permute-start(bf16[3,256,512]{2,1,0:T(8,128)(2,1)} %collective-permute-done.8.far_ref), channel_id=1, source_target_pairs={{0,1},{1,0},{2,3},{3,2},{4,5},{5,4},{6,7},{7,6},{8,9},{9,8},{10,11... | collective-permute-start | bytes 2359304 | tf_op jit(solution)/shard_map/ppermute | solution.py:27

commit v5 on v4

--- a/solution.py
+++ b/solution.py
@@ -297,6 +297,7 @@
             transcendentals=heads * chunks * WINDOW**2,
         ),
         name="attend_late",
+        compiler_params=pltpu.CompilerParams(vmem_limit_bytes=VMEM_GRANT),
     )(queries, keys, values, keys, values)
 
 
@@ -383,72 +384,98 @@
             flops=0, bytes_accessed=12 * hidden_rows * features, transcendentals=0
         ),
         name="prepare",
+        compiler_params=pltpu.CompilerParams(vmem_limit_bytes=VMEM_GRANT),
     )(gate_fast, lift_fast, down_fast)
 
 
-def edges_body(key_ref, value_ref, *refs):
-    out_refs, (held_ref, sem) = refs[:-2], refs[-2:]
-    _, tokens = key_ref.shape
-    rows, window = out_refs[0].shape[1:]
-    moves = []
-    for part, out_ref in enumerate(out_refs):
-        at = slice(part * rows, (part + 1) * rows)
-        for place, source in enumerate((key_ref, value_ref)):
-            arriving = pltpu.make_async_copy(
-                source.at[at, tokens - window :], held_ref.at[place, at], sem.at[0, place, part]
-            )
-            leaving = pltpu.make_async_copy(
-                held_ref.at[place, at], out_ref.at[place], sem.at[1, place, part]
-            )
-            arriving.start()
-            moves.append((arriving, leaving))
-    for arriving, leaving in moves:
-        arriving.wait()
-        leaving.start()
-    for _, leaving in moves:
-        leaving.wait()
-
-
-def edges(keys, values, parts):
-    features = keys.shape[0]
+def stage_body(key_ref, value_ref, rate_ref, target_ref, *refs):
+    end_refs, (held_ref, values_ref, made_ref, sem, sem_end) = refs[:-5], refs[-5:]
+    features, tokens = key_ref.shape
+    rows, window = end_refs[0].shape[1:]
+    step = HEAD_SIZE
+    last = slice(tokens - window, tokens)
+    begin = pl.multiple_of(lax.axis_index("narrow") * tokens, tokens)
+    rates = -rate_ref[pl.ds(lax.axis_index("wide"), 1), pl.ds(begin, tokens)]
+    values = [
+        pltpu.make_async_copy(
+            value_ref.at[at : at + step], values_ref.at[at : at + step], sem.at[0, at // step]
+        )
+        for at in range(0, features, step)
+    ]
+    keys = [
+        pltpu.make_async_copy(
+            key_ref.at[part * rows : (part + 1) * rows, last], held_ref.at[part], sem_end.at[0, part]
+        )
+        for part in range(len(end_refs))
+    ]
+    for copy in values + keys:
+        copy.start()
+    leaving = []
+
+    def leave(source, target, mark):
+        leaving.append(pltpu.make_async_copy(source, target, mark))
+        leaving[-1].start()
+
+    for place, copy in enumerate(values):
+        at = slice(place * step, (place + 1) * step)
+        copy.wait()
+        made_ref[at] = (values_ref[at].astype(jnp.float32) * rates).astype(jnp.bfloat16)
+        leave(made_ref.at[at], target_ref.at[at], sem.at[1, place])
+    for part, end_ref in enumerate(end_refs):
+        leave(
+            values_ref.at[part * rows : (part + 1) * rows, last], end_ref.at[1], sem_end.at[1, part]
+        )
+        keys[part].wait()
+        leave(held_ref.at[part], end_ref.at[0], sem_end.at[2, part])
+    for copy in leaving:
+        copy.wait()
+
+
+def stage(keys, values, rates, parts):
+    features, tokens = keys.shape
+    rows = features // parts
     return pl.pallas_call(
-        edges_body,
-        out_shape=(jax.ShapeDtypeStruct((2, features // parts, WINDOW), jnp.bfloat16),) * parts,
-        in_specs=anywhere(2),
-        out_specs=tuple(anywhere(parts)),
+        stage_body,
+        out_shape=(jax.ShapeDtypeStruct((features, tokens), jnp.bfloat16),)
+        + (jax.ShapeDtypeStruct((2, rows, WINDOW), jnp.bfloat16),) * parts,
+        in_specs=anywhere(2) + [pl.BlockSpec(memory_space=pltpu.VMEM)],
+        out_specs=tuple(anywhere(1 + parts)),
         scratch_shapes=[
-            pltpu.VMEM((2, features, WINDOW), jnp.bfloat16),
-            pltpu.SemaphoreType.DMA((2, 2, parts)),
+            pltpu.VMEM((parts, rows, WINDOW), jnp.bfloat16),
+            pltpu.VMEM((features, tokens), jnp.bfloat16),
+            pltpu.VMEM((features, tokens), jnp.bfloat16),
+            pltpu.SemaphoreType.DMA((2, features // HEAD_SIZE)),
+            pltpu.SemaphoreType.DMA((3, parts)),
         ],
         cost_estimate=pl.CostEstimate(
-            flops=0, bytes_accessed=8 * features * WINDOW, transcendentals=0
+            flops=features * tokens,
+            bytes_accessed=4 * features * tokens + 8 * features * WINDOW,
+            transcendentals=0,
         ),
-        name="edges",
-    )(keys, values)
-
-
-def sums_body(*refs, owned):
-    sources = refs[:-14]
+        name="stage",
+        compiler_params=pltpu.CompilerParams(vmem_limit_bytes=VMEM_GRANT),
+    )(keys, values, rates)
+
+
+def sums_body(*refs, owned, block):
+    sources = refs[:-12]
     (
-        key_ref, value_ref, pair_key_ref, pair_value_ref, rate_ref,
+        key_ref, target_ref, pair_key_ref, pair_target_ref,
         send_ref, pack_ref,
-        keys_ref, values_ref, hidden_ref, target_ref, back_ref, sem, sem_in,
-    ) = refs[-14:]
+        keys_ref, targets_ref, hidden_ref, back_ref, sem, sem_in,
+    ) = refs[-12:]
     _, tokens = key_ref.shape
     half = pack_ref.shape[1]
-    block = min(1024, tokens)
     count = tokens // block
-    wide_at = lax.axis_index("wide")
-    narrow_at = lax.axis_index("narrow")
-    role = narrow_at ^ (wide_at // owned)
-
-    def moved(keys, values, index, slot):
+    role = lax.axis_index("narrow") ^ (lax.axis_index("wide") // owned)
+
+    def moved(keys, targets, index, slot):
         source = slice(index * block, (index + 1) * block)
-        target = slice(slot * block, (slot + 1) * block)
+        place = slice(slot * block, (slot + 1) * block)
         return (
-            pltpu.make_async_copy(keys.at[:, source], keys_ref.at[:, target], sem_in.at[0, slot]),
+            pltpu.make_async_copy(keys.at[:, source], keys_ref.at[:, place], sem_in.at[0, slot]),
             pltpu.make_async_copy(
-                values.at[:, source], values_ref.at[:, target], sem_in.at[1, slot]
+                targets.at[:, source], targets_ref.at[:, place], sem_in.at[1, slot]
             ),
         )
 
@@ -458,24 +485,25 @@
         def _(source=source):
             pltpu.make_async_copy(source, pack_ref, sem).start()
 
-    arrivals = [moved(key_ref, value_ref, index, index) for index in range(count)]
-    arrivals += [moved(pair_key_ref, pair_value_ref, index, count + index) for index in range(count)]
+    arrivals = [moved(key_ref, target_ref, index, index) for index in range(count)]
+    arrivals += [moved(pair_key_ref, pair_target_ref, index, count + index) for index in range(count)]
     for copies in arrivals:
         for copy in copies:
             copy.start()
     pltpu.make_async_copy(sources[0], pack_ref, sem).wait()
     gate_lift = jnp.concatenate([pack_ref[0] * jnp.bfloat16(0.5), pack_ref[1]], axis=0)
     down = pack_ref[2]
-    for slot, copies in enumerate(arrivals):
-        for copy in copies:
+
+    def multiply(slot):
+        for copy in arrivals[slot]:
             copy.wait()
         at = slice(slot * block, (slot + 1) * block)
-        begin = (narrow_at ^ (slot // count)) * tokens + (slot % count) * block
-        rates = rate_ref[pl.ds(wide_at, 1), pl.ds(pl.multiple_of(begin, block), block)]
         pre = jnp.dot(gate_lift, keys_ref[:, at], preferred_element_type=jnp.float32)
-        target = (values_ref[:, at].astype(jnp.float32) * -rates).astype(jnp.bfloat16)
-        target_ref[:, at] = target
-        back_hidden = jnp.dot(down, target, preferred_element_type=jnp.float32)
+        back_hidden = jnp.dot(down, targets_ref[:, at], preferred_element_type=jnp.float32)
+        return pre, back_hidden
+
+    def combine(slot, pre, back_hidden):
+        at = slice(slot * block, (slot + 1) * block)
         half_gate = pre[:half]
         pre_lift = pre[half:]
         twice = jnp.tanh(half_gate) + 1.0
@@ -484,33 +512,35 @@
         slope = twice + silu_gate * (2.0 - twice)
         back_ref[:half, at] = (back_hidden * pre_lift * slope).astype(jnp.bfloat16)
         back_ref[half:, at] = (back_hidden * silu_gate).astype(jnp.bfloat16)
+
+    for slot in range(2 * count):
+        combine(slot, *multiply(slot))
     contract = (((1,), (1,)), ((), ()))
     sums = lax.dot_general(
         back_ref[...], keys_ref[...], contract, preferred_element_type=jnp.float32
     )
     down_sums = lax.dot_general(
-        hidden_ref[...], target_ref[...], contract, preferred_element_type=jnp.float32
+        hidden_ref[...], targets_ref[...], contract, preferred_element_type=jnp.float32
     )
     for place, value in enumerate((sums[:half] * 0.5, sums[half:], down_sums)):
         send_ref[place] = value.astype(jnp.bfloat16)
 
 
-def fast_sums(sources, keys, values, pair_keys, pair_values, rates, owned):
+def fast_sums(sources, keys, targets, pair_keys, pair_targets, owned):
     features, tokens = keys.shape
     shape = sources[0].shape
     half = shape[1]
-    block = min(1024, tokens)
+    block = tokens
     resident = pl.BlockSpec(memory_space=pltpu.VMEM)
     return pl.pallas_call(
-        functools.partial(sums_body, owned=owned),
+        functools.partial(sums_body, owned=owned, block=block),
         out_shape=(jax.ShapeDtypeStruct(shape, jnp.bfloat16),) * 2,
-        in_specs=anywhere(len(sources) + 4) + [resident],
+        in_specs=anywhere(len(sources) + 4),
         out_specs=(resident,) * 2,
         scratch_shapes=[
             pltpu.VMEM((features, 2 * tokens), jnp.bfloat16),
             pltpu.VMEM((features, 2 * tokens), jnp.bfloat16),
             pltpu.VMEM((half, 2 * tokens), jnp.bfloat16),
-            pltpu.VMEM((features, 2 * tokens), jnp.bfloat16),
             pltpu.VMEM((2 * half, 2 * tokens), jnp.bfloat16),
             pltpu.SemaphoreType.DMA(()),
             pltpu.SemaphoreType.DMA((2, 2 * tokens // block)),
@@ -522,62 +552,84 @@
         ),
         name="fast_sums",
         compiler_params=pltpu.CompilerParams(vmem_limit_bytes=VMEM_GRANT),
-    )(*sources, keys, values, pair_keys, pair_values, rates)
+    )(*sources, keys, targets, pair_keys, pair_targets)
 
 
 def recall_body(
     mine_ref, other_ref, far_ref, other_far_ref, pack_ref, pair_pack_ref, query_ref, out_ref,
-    w_ref, fresh_ref, far_sums_ref, turned_ref, sem,
+    w_ref, near_sums_ref, far_sums_ref, fresh_ref, turned_ref, sem,
 ):
     half = mine_ref.shape[1]
+    hidden_rows, features = fresh_ref.shape[1:]
     nt = (((1,), (1,)), ((), ()))
 
     @pl.when(pl.program_id(0) == 0)
     def _():
         side = lax.axis_index("narrow") % 2
-        copies = [
-            pltpu.make_async_copy(
-                source, target.at[:, half_rows(part, half)], sem.at[place]
+
+        def arriving(matrix):
+            moves = (
+                (mine_ref, near_sums_ref, side),
+                (other_ref, near_sums_ref, 1 - side),
+                (far_ref, far_sums_ref, side),
+                (other_far_ref, far_sums_ref, 1 - side),
             )
-            for place, (source, target, part) in enumerate(
-                (
-                    (mine_ref, fresh_ref, side),
-                    (other_ref, fresh_ref, 1 - side),
-                    (far_ref, far_sums_ref, side),
-                    (other_far_ref, far_sums_ref, 1 - side),
-                    (pack_ref, w_ref, side),
-                    (pair_pack_ref, w_ref, 1 - side),
+            return [
+                pltpu.make_async_copy(
+                    source.at[matrix],
+                    target.at[matrix, half_rows(part, half)],
+                    sem.at[place, matrix],
                 )
+                for place, (source, target, part) in enumerate(moves)
+            ]
+
+        sums = [arriving(matrix) for matrix in range(3)]
+        weights = [
+            pltpu.make_async_copy(source, w_ref.at[:, half_rows(part, half)], sem.at[4, place])
+            for place, (source, part) in enumerate(((pack_ref, side), (pair_pack_ref, 1 - side)))
+        ]
+        for copies in sums + [weights]:
+            for copy in copies:
+                copy.start()
+        rows = lax.broadcasted_iota(jnp.int32, (hidden_rows, features), 0)
+        cols = lax.broadcasted_iota(jnp.int32, (hidden_rows, features), 1)
+        diagonal = rows == cols
+        rounded, gram, scale = [], [], []
+        for matrix, copies in enumerate(sums):
+            for copy in copies:
+                copy.wait()
+            summed = near_sums_ref[matrix].astype(jnp.float32) + far_sums_ref[matrix].astype(
+                jnp.float32
             )
-        ]
-        for copy in copies:
-            copy.start()
-        for copy in copies[:4]:
-            copy.wait()
-        current = []
-        for i in range(3):
-            summed = fresh_ref[i].astype(jnp.float32) + far_sums_ref[i].astype(jnp.float32)
-            widened = summed.astype(jnp.bfloat16).astype(jnp.float32)
-            total = jnp.sum(jnp.sum(widened * widened, axis=0, keepdims=True), axis=1, keepdims=True)
-            current.append((widened * lax.rsqrt(total + EPS)).astype(jnp.bfloat16))
-        for _ in range(NS_ITERS):
-            gram = [
-                lax.dot_general(x, x, nt, preferred_element_type=jnp.float32).astype(jnp.bfloat16)
-                for x in current
-            ]
+            x = summed.astype(jnp.bfloat16)
+            product = lax.dot_general(x, x, nt, preferred_element_type=jnp.float32)
+            trace = jnp.sum(jnp.where(diagonal, product, 0.0), axis=0, keepdims=True)
+            scale.append(lax.rsqrt(jnp.sum(trace, axis=1, keepdims=True) + EPS))
+            rounded.append(x)
+            gram.append((product * (scale[-1] * scale[-1])).astype(jnp.bfloat16))
+        current = rounded
+        for sweep_index in range(NS_ITERS):
+            if sweep_index:
+                scale = [1.0] * 3
+                gram = [
+                    lax.dot_general(x, x, nt, preferred_element_type=jnp.float32).astype(
+                        jnp.bfloat16
+                    )
+                    for x in current
+                ]
             lifted = [
                 jnp.dot(g, x, preferred_element_type=jnp.float32).astype(jnp.bfloat16)
                 for x, g in zip(current, gram)
             ]
             current = [
                 (
-                    COEF_A * x.astype(jnp.float32)
-                    + COEF_B * y.astype(jnp.float32)
-                    + COEF_C * jnp.dot(g, y, preferred_element_type=jnp.float32)
+                    (COEF_A * r) * x.astype(jnp.float32)
+                    + (COEF_B * r) * y.astype(jnp.float32)
+                    + (COEF_C * r) * jnp.dot(g, y, preferred_element_type=jnp.float32)
                 ).astype(jnp.bfloat16)
-                for x, y, g in zip(current, lifted, gram)
+                for x, y, g, r in zip(current, lifted, gram, scale)
             ]
-        for copy in copies[4:]:
+        for copy in weights:
             copy.wait()
         for i in range(3):
             axis = 0 if i == 2 else 1
@@ -591,9 +643,8 @@
             else:
                 fresh_ref[i] = fresh
 
-    hidden_rows, features = fresh_ref.shape[1:]
     pre = jnp.dot(
-        fresh_ref[0:2].reshape(2 * hidden_rows, features),
+        fresh_ref[...].reshape(2 * hidden_rows, features),
         query_ref[...],
         preferred_element_type=jnp.float32,
     )
@@ -608,7 +659,7 @@
     features, tokens = queries.shape
     half = packs[0].shape[1]
     hidden_rows = 2 * half
-    block = min(512, tokens)
+    block = min(1024, tokens)
     piece = pl.BlockSpec((features, block), lambda i: (0, i))
     return pl.pallas_call(
         recall_body,
@@ -620,8 +671,9 @@
             pltpu.VMEM((3, hidden_rows, features), jnp.bfloat16),
             pltpu.VMEM((3, hidden_rows, features), jnp.bfloat16),
             pltpu.VMEM((3, hidden_rows, features), jnp.bfloat16),
+            pltpu.VMEM((2, hidden_rows, features), jnp.bfloat16),
             pltpu.VMEM((features, hidden_rows), jnp.bfloat16),
-            pltpu.SemaphoreType.DMA((6,)),
+            pltpu.SemaphoreType.DMA((5, 3)),
         ],
         cost_estimate=pl.CostEstimate(
             flops=6 * hidden_rows * features * tokens + 18 * NS_ITERS * hidden_rows * features**2,
@@ -672,21 +724,19 @@
 
     own, other = prepare(gate_fast, lift_fast, down_fast)
     arrivals = {}
-    for step in reversed(range(1, narrow_count)):
+    for step in sorted(range(1, narrow_count), key=lambda step: step < 2):
         arrivals[step] = from_owner((own, other)[step % 2], step)
     pair_keys = swapped(key_states, "narrow", 0)
-    pair_values = swapped(value_states, "narrow", 0)
     parts = 2
-    ends = edges(key_states, value_states, parts)
+    targets, *ends = stage(key_states, value_states, token_rates, parts)
+    pair_targets = swapped(targets, "narrow", 0)
     attended = attend_late(query_states, key_states, value_states)
     sources = [own] + [arrivals[step] for step in range(1, narrow_count)]
     sources, attended, ends = lax.optimization_barrier((sources, attended, ends))
     prior = []
     for end in ends:
         prior.append(from_behind(end, "narrow", 1))
-    near, pack = fast_sums(
-        sources, key_states, value_states, pair_keys, pair_values, token_rates, owned
-    )
+    near, pack = fast_sums(sources, key_states, targets, pair_keys, pair_targets, owned)
     distances = range(1, narrow_count.bit_length() - 1)
     for distance in distances:
         far = swapped(near, "narrow", distance)

time: 104 us -> 107 us (1.029)
  the two profiles are of different devices: /device:TPU:1 before, /device:TPU:20 now
where the time goes in v5:
time: 107 us
  Pallas kernels  56 us (52%)
  waiting for transfers between devices  35.7 us (33%)
  starting transfers between devices  14.4 us (13%)
    ppermute x2, waiting for transfers between devices, from_behind(): lax.ppermute(value, axis, [(source, source + steps) for source in range(i...  15.9 us
    pallas_call x1, Pallas kernels, fast_recall(): pl.pallas_call(recall_body, out_shape=jax.ShapeDtypeStruct((features, tok...  14.8 us
    ppermute x6, waiting for transfers between devices, swapped(): lax.ppermute(array, axis, [(i, i ^ 1 << distance) for i in range(lax.axis...  14.3 us
    pallas_call x1, Pallas kernels, fast_sums(): pl.pallas_call(functools.partial(sums_body, owned=owned, block=block), ou...  12.4 us
    pallas_call x2, Pallas kernels, attend_early(): pl.pallas_call(early_body, out_shape=jax.ShapeDtypeStruct((features, toke...  12.4 us
    pallas_call x1, Pallas kernels, attend_late(): pl.pallas_call(functools.partial(attend_body, block=min(256, WINDOW), win...  9.69 us
    ppermute x3, starting transfers between devices, from_owner(): return lax.ppermute(value, ('wide', 'narrow'), pairs)  7.28 us
    ppermute x2, starting transfers between devices, from_behind(): lax.ppermute(value, axis, [(source, source + steps) for source in range(i...  5.83 us
  transfers between devices with their start and end apart: 11, of which 4 were waited for; matrix products, arithmetic and copies ran while one was open for 0% of the time, Pallas kernels for 27%

profile of v5, /device:TPU:20, one launch (start us, length us, event | category | flops | bytes accessed | tf_op | source)
XLA Modules:
  0.0 106.9 jit_solution(12077170759749235641)
XLA Ops:
  0.6 0.1 collective-permute-start.5
  0.7 4.2 %stage.1 = (bf16[512,2048]{1,0:T(8,128)(2,1)}, bf16[2,256,1024]{2,1,0:T(8,128)(2,1)}, bf16[2,256,1024]{2,1,0:T(8,128)(2,1)}) custom-call(bf16[512,2048]{1,0:T(8,128)(2,1)} %refs_4_.5, bf16[512,2048]{1,0:T(8,128)(2,1)} %refs_4_.4, f32[8,8192]{1,0:T(8,128)} %rate_ref.1), custom_call_target="tpu_custom_call" | custom-call | flops 1048576 | bytes 8388608 | tf_op jit(solution)/shard_map/stage/pallas_call | solution.py:437
  4.9 0.6 collective-permute-start.6
  5.5 2.5 %prepare.1 = (bf16[3,256,512]{2,1,0:T(8,128)(2,1)}, bf16[3,256,512]{2,1,0:T(8,128)(2,1)}) custom-call(bf16[2,512,512]{2,1,0:T(8,128)(2,1)} %gate_ref.1, bf16[2,512,512]{2,1,0:T(8,128)(2,1)} %lift_ref.1, bf16[2,512,512]{2,1,0:T(8,128)(2,1)} %down_ref.1), custom_call_target="tpu_custom_call" | custom-call | bytes 3145728 | tf_op jit(solution)/shard_map/prepare/pallas_call | solution.py:373
  8.0 2.9 %collective-permute-start = (bf16[3,256,512]{2,1,0:T(8,128)(2,1)}, bf16[3,256,512]{2,1,0:T(8,128)(2,1)}, u32[]{:S(2)}, u32[]{:S(2)}) collective-permute-start(bf16[3,256,512]{2,1,0:T(8,128)(2,1)} %get-tuple-element.17), channel_id=1, source_target_pairs={{0,1},{4,5},{9,8},{13,12},{18,19},{22,23},{27,26},{31,30}} | collective-permute-start | bytes 2359304 | tf_op jit(solution)/shard_map/ppermute | solution.py:723
  10.9 2.2 %collective-permute-start.1 = (bf16[3,256,512]{2,1,0:T(8,128)(2,1)}, bf16[3,256,512]{2,1,0:T(8,128)(2,1)}, u32[]{:S(2)}, u32[]{:S(2)}) collective-permute-start(bf16[3,256,512]{2,1,0:T(8,128)(2,1)} %get-tuple-element.23.refs_0_), channel_id=1, source_target_pairs={{0,2},{4,6},{9,11},{13,15},{18,16},{22,20},{27,25},{31,29}} | collective-permute-start | bytes 2359304 | tf_op jit(solution)/shard_map/ppermute | solution.py:723
  13.1 2.2 %collective-permute-start.2 = (bf16[3,256,512]{2,1,0:T(8,128)(2,1)}, bf16[3,256,512]{2,1,0:T(8,128)(2,1)}, u32[]{:S(2)}, u32[]{:S(2)}) collective-permute-start(bf16[3,256,512]{2,1,0:T(8,128)(2,1)} %get-tuple-element.17), channel_id=1, source_target_pairs={{0,3},{4,7},{9,10},{13,14},{18,17},{22,21},{27,24},{31,28}} | collective-permute-start | bytes 2359304 | tf_op jit(solution)/shard_map/ppermute | solution.py:723
  15.2 9.7 %attend_late.1.refs_7_ = bf16[512,2048]{1,0:T(8,128)(2,1)} custom-call(bf16[512,2048]{1,0:T(8,128)(2,1)} %query_ref.1, bf16[512,2048]{1,0:T(8,128)(2,1)} %refs_4_.5, bf16[512,2048]{1,0:T(8,128)(2,1)} %refs_4_.4, bf16[512,2048]{1,0:T(8,128)(2,1)} %refs_4_.5, bf16[512,2048]{1,0:T(8,128)(2,1)} %refs_4_.4), custom_call_target="tpu_custom_call" | custom-call | flops 2684354560 | bytes 5242880 | tf_op jit(solution)/shard_map/attend_late/pallas_call | solution.py:287
  24.9 0.0 collective-permute-done.refs_1_
  24.9 0.0 collective-permute-done.1.refs_2_
  24.9 5.5 %collective-permute-done.2.refs_3_ = bf16[3,256,512]{2,1,0:T(8,128)(2,1)} collective-permute-done((bf16[3,256,512]{2,1,0:T(8,128)(2,1)}, bf16[3,256,512]{2,1,0:T(8,128)(2,1)}, u32[]{:S(2)}, u32[]{:S(2)}) %collective-permute-start.2) | collective-permute-done | bytes 786464 | tf_op jit(solution)/shard_map/ppermute | solution.py:723
  30.4 0.0 collective-permute-done.5.refs_6_
  30.4 0.0 collective-permute-done.6.refs_7_
  30.4 12.4 %fast_sums.1 = (bf16[3,256,512]{2,1,0:T(8,128)(2,1)}, bf16[3,256,512]{2,1,0:T(8,128)(2,1)}) custom-call(bf16[3,256,512]{2,1,0:T(8,128)(2,1)} %get-tuple-element.23.refs_0_, bf16[3,256,512]{2,1,0:T(8,128)(2,1)} %collective-permute-done.refs_1_, bf16[3,256,512]{2,1,0:T(8,128)(2,1)} %collective-permute-done.1.refs_2_, ...), custom_call_target="tpu_custom_call" | custom-call | flops 6442450944 | bytes 10747904 | tf_op jit(solution)/shard_map/fast_sums/pallas_call | solution.py:535
  42.8 0.1 collective-permute-start.8
  42.9 3.9 %collective-permute-start.4 = (bf16[2,256,1024]{2,1,0:T(8,128)(2,1)}, bf16[2,256,1024]{2,1,0:T(8,128)(2,1)}, u32[]{:S(2)}, u32[]{:S(2)}) collective-permute-start(bf16[2,256,1024]{2,1,0:T(8,128)(2,1)} %get-tuple-element.21), channel_id=1, source_target_pairs={{0,1},{1,2},{2,3},{4,5},{5,6},{6,7},{8,9},{9,10},{10,11},{12,13},{... | collective-permute-start | bytes 3145736 | tf_op jit(solution)/shard_map/ppermute | solution.py:41
  46.8 1.9 %collective-permute-start.3 = (bf16[2,256,1024]{2,1,0:T(8,128)(2,1)}, bf16[2,256,1024]{2,1,0:T(8,128)(2,1)}, u32[]{:S(2)}, u32[]{:S(2)}) collective-permute-start(bf16[2,256,1024]{2,1,0:T(8,128)(2,1)} %get-tuple-element.20), channel_id=1, source_target_pairs={{0,1},{1,2},{2,3},{4,5},{5,6},{6,7},{8,9},{9,10},{10,11},{12,13},{... | collective-permute-start | bytes 3145736 | tf_op jit(solution)/shard_map/ppermute | solution.py:41
  48.7 0.1 collective-permute-start.7
  48.8 0.5 collective-permute-start.10
  49.3 14.3 %collective-permute-done.8.far_ref = bf16[3,256,512]{2,1,0:T(8,128)(2,1)} collective-permute-done((bf16[3,256,512]{2,1,0:T(8,128)(2,1)}, bf16[3,256,512]{2,1,0:T(8,128)(2,1)}, u32[]{:S(2)}, u32[]{:S(2)}) %collective-permute-start.8) | collective-permute-done | bytes 786464 | tf_op jit(solution)/shard_map/ppermute | solution.py:27
  63.6 0.0 collective-permute-start.9
  63.6 10.8 %collective-permute-done.4.refs_1_.refs_2_ = bf16[2,256,1024]{2,1,0:T(8,128)(2,1)} collective-permute-done((bf16[2,256,1024]{2,1,0:T(8,128)(2,1)}, bf16[2,256,1024]{2,1,0:T(8,128)(2,1)}, u32[]{:S(2)}, u32[]{:S(2)}) %collective-permute-start.4) | collective-permute-done | bytes 1048608 | tf_op jit(solution)/shard_map/ppermute | solution.py:41
  74.4 6.2 %attend_early.2.refs_7_ = bf16[512,2048]{1,0:T(8,128)(2,1)} custom-call(bf16[512,2048]{1,0:T(8,128)(2,1)} %query_ref.1, bf16[2,256,1024]{2,1,0:T(8,128)(2,1)} %collective-permute-done.4.refs_1_.refs_2_, bf16[2,256,1024]{2,1,0:T(8,128)(2,1)} %collective-permute-done.4.refs_1_.refs_2_, bf16[512,2048]{1,0:T(8,128)(2,1)} %refs_4_.5, ...), custom_call_target="tpu_custom_call", output_to_operand_aliasing={{}: (7, {})} | custom-call | flops 1342177280 | bytes 3670016 | tf_op jit(solution)/shard_map/attend_early/pallas_call | solution.py:315
  80.6 5.0 %collective-permute-done.3.refs_1_.refs_2_ = bf16[2,256,1024]{2,1,0:T(8,128)(2,1)} collective-permute-done((bf16[2,256,1024]{2,1,0:T(8,128)(2,1)}, bf16[2,256,1024]{2,1,0:T(8,128)(2,1)}, u32[]{:S(2)}, u32[]{:S(2)}) %collective-permute-start.3) | collective-permute-done | bytes 1048608 | tf_op jit(solution)/shard_map/ppermute | solution.py:41
  85.7 6.2 %attend_early.3 = bf16[512,2048]{1,0:T(8,128)(2,1)} custom-call(bf16[512,2048]{1,0:T(8,128)(2,1)} %query_ref.1, bf16[2,256,1024]{2,1,0:T(8,128)(2,1)} %collective-permute-done.3.refs_1_.refs_2_, bf16[2,256,1024]{2,1,0:T(8,128)(2,1)} %collective-permute-done.3.refs_1_.refs_2_, bf16[512,2048]{1,0:T(8,128)(2,1)} %refs_4_.5, ...), custom_call_target="tpu_custom_call", output_to_operand_aliasing={{}: (7, {})} | custom-call | flops 1342177280 | bytes 3670016 | tf_op jit(solution)/shard_map/attend_early/pallas_call | solution.py:315
  91.9 0.0 collective-permute-done.7.other_ref
  91.9 0.0 collective-permute-done.10.pair_pack_ref
  91.9 0.0 collective-permute-done.9.other_far_ref
  91.9 14.8 %fast_recall.1 = bf16[512,2048]{1,0:T(8,128)(2,1)} custom-call(bf16[3,256,512]{2,1,0:T(8,128)(2,1)} %get-tuple-element.28.mine_ref, bf16[3,256,512]{2,1,0:T(8,128)(2,1)} %collective-permute-done.7.other_ref, bf16[3,256,512]{2,1,0:T(8,128)(2,1)} %collective-permute-done.8.far_ref, bf16[3,256,512]{2,1,0:T(8,128)(2,1)} %collective-permute-done.9.other_far_ref, ...), custom_call_target="tpu_custom_call" | custom-call | flops 8053063680 | bytes 7340032 | tf_op jit(solution)/shard_map/fast_recall/pallas_call | solution.py:664
Async XLA Ops:
  0.6 29.8 %collective-permute-start.5 = (bf16[512,2048]{1,0:T(8,128)(2,1)}, bf16[512,2048]{1,0:T(8,128)(2,1)}, u32[]{:S(2)}, u32[]{:S(2)}) collective-permute-start(bf16[512,2048]{1,0:T(8,128)(2,1)} %refs_4_.5), channel_id=1, source_target_pairs={{0,1},{1,0},{2,3},{3,2},{4,5},{5,4},{6,7},{7,6},{8,9},{9,8},{10,11... | collective-permute-start | bytes 6291464 | tf_op jit(solution)/shard_map/ppermute | solution.py:27
  4.9 25.5 %collective-permute-start.6 = (bf16[512,2048]{1,0:T(8,128)(2,1)}, bf16[512,2048]{1,0:T(8,128)(2,1)}, u32[]{:S(2)}, u32[]{:S(2)}) collective-permute-start(bf16[512,2048]{1,0:T(8,128)(2,1)} %get-tuple-element.27.refs_5_), channel_id=1, source_target_pairs={{0,1},{1,0},{2,3},{3,2},{4,5},{5,4},{6,7},{7,6},{8,9},{9,8},{10,11... | collective-permute-start | bytes 6291464 | tf_op jit(solution)/shard_map/ppermute | solution.py:27
  8.0 17.0 %collective-permute-start = (bf16[3,256,512]{2,1,0:T(8,128)(2,1)}, bf16[3,256,512]{2,1,0:T(8,128)(2,1)}, u32[]{:S(2)}, u32[]{:S(2)}) collective-permute-start(bf16[3,256,512]{2,1,0:T(8,128)(2,1)} %get-tuple-element.17), channel_id=1, source_target_pairs={{0,1},{4,5},{9,8},{13,12},{18,19},{22,23},{27,26},{31,30}} | collective-permute-start | bytes 2359304 | tf_op jit(solution)/shard_map/ppermute | solution.py:723
  10.9 14.1 %collective-permute-start.1 = (bf16[3,256,512]{2,1,0:T(8,128)(2,1)}, bf16[3,256,512]{2,1,0:T(8,128)(2,1)}, u32[]{:S(2)}, u32[]{:S(2)}) collective-permute-start(bf16[3,256,512]{2,1,0:T(8,128)(2,1)} %get-tuple-element.23.refs_0_), channel_id=1, source_target_pairs={{0,2},{4,6},{9,11},{13,15},{18,16},{22,20},{27,25},{31,29}} | collective-permute-start | bytes 2359304 | tf_op jit(solution)/shard_map/ppermute | solution.py:723
  13.1 17.3 %collective-permute-start.2 = (bf16[3,256,512]{2,1,0:T(8,128)(2,1)}, bf16[3,256,512]{2,1,0:T(8,128)(2,1)}, u32[]{:S(2)}, u32[]{:S(2)}) collective-permute-start(bf16[3,256,512]{2,1,0:T(8,128)(2,1)} %get-tuple-element.17), channel_id=1, source_target_pairs={{0,3},{4,7},{9,10},{13,14},{18,17},{22,21},{27,24},{31,28}} | collective-permute-start | bytes 2359304 | tf_op jit(solution)/shard_map/ppermute | solution.py:723
  42.8 20.8 %collective-permute-start.8 = (bf16[3,256,512]{2,1,0:T(8,128)(2,1)}, bf16[3,256,512]{2,1,0:T(8,128)(2,1)}, u32[]{:S(2)}, u32[]{:S(2)}) collective-permute-start(bf16[3,256,512]{2,1,0:T(8,128)(2,1)} %get-tuple-element.28.mine_ref), channel_id=1, source_target_pairs={{0,2},{1,3},{2,0},{3,1},{4,6},{5,7},{6,4},{7,5},{8,10},{9,11},{10,... | collective-permute-start | bytes 2359304 | tf_op jit(solution)/shard_map/ppermute | solution.py:27
  42.9 31.5 %collective-permute-start.4 = (bf16[2,256,1024]{2,1,0:T(8,128)(2,1)}, bf16[2,256,1024]{2,1,0:T(8,128)(2,1)}, u32[]{:S(2)}, u32[]{:S(2)}) collective-permute-start(bf16[2,256,1024]{2,1,0:T(8,128)(2,1)} %get-tuple-element.21), channel_id=1, source_target_pairs={{0,1},{1,2},{2,3},{4,5},{5,6},{6,7},{8,9},{9,10},{10,11},{12,13},{... | collective-permute-start | bytes 3145736 | tf_op jit(solution)/shard_map/ppermute | solution.py:41
  46.8 38.9 %collective-permute-start.3 = (bf16[2,256,1024]{2,1,0:T(8,128)(2,1)}, bf16[2,256,1024]{2,1,0:T(8,128)(2,1)}, u32[]{:S(2)}, u32[]{:S(2)}) collective-permute-start(bf16[2,256,1024]{2,1,0:T(8,128)(2,1)} %get-tuple-element.20), channel_id=1, source_target_pairs={{0,1},{1,2},{2,3},{4,5},{5,6},{6,7},{8,9},{9,10},{10,11},{12,13},{... | collective-permute-start | bytes 3145736 | tf_op jit(solution)/shard_map/ppermute | solution.py:41
  48.7 43.1 %collective-permute-start.7 = (bf16[3,256,512]{2,1,0:T(8,128)(2,1)}, bf16[3,256,512]{2,1,0:T(8,128)(2,1)}, u32[]{:S(2)}, u32[]{:S(2)}) collective-permute-start(bf16[3,256,512]{2,1,0:T(8,128)(2,1)} %get-tuple-element.28.mine_ref), channel_id=1, source_target_pairs={{0,1},{1,0},{2,3},{3,2},{4,5},{5,4},{6,7},{7,6},{8,9},{9,8},{10,11... | collective-permute-start | bytes 2359304 | tf_op jit(solution)/shard_map/ppermute | solution.py:27
  48.8 43.1 %collective-permute-start.10 = (bf16[3,256,512]{2,1,0:T(8,128)(2,1)}, bf16[3,256,512]{2,1,0:T(8,128)(2,1)}, u32[]{:S(2)}, u32[]{:S(2)}) collective-permute-start(bf16[3,256,512]{2,1,0:T(8,128)(2,1)} %get-tuple-element.29.pack_ref), channel_id=1, source_target_pairs={{0,1},{1,0},{2,3},{3,2},{4,5},{5,4},{6,7},{7,6},{8,9},{9,8},{10,11... | collective-permute-start | bytes 2359304 | tf_op jit(solution)/shard_map/ppermute | solution.py:27
  63.6 28.3 %collective-permute-start.9 = (bf16[3,256,512]{2,1,0:T(8,128)(2,1)}, bf16[3,256,512]{2,1,0:T(8,128)(2,1)}, u32[]{:S(2)}, u32[]{:S(2)}) collective-permute-start(bf16[3,256,512]{2,1,0:T(8,128)(2,1)} %collective-permute-done.8.far_ref), channel_id=1, source_target_pairs={{0,1},{1,0},{2,3},{3,2},{4,5},{5,4},{6,7},{7,6},{8,9},{9,8},{10,11... | collective-permute-start | bytes 2359304 | tf_op jit(solution)/shard_map/ppermute | solution.py:27

commit v6 on v5

--- a/solution.py
+++ b/solution.py
@@ -458,12 +458,12 @@
 
 
 def sums_body(*refs, owned, block):
-    sources = refs[:-12]
+    sources = refs[:-15]
     (
         key_ref, target_ref, pair_key_ref, pair_target_ref,
-        send_ref, pack_ref,
-        keys_ref, targets_ref, hidden_ref, back_ref, sem, sem_in,
-    ) = refs[-12:]
+        send_out, pack_out,
+        send_ref, pack_ref, keys_ref, targets_ref, hidden_ref, back_ref, sem, sem_in, sem_out,
+    ) = refs[-15:]
     _, tokens = key_ref.shape
     half = pack_ref.shape[1]
     count = tokens // block
@@ -491,6 +491,8 @@
         for copy in copies:
             copy.start()
     pltpu.make_async_copy(sources[0], pack_ref, sem).wait()
+    leaving = [pltpu.make_async_copy(pack_ref, pack_out, sem_out.at[3])]
+    leaving[0].start()
     gate_lift = jnp.concatenate([pack_ref[0] * jnp.bfloat16(0.5), pack_ref[1]], axis=0)
     down = pack_ref[2]
 
@@ -515,15 +517,26 @@
 
     for slot in range(2 * count):
         combine(slot, *multiply(slot))
+
+    def leave(place, value):
+        send_ref[place] = value.astype(jnp.bfloat16)
+        leaving.append(
+            pltpu.make_async_copy(send_ref.at[place], send_out.at[place], sem_out.at[place])
+        )
+        leaving[-1].start()
+
     contract = (((1,), (1,)), ((), ()))
     sums = lax.dot_general(
         back_ref[...], keys_ref[...], contract, preferred_element_type=jnp.float32
     )
-    down_sums = lax.dot_general(
+    leave(0, sums[:half] * 0.5)
+    leave(1, sums[half:])
+    sums = lax.dot_general(
         hidden_ref[...], targets_ref[...], contract, preferred_element_type=jnp.float32
     )
-    for place, value in enumerate((sums[:half] * 0.5, sums[half:], down_sums)):
-        send_ref[place] = value.astype(jnp.bfloat16)
+    leave(2, sums)
+    for copy in leaving:
+        copy.wait()
 
 
 def fast_sums(sources, keys, targets, pair_keys, pair_targets, owned):
@@ -531,19 +544,21 @@
     shape = sources[0].shape
     half = shape[1]
     block = tokens
-    resident = pl.BlockSpec(memory_space=pltpu.VMEM)
     return pl.pallas_call(
         functools.partial(sums_body, owned=owned, block=block),
         out_shape=(jax.ShapeDtypeStruct(shape, jnp.bfloat16),) * 2,
         in_specs=anywhere(len(sources) + 4),
-        out_specs=(resident,) * 2,
+        out_specs=tuple(anywhere(2)),
         scratch_shapes=[
+            pltpu.VMEM(shape, jnp.bfloat16),
+            pltpu.VMEM(shape, jnp.bfloat16),
             pltpu.VMEM((features, 2 * tokens), jnp.bfloat16),
             pltpu.VMEM((features, 2 * tokens), jnp.bfloat16),
             pltpu.VMEM((half, 2 * tokens), jnp.bfloat16),
             pltpu.VMEM((2 * half, 2 * tokens), jnp.bfloat16),
             pltpu.SemaphoreType.DMA(()),
             pltpu.SemaphoreType.DMA((2, 2 * tokens // block)),
+            pltpu.SemaphoreType.DMA((4,)),
         ],
         cost_estimate=pl.CostEstimate(
             flops=24 * half * features * tokens,
@@ -557,123 +572,132 @@
 
 def recall_body(
     mine_ref, other_ref, far_ref, other_far_ref, pack_ref, pair_pack_ref, query_ref, out_ref,
-    w_ref, near_sums_ref, far_sums_ref, fresh_ref, turned_ref, sem,
+    w_ref, near_sums_ref, far_sums_ref, held_ref, made_ref, sem,
 ):
     half = mine_ref.shape[1]
-    hidden_rows, features = fresh_ref.shape[1:]
+    hidden_rows, features = w_ref.shape[1:]
     nt = (((1,), (1,)), ((), ()))
 
-    @pl.when(pl.program_id(0) == 0)
-    def _():
-        side = lax.axis_index("narrow") % 2
-
-        def arriving(matrix):
-            moves = (
-                (mine_ref, near_sums_ref, side),
-                (other_ref, near_sums_ref, 1 - side),
-                (far_ref, far_sums_ref, side),
-                (other_far_ref, far_sums_ref, 1 - side),
+    side = lax.axis_index("narrow") % 2
+
+    def arriving(matrix):
+        moves = (
+            (mine_ref, near_sums_ref, side),
+            (other_ref, near_sums_ref, 1 - side),
+            (far_ref, far_sums_ref, side),
+            (other_far_ref, far_sums_ref, 1 - side),
+        )
+        return [
+            pltpu.make_async_copy(
+                source.at[matrix],
+                target.at[matrix, half_rows(part, half)],
+                sem.at[place, matrix],
             )
-            return [
-                pltpu.make_async_copy(
-                    source.at[matrix],
-                    target.at[matrix, half_rows(part, half)],
-                    sem.at[place, matrix],
+            for place, (source, target, part) in enumerate(moves)
+        ]
+
+    sums = [arriving(matrix) for matrix in range(3)]
+    weights = [
+        pltpu.make_async_copy(source, w_ref.at[:, half_rows(part, half)], sem.at[4, place])
+        for place, (source, part) in enumerate(((pack_ref, side), (pair_pack_ref, 1 - side)))
+    ]
+    queries = pltpu.make_async_copy(query_ref, held_ref, sem.at[5, 2])
+    for copies in sums + [weights, [queries]]:
+        for copy in copies:
+            copy.start()
+    rows = lax.broadcasted_iota(jnp.int32, (hidden_rows, features), 0)
+    cols = lax.broadcasted_iota(jnp.int32, (hidden_rows, features), 1)
+    diagonal = rows == cols
+    rounded, gram, scale = [], [], []
+    for matrix, copies in enumerate(sums):
+        for copy in copies:
+            copy.wait()
+        summed = near_sums_ref[matrix].astype(jnp.float32) + far_sums_ref[matrix].astype(
+            jnp.float32
+        )
+        x = summed.astype(jnp.bfloat16)
+        product = lax.dot_general(x, x, nt, preferred_element_type=jnp.float32)
+        trace = jnp.sum(jnp.where(diagonal, product, 0.0), axis=0, keepdims=True)
+        scale.append(lax.rsqrt(jnp.sum(trace, axis=1, keepdims=True) + EPS))
+        rounded.append(x)
+        gram.append((product * (scale[-1] * scale[-1])).astype(jnp.bfloat16))
+    current = rounded
+    for sweep_index in range(NS_ITERS):
+        if sweep_index:
+            scale = [1.0] * 3
+            gram = [
+                lax.dot_general(x, x, nt, preferred_element_type=jnp.float32).astype(
+                    jnp.bfloat16
                 )
-                for place, (source, target, part) in enumerate(moves)
+                for x in current
             ]
-
-        sums = [arriving(matrix) for matrix in range(3)]
-        weights = [
-            pltpu.make_async_copy(source, w_ref.at[:, half_rows(part, half)], sem.at[4, place])
-            for place, (source, part) in enumerate(((pack_ref, side), (pair_pack_ref, 1 - side)))
+        lifted = [
+            jnp.dot(g, x, preferred_element_type=jnp.float32).astype(jnp.bfloat16)
+            for x, g in zip(current, gram)
         ]
-        for copies in sums + [weights]:
-            for copy in copies:
-                copy.start()
-        rows = lax.broadcasted_iota(jnp.int32, (hidden_rows, features), 0)
-        cols = lax.broadcasted_iota(jnp.int32, (hidden_rows, features), 1)
-        diagonal = rows == cols
-        rounded, gram, scale = [], [], []
-        for matrix, copies in enumerate(sums):
-            for copy in copies:
-                copy.wait()
-            summed = near_sums_ref[matrix].astype(jnp.float32) + far_sums_ref[matrix].astype(
-                jnp.float32
-            )
-            x = summed.astype(jnp.bfloat16)
-            product = lax.dot_general(x, x, nt, preferred_element_type=jnp.float32)
-            trace = jnp.sum(jnp.where(diagonal, product, 0.0), axis=0, keepdims=True)
-            scale.append(lax.rsqrt(jnp.sum(trace, axis=1, keepdims=True) + EPS))
-            rounded.append(x)
-            gram.append((product * (scale[-1] * scale[-1])).astype(jnp.bfloat16))
-        current = rounded
-        for sweep_index in range(NS_ITERS):
-            if sweep_index:
-                scale = [1.0] * 3
-                gram = [
-                    lax.dot_general(x, x, nt, preferred_element_type=jnp.float32).astype(
-                        jnp.bfloat16
-                    )
-                    for x in current
-                ]
-            lifted = [
-                jnp.dot(g, x, preferred_element_type=jnp.float32).astype(jnp.bfloat16)
-                for x, g in zip(current, gram)
-            ]
-            current = [
-                (
-                    (COEF_A * r) * x.astype(jnp.float32)
-                    + (COEF_B * r) * y.astype(jnp.float32)
-                    + (COEF_C * r) * jnp.dot(g, y, preferred_element_type=jnp.float32)
-                ).astype(jnp.bfloat16)
-                for x, y, g, r in zip(current, lifted, gram, scale)
-            ]
-        for copy in weights:
-            copy.wait()
-        for i in range(3):
-            axis = 0 if i == 2 else 1
-            initial = w_ref[i].astype(jnp.float32)
-            moved = initial - current[i].astype(jnp.float32)
-            wanted = jnp.mean(jnp.square(initial), axis=axis, keepdims=True) + EPS
-            present = jnp.mean(jnp.square(moved), axis=axis, keepdims=True) + EPS
-            fresh = (moved * (wanted * lax.rsqrt(wanted * present))).astype(jnp.bfloat16)
-            if i == 2:
-                turned_ref[...] = fresh.T
-            else:
-                fresh_ref[i] = fresh
-
-    pre = jnp.dot(
-        fresh_ref[...].reshape(2 * hidden_rows, features),
-        query_ref[...],
-        preferred_element_type=jnp.float32,
-    )
-    gate = 0.5 * pre[:hidden_rows]
-    hidden = (gate * (jnp.tanh(gate) + 1.0) * pre[hidden_rows:]).astype(jnp.bfloat16)
-    out_ref[...] = jnp.dot(turned_ref[...], hidden, preferred_element_type=jnp.float32).astype(
-        jnp.bfloat16
-    )
+        current = [
+            (
+                (COEF_A * r) * x.astype(jnp.float32)
+                + (COEF_B * r) * y.astype(jnp.float32)
+                + (COEF_C * r) * jnp.dot(g, y, preferred_element_type=jnp.float32)
+            ).astype(jnp.bfloat16)
+            for x, y, g, r in zip(current, lifted, gram, scale)
+        ]
+    for copy in weights:
+        copy.wait()
+
+    def fresh(i):
+        axis = 0 if i == 2 else 1
+        initial = w_ref[i].astype(jnp.float32)
+        moved = initial - current[i].astype(jnp.float32)
+        wanted = jnp.mean(jnp.square(initial), axis=axis, keepdims=True) + EPS
+        present = jnp.mean(jnp.square(moved), axis=axis, keepdims=True) + EPS
+        return (moved * (wanted * lax.rsqrt(wanted * present))).astype(jnp.bfloat16)
+
+    queries.wait()
+    tokens = held_ref.shape[1]
+    block = tokens // 2
+    spans = [slice(at, at + block) for at in range(0, tokens, block)]
+    fresh_gate = fresh(0)
+    gates = [
+        jnp.dot(fresh_gate * jnp.bfloat16(0.5), held_ref[:, span], preferred_element_type=jnp.float32)
+        for span in spans
+    ]
+    fresh_lift = fresh(1)
+    lifts = [
+        jnp.dot(fresh_lift, held_ref[:, span], preferred_element_type=jnp.float32) for span in spans
+    ]
+    fresh_down = fresh(2).T
+    leaving = []
+    for place, (span, gate, lift) in enumerate(zip(spans, gates, lifts)):
+        hidden = (gate * (jnp.tanh(gate) + 1.0) * lift).astype(jnp.bfloat16)
+        made_ref[:, span] = jnp.dot(
+            fresh_down, hidden, preferred_element_type=jnp.float32
+        ).astype(jnp.bfloat16)
+        leaving.append(
+            pltpu.make_async_copy(made_ref.at[:, span], out_ref.at[:, span], sem.at[5, place])
+        )
+        leaving[-1].start()
+    for copy in leaving:
+        copy.wait()
 
 
 def fast_recall(sums, packs, queries):
     features, tokens = queries.shape
     half = packs[0].shape[1]
     hidden_rows = 2 * half
-    block = min(1024, tokens)
-    piece = pl.BlockSpec((features, block), lambda i: (0, i))
     return pl.pallas_call(
         recall_body,
         out_shape=jax.ShapeDtypeStruct((features, tokens), jnp.bfloat16),
-        grid=(tokens // block,),
-        in_specs=anywhere(6) + [piece],
-        out_specs=piece,
+        in_specs=anywhere(7),
+        out_specs=pl.BlockSpec(memory_space=pl.ANY),
         scratch_shapes=[
             pltpu.VMEM((3, hidden_rows, features), jnp.bfloat16),
             pltpu.VMEM((3, hidden_rows, features), jnp.bfloat16),
             pltpu.VMEM((3, hidden_rows, features), jnp.bfloat16),
-            pltpu.VMEM((2, hidden_rows, features), jnp.bfloat16),
-            pltpu.VMEM((features, hidden_rows), jnp.bfloat16),
-            pltpu.SemaphoreType.DMA((5, 3)),
+            pltpu.VMEM((features, tokens), jnp.bfloat16),
+            pltpu.VMEM((features, tokens), jnp.bfloat16),
+            pltpu.SemaphoreType.DMA((6, 3)),
         ],
         cost_estimate=pl.CostEstimate(
             flops=6 * hidden_rows * features * tokens + 18 * NS_ITERS * hidden_rows * features**2,

time: 107 us -> 105 us (0.981)
  Pallas kernels: 56 us -> 53.8 us
    pallas_call x1, Pallas kernels: 14.8 us -> 12.8 us  [fast_recall(): pl.pallas_call(recall_body, out_shape=jax.ShapeDtypeStruct((features, tok...]
where the time goes in v6:
time: 105 us
  Pallas kernels  53.8 us (51%)
  waiting for transfers between devices  35.5 us (34%)
  starting transfers between devices  14.6 us (14%)
    ppermute x2, waiting for transfers between devices, from_behind(): lax.ppermute(value, axis, [(source, source + steps) for source in range(i...  15.9 us
    ppermute x6, waiting for transfers between devices, swapped(): lax.ppermute(array, axis, [(i, i ^ 1 << distance) for i in range(lax.axis...  14.1 us
    pallas_call x1, Pallas kernels, fast_recall(): pl.pallas_call(recall_body, out_shape=jax.ShapeDtypeStruct((features, tok...  12.8 us
    pallas_call x2, Pallas kernels, attend_early(): pl.pallas_call(early_body, out_shape=jax.ShapeDtypeStruct((features, toke...  12.4 us
    pallas_call x1, Pallas kernels, fast_sums(): pl.pallas_call(functools.partial(sums_body, owned=owned, block=block), ou...  12.2 us
    pallas_call x1, Pallas kernels, attend_late(): pl.pallas_call(functools.partial(attend_body, block=min(256, WINDOW), win...  9.69 us
    ppermute x3, starting transfers between devices, from_owner(): return lax.ppermute(value, ('wide', 'narrow'), pairs)  7.28 us
    ppermute x2, starting transfers between devices, from_behind(): lax.ppermute(value, axis, [(source, source + steps) for source in range(i...  6.01 us
  transfers between devices with their start and end apart: 11, of which 4 were waited for; matrix products, arithmetic and copies ran while one was open for 0% of the time, Pallas kernels for 27%

profile of v6, /device:TPU:20, one launch (start us, length us, event | category | flops | bytes accessed | tf_op | source)
XLA Modules:
  0.0 104.7 jit_solution(11833555221789348484)
XLA Ops:
  0.6 0.1 collective-permute-start.5
  0.7 4.2 %stage.1 = (bf16[512,2048]{1,0:T(8,128)(2,1)}, bf16[2,256,1024]{2,1,0:T(8,128)(2,1)}, bf16[2,256,1024]{2,1,0:T(8,128)(2,1)}) custom-call(bf16[512,2048]{1,0:T(8,128)(2,1)} %refs_4_.5, bf16[512,2048]{1,0:T(8,128)(2,1)} %refs_4_.4, f32[8,8192]{1,0:T(8,128)} %rate_ref.1), custom_call_target="tpu_custom_call" | custom-call | flops 1048576 | bytes 8388608 | tf_op jit(solution)/shard_map/stage/pallas_call | solution.py:437
  4.9 0.6 collective-permute-start.6
  5.5 2.5 %prepare.1 = (bf16[3,256,512]{2,1,0:T(8,128)(2,1)}, bf16[3,256,512]{2,1,0:T(8,128)(2,1)}) custom-call(bf16[2,512,512]{2,1,0:T(8,128)(2,1)} %gate_ref.1, bf16[2,512,512]{2,1,0:T(8,128)(2,1)} %lift_ref.1, bf16[2,512,512]{2,1,0:T(8,128)(2,1)} %down_ref.1), custom_call_target="tpu_custom_call" | custom-call | bytes 3145728 | tf_op jit(solution)/shard_map/prepare/pallas_call | solution.py:373
  8.0 2.9 %collective-permute-start = (bf16[3,256,512]{2,1,0:T(8,128)(2,1)}, bf16[3,256,512]{2,1,0:T(8,128)(2,1)}, u32[]{:S(2)}, u32[]{:S(2)}) collective-permute-start(bf16[3,256,512]{2,1,0:T(8,128)(2,1)} %get-tuple-element.17), channel_id=1, source_target_pairs={{0,1},{4,5},{9,8},{13,12},{18,19},{22,23},{27,26},{31,30}} | collective-permute-start | bytes 2359304 | tf_op jit(solution)/shard_map/ppermute | solution.py:747
  10.9 2.2 %collective-permute-start.1 = (bf16[3,256,512]{2,1,0:T(8,128)(2,1)}, bf16[3,256,512]{2,1,0:T(8,128)(2,1)}, u32[]{:S(2)}, u32[]{:S(2)}) collective-permute-start(bf16[3,256,512]{2,1,0:T(8,128)(2,1)} %get-tuple-element.23.refs_0_), channel_id=1, source_target_pairs={{0,2},{4,6},{9,11},{13,15},{18,16},{22,20},{27,25},{31,29}} | collective-permute-start | bytes 2359304 | tf_op jit(solution)/shard_map/ppermute | solution.py:747
  13.1 2.2 %collective-permute-start.2 = (bf16[3,256,512]{2,1,0:T(8,128)(2,1)}, bf16[3,256,512]{2,1,0:T(8,128)(2,1)}, u32[]{:S(2)}, u32[]{:S(2)}) collective-permute-start(bf16[3,256,512]{2,1,0:T(8,128)(2,1)} %get-tuple-element.17), channel_id=1, source_target_pairs={{0,3},{4,7},{9,10},{13,14},{18,17},{22,21},{27,24},{31,28}} | collective-permute-start | bytes 2359304 | tf_op jit(solution)/shard_map/ppermute | solution.py:747
  15.2 9.7 %attend_late.1.refs_7_ = bf16[512,2048]{1,0:T(8,128)(2,1)} custom-call(bf16[512,2048]{1,0:T(8,128)(2,1)} %query_ref.1, bf16[512,2048]{1,0:T(8,128)(2,1)} %refs_4_.5, bf16[512,2048]{1,0:T(8,128)(2,1)} %refs_4_.4, bf16[512,2048]{1,0:T(8,128)(2,1)} %refs_4_.5, bf16[512,2048]{1,0:T(8,128)(2,1)} %refs_4_.4), custom_call_target="tpu_custom_call" | custom-call | flops 2684354560 | bytes 5242880 | tf_op jit(solution)/shard_map/attend_late/pallas_call | solution.py:287
  24.9 0.0 collective-permute-done.refs_1_
  24.9 0.0 collective-permute-done.1.refs_2_
  24.9 5.5 %collective-permute-done.2.refs_3_ = bf16[3,256,512]{2,1,0:T(8,128)(2,1)} collective-permute-done((bf16[3,256,512]{2,1,0:T(8,128)(2,1)}, bf16[3,256,512]{2,1,0:T(8,128)(2,1)}, u32[]{:S(2)}, u32[]{:S(2)}) %collective-permute-start.2) | collective-permute-done | bytes 786464 | tf_op jit(solution)/shard_map/ppermute | solution.py:747
  30.4 0.0 collective-permute-done.5.refs_6_
  30.4 0.0 collective-permute-done.6.refs_7_
  30.4 12.2 %fast_sums.1 = (bf16[3,256,512]{2,1,0:T(8,128)(2,1)}, bf16[3,256,512]{2,1,0:T(8,128)(2,1)}) custom-call(bf16[3,256,512]{2,1,0:T(8,128)(2,1)} %get-tuple-element.23.refs_0_, bf16[3,256,512]{2,1,0:T(8,128)(2,1)} %collective-permute-done.refs_1_, bf16[3,256,512]{2,1,0:T(8,128)(2,1)} %collective-permute-done.1.refs_2_, ...), custom_call_target="tpu_custom_call" | custom-call | flops 6442450944 | bytes 10747904 | tf_op jit(solution)/shard_map/fast_sums/pallas_call | solution.py:547
  42.7 0.1 collective-permute-start.8
  42.7 3.9 %collective-permute-start.4 = (bf16[2,256,1024]{2,1,0:T(8,128)(2,1)}, bf16[2,256,1024]{2,1,0:T(8,128)(2,1)}, u32[]{:S(2)}, u32[]{:S(2)}) collective-permute-start(bf16[2,256,1024]{2,1,0:T(8,128)(2,1)} %get-tuple-element.21), channel_id=1, source_target_pairs={{0,1},{1,2},{2,3},{4,5},{5,6},{6,7},{8,9},{9,10},{10,11},{12,13},{... | collective-permute-start | bytes 3145736 | tf_op jit(solution)/shard_map/ppermute | solution.py:41
  46.6 2.1 %collective-permute-start.3 = (bf16[2,256,1024]{2,1,0:T(8,128)(2,1)}, bf16[2,256,1024]{2,1,0:T(8,128)(2,1)}, u32[]{:S(2)}, u32[]{:S(2)}) collective-permute-start(bf16[2,256,1024]{2,1,0:T(8,128)(2,1)} %get-tuple-element.20), channel_id=1, source_target_pairs={{0,1},{1,2},{2,3},{4,5},{5,6},{6,7},{8,9},{9,10},{10,11},{12,13},{... | collective-permute-start | bytes 3145736 | tf_op jit(solution)/shard_map/ppermute | solution.py:41
  48.8 0.1 collective-permute-start.7
  48.8 0.5 collective-permute-start.10
  49.3 14.1 %collective-permute-done.8.far_ref = bf16[3,256,512]{2,1,0:T(8,128)(2,1)} collective-permute-done((bf16[3,256,512]{2,1,0:T(8,128)(2,1)}, bf16[3,256,512]{2,1,0:T(8,128)(2,1)}, u32[]{:S(2)}, u32[]{:S(2)}) %collective-permute-start.8) | collective-permute-done | bytes 786464 | tf_op jit(solution)/shard_map/ppermute | solution.py:27
  63.5 0.0 collective-permute-start.9
  63.5 10.8 %collective-permute-done.4.refs_1_.refs_2_ = bf16[2,256,1024]{2,1,0:T(8,128)(2,1)} collective-permute-done((bf16[2,256,1024]{2,1,0:T(8,128)(2,1)}, bf16[2,256,1024]{2,1,0:T(8,128)(2,1)}, u32[]{:S(2)}, u32[]{:S(2)}) %collective-permute-start.4) | collective-permute-done | bytes 1048608 | tf_op jit(solution)/shard_map/ppermute | solution.py:41
  74.3 6.2 %attend_early.2.refs_7_ = bf16[512,2048]{1,0:T(8,128)(2,1)} custom-call(bf16[512,2048]{1,0:T(8,128)(2,1)} %query_ref.1, bf16[2,256,1024]{2,1,0:T(8,128)(2,1)} %collective-permute-done.4.refs_1_.refs_2_, bf16[2,256,1024]{2,1,0:T(8,128)(2,1)} %collective-permute-done.4.refs_1_.refs_2_, bf16[512,2048]{1,0:T(8,128)(2,1)} %refs_4_.5, ...), custom_call_target="tpu_custom_call", output_to_operand_aliasing={{}: (7, {})} | custom-call | flops 1342177280 | bytes 3670016 | tf_op jit(solution)/shard_map/attend_early/pallas_call | solution.py:315
  80.5 5.0 %collective-permute-done.3.refs_1_.refs_2_ = bf16[2,256,1024]{2,1,0:T(8,128)(2,1)} collective-permute-done((bf16[2,256,1024]{2,1,0:T(8,128)(2,1)}, bf16[2,256,1024]{2,1,0:T(8,128)(2,1)}, u32[]{:S(2)}, u32[]{:S(2)}) %collective-permute-start.3) | collective-permute-done | bytes 1048608 | tf_op jit(solution)/shard_map/ppermute | solution.py:41
  85.5 6.2 %attend_early.3 = bf16[512,2048]{1,0:T(8,128)(2,1)} custom-call(bf16[512,2048]{1,0:T(8,128)(2,1)} %query_ref.1, bf16[2,256,1024]{2,1,0:T(8,128)(2,1)} %collective-permute-done.3.refs_1_.refs_2_, bf16[2,256,1024]{2,1,0:T(8,128)(2,1)} %collective-permute-done.3.refs_1_.refs_2_, bf16[512,2048]{1,0:T(8,128)(2,1)} %refs_4_.5, ...), custom_call_target="tpu_custom_call", output_to_operand_aliasing={{}: (7, {})} | custom-call | flops 1342177280 | bytes 3670016 | tf_op jit(solution)/shard_map/attend_early/pallas_call | solution.py:315
  91.7 0.0 collective-permute-done.7.other_ref
  91.7 0.0 collective-permute-done.10.pair_pack_ref
  91.7 0.0 collective-permute-done.9.other_far_ref
  91.7 12.8 %fast_recall.1 = bf16[512,2048]{1,0:T(8,128)(2,1)} custom-call(bf16[3,256,512]{2,1,0:T(8,128)(2,1)} %get-tuple-element.28.mine_ref, bf16[3,256,512]{2,1,0:T(8,128)(2,1)} %collective-permute-done.7.other_ref, bf16[3,256,512]{2,1,0:T(8,128)(2,1)} %collective-permute-done.8.far_ref, bf16[3,256,512]{2,1,0:T(8,128)(2,1)} %collective-permute-done.9.other_far_ref, ...), custom_call_target="tpu_custom_call" | custom-call | flops 8053063680 | bytes 7340032 | tf_op jit(solution)/shard_map/fast_recall/pallas_call | solution.py:689
Async XLA Ops:
  0.6 29.8 %collective-permute-start.5 = (bf16[512,2048]{1,0:T(8,128)(2,1)}, bf16[512,2048]{1,0:T(8,128)(2,1)}, u32[]{:S(2)}, u32[]{:S(2)}) collective-permute-start(bf16[512,2048]{1,0:T(8,128)(2,1)} %refs_4_.5), channel_id=1, source_target_pairs={{0,1},{1,0},{2,3},{3,2},{4,5},{5,4},{6,7},{7,6},{8,9},{9,8},{10,11... | collective-permute-start | bytes 6291464 | tf_op jit(solution)/shard_map/ppermute | solution.py:27
  4.9 25.5 %collective-permute-start.6 = (bf16[512,2048]{1,0:T(8,128)(2,1)}, bf16[512,2048]{1,0:T(8,128)(2,1)}, u32[]{:S(2)}, u32[]{:S(2)}) collective-permute-start(bf16[512,2048]{1,0:T(8,128)(2,1)} %get-tuple-element.27.refs_5_), channel_id=1, source_target_pairs={{0,1},{1,0},{2,3},{3,2},{4,5},{5,4},{6,7},{7,6},{8,9},{9,8},{10,11... | collective-permute-start | bytes 6291464 | tf_op jit(solution)/shard_map/ppermute | solution.py:27
  8.0 17.0 %collective-permute-start = (bf16[3,256,512]{2,1,0:T(8,128)(2,1)}, bf16[3,256,512]{2,1,0:T(8,128)(2,1)}, u32[]{:S(2)}, u32[]{:S(2)}) collective-permute-start(bf16[3,256,512]{2,1,0:T(8,128)(2,1)} %get-tuple-element.17), channel_id=1, source_target_pairs={{0,1},{4,5},{9,8},{13,12},{18,19},{22,23},{27,26},{31,30}} | collective-permute-start | bytes 2359304 | tf_op jit(solution)/shard_map/ppermute | solution.py:747
  10.9 14.1 %collective-permute-start.1 = (bf16[3,256,512]{2,1,0:T(8,128)(2,1)}, bf16[3,256,512]{2,1,0:T(8,128)(2,1)}, u32[]{:S(2)}, u32[]{:S(2)}) collective-permute-start(bf16[3,256,512]{2,1,0:T(8,128)(2,1)} %get-tuple-element.23.refs_0_), channel_id=1, source_target_pairs={{0,2},{4,6},{9,11},{13,15},{18,16},{22,20},{27,25},{31,29}} | collective-permute-start | bytes 2359304 | tf_op jit(solution)/shard_map/ppermute | solution.py:747
  13.1 17.3 %collective-permute-start.2 = (bf16[3,256,512]{2,1,0:T(8,128)(2,1)}, bf16[3,256,512]{2,1,0:T(8,128)(2,1)}, u32[]{:S(2)}, u32[]{:S(2)}) collective-permute-start(bf16[3,256,512]{2,1,0:T(8,128)(2,1)} %get-tuple-element.17), channel_id=1, source_target_pairs={{0,3},{4,7},{9,10},{13,14},{18,17},{22,21},{27,24},{31,28}} | collective-permute-start | bytes 2359304 | tf_op jit(solution)/shard_map/ppermute | solution.py:747
  42.7 20.8 %collective-permute-start.8 = (bf16[3,256,512]{2,1,0:T(8,128)(2,1)}, bf16[3,256,512]{2,1,0:T(8,128)(2,1)}, u32[]{:S(2)}, u32[]{:S(2)}) collective-permute-start(bf16[3,256,512]{2,1,0:T(8,128)(2,1)} %get-tuple-element.28.mine_ref), channel_id=1, source_target_pairs={{0,2},{1,3},{2,0},{3,1},{4,6},{5,7},{6,4},{7,5},{8,10},{9,11},{10,... | collective-permute-start | bytes 2359304 | tf_op jit(solution)/shard_map/ppermute | solution.py:27
  42.7 31.5 %collective-permute-start.4 = (bf16[2,256,1024]{2,1,0:T(8,128)(2,1)}, bf16[2,256,1024]{2,1,0:T(8,128)(2,1)}, u32[]{:S(2)}, u32[]{:S(2)}) collective-permute-start(bf16[2,256,1024]{2,1,0:T(8,128)(2,1)} %get-tuple-element.21), channel_id=1, source_target_pairs={{0,1},{1,2},{2,3},{4,5},{5,6},{6,7},{8,9},{9,10},{10,11},{12,13},{... | collective-permute-start | bytes 3145736 | tf_op jit(solution)/shard_map/ppermute | solution.py:41
  46.6 38.9 %collective-permute-start.3 = (bf16[2,256,1024]{2,1,0:T(8,128)(2,1)}, bf16[2,256,1024]{2,1,0:T(8,128)(2,1)}, u32[]{:S(2)}, u32[]{:S(2)}) collective-permute-start(bf16[2,256,1024]{2,1,0:T(8,128)(2,1)} %get-tuple-element.20), channel_id=1, source_target_pairs={{0,1},{1,2},{2,3},{4,5},{5,6},{6,7},{8,9},{9,10},{10,11},{12,13},{... | collective-permute-start | bytes 3145736 | tf_op jit(solution)/shard_map/ppermute | solution.py:41
  48.8 43.0 %collective-permute-start.7 = (bf16[3,256,512]{2,1,0:T(8,128)(2,1)}, bf16[3,256,512]{2,1,0:T(8,128)(2,1)}, u32[]{:S(2)}, u32[]{:S(2)}) collective-permute-start(bf16[3,256,512]{2,1,0:T(8,128)(2,1)} %get-tuple-element.28.mine_ref), channel_id=1, source_target_pairs={{0,1},{1,0},{2,3},{3,2},{4,5},{5,4},{6,7},{7,6},{8,9},{9,8},{10,11... | collective-permute-start | bytes 2359304 | tf_op jit(solution)/shard_map/ppermute | solution.py:27
  48.8 42.9 %collective-permute-start.10 = (bf16[3,256,512]{2,1,0:T(8,128)(2,1)}, bf16[3,256,512]{2,1,0:T(8,128)(2,1)}, u32[]{:S(2)}, u32[]{:S(2)}) collective-permute-start(bf16[3,256,512]{2,1,0:T(8,128)(2,1)} %get-tuple-element.29.pack_ref), channel_id=1, source_target_pairs={{0,1},{1,0},{2,3},{3,2},{4,5},{5,4},{6,7},{7,6},{8,9},{9,8},{10,11... | collective-permute-start | bytes 2359304 | tf_op jit(solution)/shard_map/ppermute | solution.py:27
  63.5 28.3 %collective-permute-start.9 = (bf16[3,256,512]{2,1,0:T(8,128)(2,1)}, bf16[3,256,512]{2,1,0:T(8,128)(2,1)}, u32[]{:S(2)}, u32[]{:S(2)}) collective-permute-start(bf16[3,256,512]{2,1,0:T(8,128)(2,1)} %collective-permute-done.8.far_ref), channel_id=1, source_target_pairs={{0,1},{1,0},{2,3},{3,2},{4,5},{5,4},{6,7},{7,6},{8,9},{9,8},{10,11... | collective-permute-start | bytes 2359304 | tf_op jit(solution)/shard_map/ppermute | solution.py:27

commit v7 on v6

--- a/solution.py
+++ b/solution.py
@@ -204,32 +204,14 @@
     ).astype(jnp.bfloat16)
 
 
-def attend_body(q_ref, kp_ref, vp_ref, kc_ref, vc_ref, *rest, block, window):
-    cached = len(rest) > 3
-    o_ref, kt_ref, v_ref = rest[-3:]
+def attend_body(
+    q_ref, kp_ref, vp_ref, kc_ref, vc_ref, o_ref, kt_ref, v_ref, *, block, window
+):
     hd = q_ref.shape[0]
     scale = LOG2E / math.sqrt(hd)
 
-    def place(k, v, at):
-        turned = k[...].T
-        kt_ref[at : at + window, :hd] = turned
-        kt_ref[at : at + window, hd:] = turned
-        v_ref[:hd, at : at + window] = v[...]
-
-    if cached:
-        leading = lax.axis_index("narrow") == 0
-
-        @pl.when(leading)
-        def _():
-            place(*rest[:2], 0)
-
-        @pl.when(jnp.logical_not(leading))
-        def _():
-            place(kp_ref, vp_ref, 0)
-
-    else:
-        place(kp_ref, vp_ref, 0)
-    place(kc_ref, vc_ref, window)
+    placed(kp_ref, vp_ref, kt_ref, v_ref, 0)
+    placed(kc_ref, vc_ref, kt_ref, v_ref, window)
     v_ref[hd:, :] = jnp.ones((v_ref.shape[0] - hd, 2 * window), jnp.bfloat16)
     rows = lax.broadcasted_iota(jnp.int32, (block, block), 0)
     cols = lax.broadcasted_iota(jnp.int32, (block, block), 1)
@@ -301,34 +283,249 @@
     )(queries, keys, values, keys, values)
 
 
-def attend_early(queries, keys, values, prior, cache_keys, cache_values, late, part):
+def two_term(q_ref, at, scale):
+    q = q_ref[:, at].astype(jnp.float32) * scale
+    high = q.astype(jnp.bfloat16)
+    low = (q - high.astype(jnp.float32)).astype(jnp.bfloat16)
+    return jnp.concatenate([high, low], axis=0)
+
+
+def placed(k, v, kt_ref, v_ref, at):
+    hd, width = k.shape
+    turned = k[...].T
+    kt_ref[at : at + width, :hd] = turned
+    kt_ref[at : at + width, hd:] = turned
+    v_ref[:hd, at : at + width] = v[...]
+
+
+def early_body(
+    q_ref, kp_ref, vp_ref, kc_ref, vc_ref, ck_ref, cv_ref, _, o_ref, part_ref, top_ref, mass_ref,
+    kt_ref, v_ref, *, block,
+):
+    hd, window = q_ref.shape
+    scale = LOG2E / math.sqrt(hd)
+    near = kp_ref.shape[1]
+    inner = window // block
+    missing = (window - near) // block
+    leading = lax.axis_index("narrow") == 0
+
+    @pl.when(leading)
+    def _():
+        placed(ck_ref, cv_ref, kt_ref, v_ref, 0)
+
+    @pl.when(jnp.logical_not(leading))
+    def _():
+        placed(kp_ref, vp_ref, kt_ref, v_ref, 0)
+
+    placed(kc_ref, vc_ref, kt_ref, v_ref, near)
+    v_ref[hd:, :] = jnp.ones((v_ref.shape[0] - hd, v_ref.shape[1]), jnp.bfloat16)
+    rows = lax.broadcasted_iota(jnp.int32, (block, block), 0)
+    cols = lax.broadcasted_iota(jnp.int32, (block, block), 1)
+    first = rows > cols
+
+    def chunk(j):
+        return slice((j - missing) * block, (j - missing + 1) * block)
+
+    def scores(b):
+        pair = two_term(q_ref, slice(b * block, (b + 1) * block), scale)
+        parts = [
+            jnp.dot(kt_ref[chunk(j), :], pair, preferred_element_type=jnp.float32)
+            for j in range(max(b, missing), b + inner + 1)
+        ]
+        if b >= missing:
+            return [jnp.where(first, parts[0], parts[inner])] + parts[1:inner]
+        return parts[:-1] + [jnp.where(first, -jnp.inf, parts[-1])]
+
+    def blend(b, parts):
+        top = functools.reduce(jnp.maximum, parts)
+        top = jnp.max(top, axis=0, keepdims=True)
+        raised = [jnp.exp2(part - top).astype(jnp.bfloat16) for part in parts]
+        if b >= missing:
+            zero = jnp.zeros_like(raised[0])
+            ends = jnp.where(first, raised[0], zero), jnp.where(first, zero, raised[0])
+            raised = [ends[0]] + raised[1:] + [ends[1]]
+        span = v_ref[:, chunk(max(b, missing)).start : chunk(b + inner).stop]
+        out = jnp.dot(span, jnp.concatenate(raised, axis=0), preferred_element_type=jnp.float32)
+        if b >= missing:
+            at = slice((b - missing) * block, (b - missing + 1) * block)
+            o_ref[:, at] = (out[:hd] * (1.0 / out[hd : hd + 1])).astype(jnp.bfloat16)
+        else:
+            at = slice(b * block, (b + 1) * block)
+            part_ref[:, at] = out[:hd]
+            top_ref[:, at] = jnp.broadcast_to(top, (top_ref.shape[0], block))
+            mass_ref[:, at] = jnp.broadcast_to(out[hd : hd + 1], (top_ref.shape[0], block))
+
+    ready = scores(0)
+    for b in range(1, inner):
+        following = scores(b)
+        blend(b - 1, ready)
+        ready = following
+    blend(inner - 1, ready)
+
+
+def attend_early(queries, keys, values, prior, cache_keys, cache_values, late):
     features, tokens = queries.shape
-    heads = prior.shape[1] // HEAD_SIZE
-    here = pl.BlockSpec((HEAD_SIZE, WINDOW), lambda h: (h + part * heads, 0))
-    prior_keys = pl.BlockSpec((None, HEAD_SIZE, WINDOW), lambda h: (0, h, 0))
-    prior_values = pl.BlockSpec((None, HEAD_SIZE, WINDOW), lambda h: (1, h, 0))
-    body = functools.partial(attend_body, block=min(256, WINDOW), window=WINDOW)
-
-    def early_body(*refs):
-        body(*refs[:7], *refs[8:])
-
+    heads = features // HEAD_SIZE
+    near = prior.shape[2]
+    far = WINDOW - near
+    here = pl.BlockSpec((HEAD_SIZE, WINDOW), lambda h: (h, 0))
+    nearer = pl.BlockSpec((HEAD_SIZE, near), lambda h: (h, far // near))
+    prior_keys = pl.BlockSpec((None, HEAD_SIZE, near), lambda h: (0, h, 0))
+    prior_values = pl.BlockSpec((None, HEAD_SIZE, near), lambda h: (1, h, 0))
+    rows = 8
+    stats = jax.ShapeDtypeStruct((heads * rows, far), jnp.float32)
+    stat = pl.BlockSpec((rows, far), lambda h: (h, 0))
     return pl.pallas_call(
-        early_body,
-        out_shape=jax.ShapeDtypeStruct((features, tokens), jnp.bfloat16),
+        functools.partial(early_body, block=min(256, near)),
+        out_shape=(
+            jax.ShapeDtypeStruct((features, tokens), jnp.bfloat16),
+            jax.ShapeDtypeStruct((features, far), jnp.float32),
+            stats,
+            stats,
+        ),
         grid=(heads,),
-        in_specs=[here, prior_keys, prior_values, here, here, here, here]
+        in_specs=[here, prior_keys, prior_values, here, here, nearer, nearer]
         + [pl.BlockSpec(memory_space=pl.ANY)],
-        out_specs=here,
-        scratch_shapes=attend_scratch(),
+        out_specs=(nearer, pl.BlockSpec((HEAD_SIZE, far), lambda h: (h, 0)), stat, stat),
+        scratch_shapes=[
+            pltpu.VMEM((near + WINDOW, 2 * HEAD_SIZE), jnp.bfloat16),
+            pltpu.VMEM((HEAD_SIZE + 16, near + WINDOW), jnp.bfloat16),
+        ],
         input_output_aliases={7: 0},
         cost_estimate=pl.CostEstimate(
-            flops=5 * heads * HEAD_SIZE * WINDOW**2,
-            bytes_accessed=14 * heads * HEAD_SIZE * WINDOW,
+            flops=5 * features * WINDOW**2,
+            bytes_accessed=14 * features * WINDOW,
             transcendentals=heads * WINDOW**2,
         ),
         name="attend_early",
         compiler_params=pltpu.CompilerParams(vmem_limit_bytes=VMEM_GRANT),
     )(queries, prior, prior, keys, values, cache_keys, cache_values, late)
+
+
+def last_body(
+    q_ref, prior_ref, ck_ref, cv_ref, part_ref, top_ref, mass_ref, _, o_ref,
+    held_q, held_k, held_v, held_part, held_top, held_mass, kt_ref, v_ref, made_ref, sem,
+    *, block,
+):
+    features, far = part_ref.shape
+    hd = HEAD_SIZE
+    heads = features // hd
+    scale = LOG2E / math.sqrt(hd)
+    missing = far // block
+    leading = lax.axis_index("narrow") == 0
+    plain = [
+        pltpu.make_async_copy(top_ref, held_top, sem.at[0, 0]),
+        pltpu.make_async_copy(mass_ref, held_mass, sem.at[0, 1]),
+    ]
+    arriving = []
+    for h in range(heads):
+        at = slice(h * hd, (h + 1) * hd)
+        keys = pltpu.make_async_copy(prior_ref.at[0, at], held_k.at[at], sem.at[1, h])
+        values = pltpu.make_async_copy(prior_ref.at[1, at], held_v.at[at], sem.at[2, h])
+
+        @pl.when(leading)
+        def _(at=at, h=h):
+            pltpu.make_async_copy(ck_ref.at[at, :far], held_k.at[at], sem.at[1, h]).start()
+            pltpu.make_async_copy(cv_ref.at[at, :far], held_v.at[at], sem.at[2, h]).start()
+
+        @pl.when(jnp.logical_not(leading))
+        def _(keys=keys, values=values):
+            keys.start()
+            values.start()
+
+        others = [
+            pltpu.make_async_copy(q_ref.at[at, :far], held_q.at[at], sem.at[3, h]),
+            pltpu.make_async_copy(part_ref.at[at], held_part.at[at], sem.at[4, h]),
+        ]
+        for copy in others + (plain if h == 0 else []):
+            copy.start()
+        arriving.append([keys, values] + others)
+    rows = lax.broadcasted_iota(jnp.int32, (block, block), 0)
+    cols = lax.broadcasted_iota(jnp.int32, (block, block), 1)
+    first = rows > cols
+    v_ref[:, hd:, :] = jnp.ones((heads, v_ref.shape[1] - hd, far), jnp.bfloat16)
+    leaving = []
+    for copy in plain:
+        copy.wait()
+
+    def scores(h, b):
+        at = slice(h * hd, (h + 1) * hd)
+        if b == 0:
+            for copy in arriving[h]:
+                copy.wait()
+            placed(held_k.at[at], held_v.at[at], kt_ref.at[h], v_ref.at[h], 0)
+        pair = two_term(held_q.at[at], slice(b * block, (b + 1) * block), scale)
+        parts = [
+            jnp.dot(
+                kt_ref[h, j * block : (j + 1) * block, :], pair, preferred_element_type=jnp.float32
+            )
+            for j in range(b, missing)
+        ]
+        return [jnp.where(first, parts[0], -jnp.inf)] + parts[1:]
+
+    def blend(h, b, parts):
+        at = slice(h * hd, (h + 1) * hd)
+        span = slice(b * block, (b + 1) * block)
+        before = held_top[h * 8 : h * 8 + 1, span]
+        top = functools.reduce(jnp.maximum, parts)
+        top = jnp.maximum(jnp.max(top, axis=0, keepdims=True), before)
+        kept = jnp.exp2(before - top)
+        weights = jnp.concatenate(
+            [jnp.exp2(part - top).astype(jnp.bfloat16) for part in parts], axis=0
+        )
+        out = jnp.dot(v_ref[h, :, b * block :], weights, preferred_element_type=jnp.float32)
+        mass = held_mass[h * 8 : h * 8 + 1, span] * kept + out[hd : hd + 1]
+        made_ref[at, span] = ((held_part[at, span] * kept + out[:hd]) * (1.0 / mass)).astype(
+            jnp.bfloat16
+        )
+        if b == missing - 1:
+            leaving.append(
+                pltpu.make_async_copy(made_ref.at[at], o_ref.at[at, :far], sem.at[5, h])
+            )
+            leaving[-1].start()
+
+    turns = [(h, b) for h in range(heads) for b in range(missing)]
+    ready = scores(*turns[0])
+    for turn, ahead in zip(turns, turns[1:]):
+        following = scores(*ahead)
+        blend(*turn, ready)
+        ready = following
+    blend(*turns[-1], ready)
+    for copy in leaving:
+        copy.wait()
+
+
+def attend_last(queries, prior, cache_keys, cache_values, part, top, mass, early):
+    features, tokens = queries.shape
+    heads = features // HEAD_SIZE
+    far = part.shape[1]
+    pieces = pltpu.VMEM((features, far), jnp.bfloat16)
+    return pl.pallas_call(
+        functools.partial(last_body, block=min(256, far)),
+        out_shape=jax.ShapeDtypeStruct((features, tokens), jnp.bfloat16),
+        in_specs=[pl.BlockSpec(memory_space=pl.ANY)] * 8,
+        out_specs=pl.BlockSpec(memory_space=pl.ANY),
+        scratch_shapes=[
+            pieces,
+            pieces,
+            pieces,
+            pltpu.VMEM((features, far), jnp.float32),
+            pltpu.VMEM(top.shape, jnp.float32),
+            pltpu.VMEM(top.shape, jnp.float32),
+            pltpu.VMEM((heads, far, 2 * HEAD_SIZE), jnp.bfloat16),
+            pltpu.VMEM((heads, HEAD_SIZE + 16, far), jnp.bfloat16),
+            pieces,
+            pltpu.SemaphoreType.DMA((6, max(heads, 2))),
+        ],
+        input_output_aliases={7: 0},
+        cost_estimate=pl.CostEstimate(
+            flops=3 * features * far**2,
+            bytes_accessed=14 * features * far,
+            transcendentals=heads * far**2,
+        ),
+        name="attend_last",
+        compiler_params=pltpu.CompilerParams(vmem_limit_bytes=VMEM_GRANT),
+    )(queries, prior, cache_keys, cache_values, part, top, mass, early)
 
 
 def anywhere(count):
@@ -391,9 +588,9 @@
 def stage_body(key_ref, value_ref, rate_ref, target_ref, *refs):
     end_refs, (held_ref, values_ref, made_ref, sem, sem_end) = refs[:-5], refs[-5:]
     features, tokens = key_ref.shape
-    rows, window = end_refs[0].shape[1:]
+    width = end_refs[0].shape[2]
     step = HEAD_SIZE
-    last = slice(tokens - window, tokens)
+    lasts = [slice(tokens - (part + 1) * width, tokens - part * width) for part in range(len(end_refs))]
     begin = pl.multiple_of(lax.axis_index("narrow") * tokens, tokens)
     rates = -rate_ref[pl.ds(lax.axis_index("wide"), 1), pl.ds(begin, tokens)]
     values = [
@@ -404,9 +601,9 @@
     ]
     keys = [
         pltpu.make_async_copy(
-            key_ref.at[part * rows : (part + 1) * rows, last], held_ref.at[part], sem_end.at[0, part]
-        )
-        for part in range(len(end_refs))
+            key_ref.at[:, last], held_ref.at[part], sem_end.at[0, part]
+        )
+        for part, last in enumerate(lasts)
     ]
     for copy in values + keys:
         copy.start()
@@ -422,9 +619,7 @@
         made_ref[at] = (values_ref[at].astype(jnp.float32) * rates).astype(jnp.bfloat16)
         leave(made_ref.at[at], target_ref.at[at], sem.at[1, place])
     for part, end_ref in enumerate(end_refs):
-        leave(
-            values_ref.at[part * rows : (part + 1) * rows, last], end_ref.at[1], sem_end.at[1, part]
-        )
+        leave(values_ref.at[:, lasts[part]], end_ref.at[1], sem_end.at[1, part])
         keys[part].wait()
         leave(held_ref.at[part], end_ref.at[0], sem_end.at[2, part])
     for copy in leaving:
@@ -433,15 +628,15 @@
 
 def stage(keys, values, rates, parts):
     features, tokens = keys.shape
-    rows = features // parts
+    width = WINDOW // parts
     return pl.pallas_call(
         stage_body,
         out_shape=(jax.ShapeDtypeStruct((features, tokens), jnp.bfloat16),)
-        + (jax.ShapeDtypeStruct((2, rows, WINDOW), jnp.bfloat16),) * parts,
+        + (jax.ShapeDtypeStruct((2, features, width), jnp.bfloat16),) * parts,
         in_specs=anywhere(2) + [pl.BlockSpec(memory_space=pltpu.VMEM)],
         out_specs=tuple(anywhere(1 + parts)),
         scratch_shapes=[
-            pltpu.VMEM((parts, rows, WINDOW), jnp.bfloat16),
+            pltpu.VMEM((parts, features, width), jnp.bfloat16),
             pltpu.VMEM((features, tokens), jnp.bfloat16),
             pltpu.VMEM((features, tokens), jnp.bfloat16),
             pltpu.SemaphoreType.DMA((2, features // HEAD_SIZE)),
@@ -769,10 +964,10 @@
     pair_pack = swapped(pack, "narrow", 0)
     pair_near = swapped(near, "narrow", 0)
     pair_far = swapped(far, "narrow", 0)
-    for part, before in enumerate(prior):
-        attended = attend_early(
-            query_states, key_states, value_states, before, cache_keys, cache_values, attended, part
-        )
+    attended, *state = attend_early(
+        query_states, key_states, value_states, prior[0], cache_keys, cache_values, attended
+    )
+    attended = attend_last(query_states, prior[1], cache_keys, cache_values, *state, attended)
     recalled = fast_recall((near, pair_near, far, pair_far), (pack, pair_pack), query_states)
     return (attended, recalled)
 

time: 105 us -> 103 us (0.981)
  waiting for transfers between devices: 35.5 us -> 32.6 us
  Pallas kernels: 53.8 us -> 55.1 us
    ppermute x2, waiting for transfers between devices: 15.9 us -> 12.9 us  [from_behind(): lax.ppermute(value, axis, [(source, source + steps) for source in range(i...]
    pallas_call x2, Pallas kernels: 12.4 us -> 13.7 us  [the longest x1 9.2 us: attend_early(): pl.pallas_call(functools.partial(early_body, block=min(256, near)), out_s...]
  transfers between devices with their start and end apart: 11 -> 11, of which waited for: 4 -> 4; matrix products, arithmetic and copies ran while one was open for 0% -> 0% of each run, Pallas kernels for 27% -> 29%
where the time goes in v7:
time: 103 us
  Pallas kernels  55.1 us (53%)
  waiting for transfers between devices  32.6 us (32%)
  starting transfers between devices  14.4 us (14%)
    ppermute x6, waiting for transfers between devices, swapped(): lax.ppermute(array, axis, [(i, i ^ 1 << distance) for i in range(lax.axis...  14.3 us
    ppermute x2, waiting for transfers between devices, from_behind(): lax.ppermute(value, axis, [(source, source + steps) for source in range(i...  12.9 us
    pallas_call x1, Pallas kernels, fast_recall(): pl.pallas_call(recall_body, out_shape=jax.ShapeDtypeStruct((features, tok...  12.8 us
    pallas_call x1, Pallas kernels, fast_sums(): pl.pallas_call(functools.partial(sums_body, owned=owned, block=block), ou...  12.2 us
    pallas_call x1, Pallas kernels, attend_late(): pl.pallas_call(functools.partial(attend_body, block=min(256, WINDOW), win...  9.69 us
    pallas_call x1, Pallas kernels, attend_early(): pl.pallas_call(functools.partial(early_body, block=min(256, near)), out_s...  9.2 us
    ppermute x3, starting transfers between devices, from_owner(): return lax.ppermute(value, ('wide', 'narrow'), pairs)  7.28 us
    ppermute x2, starting transfers between devices, from_behind(): lax.ppermute(value, axis, [(source, source + steps) for source in range(i...  5.82 us
  transfers between devices with their start and end apart: 11, of which 4 were waited for; matrix products, arithmetic and copies ran while one was open for 0% of the time, Pallas kernels for 29%

profile of v7, /device:TPU:20, one launch (start us, length us, event | category | flops | bytes accessed | tf_op | source)
XLA Modules:
  0.0 103.0 jit_solution(10964017989046127714)
XLA Ops:
  0.6 0.1 collective-permute-start.5
  0.7 4.2 %stage.1 = (bf16[512,2048]{1,0:T(8,128)(2,1)}, bf16[2,512,512]{2,1,0:T(8,128)(2,1)}, bf16[2,512,512]{2,1,0:T(8,128)(2,1)}) custom-call(bf16[512,2048]{1,0:T(8,128)(2,1)} %refs_4_.1, bf16[512,2048]{1,0:T(8,128)(2,1)} %vc_ref.3, f32[8,8192]{1,0:T(8,128)} %rate_ref.1), custom_call_target="tpu_custom_call" | custom-call | flops 1048576 | bytes 8388608 | tf_op jit(solution)/shard_map/stage/pallas_call | solution.py:632
  4.9 0.6 collective-permute-start.6
  5.5 2.5 %prepare.1 = (bf16[3,256,512]{2,1,0:T(8,128)(2,1)}, bf16[3,256,512]{2,1,0:T(8,128)(2,1)}) custom-call(bf16[2,512,512]{2,1,0:T(8,128)(2,1)} %gate_ref.1, bf16[2,512,512]{2,1,0:T(8,128)(2,1)} %lift_ref.1, bf16[2,512,512]{2,1,0:T(8,128)(2,1)} %down_ref.1), custom_call_target="tpu_custom_call" | custom-call | bytes 3145728 | tf_op jit(solution)/shard_map/prepare/pallas_call | solution.py:570
  8.0 2.9 %collective-permute-start = (bf16[3,256,512]{2,1,0:T(8,128)(2,1)}, bf16[3,256,512]{2,1,0:T(8,128)(2,1)}, u32[]{:S(2)}, u32[]{:S(2)}) collective-permute-start(bf16[3,256,512]{2,1,0:T(8,128)(2,1)} %get-tuple-element.21), channel_id=1, source_target_pairs={{0,1},{4,5},{9,8},{13,12},{18,19},{22,23},{27,26},{31,30}} | collective-permute-start | bytes 2359304 | tf_op jit(solution)/shard_map/ppermute | solution.py:942
  10.9 2.2 %collective-permute-start.1 = (bf16[3,256,512]{2,1,0:T(8,128)(2,1)}, bf16[3,256,512]{2,1,0:T(8,128)(2,1)}, u32[]{:S(2)}, u32[]{:S(2)}) collective-permute-start(bf16[3,256,512]{2,1,0:T(8,128)(2,1)} %get-tuple-element.31.refs_0_), channel_id=1, source_target_pairs={{0,2},{4,6},{9,11},{13,15},{18,16},{22,20},{27,25},{31,29}} | collective-permute-start | bytes 2359304 | tf_op jit(solution)/shard_map/ppermute | solution.py:942
  13.1 2.2 %collective-permute-start.2 = (bf16[3,256,512]{2,1,0:T(8,128)(2,1)}, bf16[3,256,512]{2,1,0:T(8,128)(2,1)}, u32[]{:S(2)}, u32[]{:S(2)}) collective-permute-start(bf16[3,256,512]{2,1,0:T(8,128)(2,1)} %get-tuple-element.21), channel_id=1, source_target_pairs={{0,3},{4,7},{9,10},{13,14},{18,17},{22,21},{27,24},{31,28}} | collective-permute-start | bytes 2359304 | tf_op jit(solution)/shard_map/ppermute | solution.py:942
  15.3 9.7 %attend_late.1._ = bf16[512,2048]{1,0:T(8,128)(2,1)} custom-call(bf16[512,2048]{1,0:T(8,128)(2,1)} %query_ref.1, bf16[512,2048]{1,0:T(8,128)(2,1)} %refs_4_.1, bf16[512,2048]{1,0:T(8,128)(2,1)} %vc_ref.3, bf16[512,2048]{1,0:T(8,128)(2,1)} %refs_4_.1, bf16[512,2048]{1,0:T(8,128)(2,1)} %vc_ref.3), custom_call_target="tpu_custom_call" | custom-call | flops 2684354560 | bytes 5242880 | tf_op jit(solution)/shard_map/attend_late/pallas_call | solution.py:269
  25.0 0.0 collective-permute-done.refs_1_
  25.0 0.0 collective-permute-done.1.refs_2_
  25.0 5.5 %collective-permute-done.2.refs_3_ = bf16[3,256,512]{2,1,0:T(8,128)(2,1)} collective-permute-done((bf16[3,256,512]{2,1,0:T(8,128)(2,1)}, bf16[3,256,512]{2,1,0:T(8,128)(2,1)}, u32[]{:S(2)}, u32[]{:S(2)}) %collective-permute-start.2) | collective-permute-done | bytes 786464 | tf_op jit(solution)/shard_map/ppermute | solution.py:942
  30.4 0.0 collective-permute-done.5.refs_6_
  30.4 0.0 collective-permute-done.6.refs_7_
  30.4 12.2 %fast_sums.1 = (bf16[3,256,512]{2,1,0:T(8,128)(2,1)}, bf16[3,256,512]{2,1,0:T(8,128)(2,1)}) custom-call(bf16[3,256,512]{2,1,0:T(8,128)(2,1)} %get-tuple-element.31.refs_0_, bf16[3,256,512]{2,1,0:T(8,128)(2,1)} %collective-permute-done.refs_1_, bf16[3,256,512]{2,1,0:T(8,128)(2,1)} %collective-permute-done.1.refs_2_, ...), custom_call_target="tpu_custom_call" | custom-call | flops 6442450944 | bytes 10747904 | tf_op jit(solution)/shard_map/fast_sums/pallas_call | solution.py:742
  42.7 0.1 collective-permute-start.8
  42.8 3.9 %collective-permute-start.4 = (bf16[2,512,512]{2,1,0:T(8,128)(2,1)}, bf16[2,512,512]{2,1,0:T(8,128)(2,1)}, u32[]{:S(2)}, u32[]{:S(2)}) collective-permute-start(bf16[2,512,512]{2,1,0:T(8,128)(2,1)} %get-tuple-element.25), channel_id=1, source_target_pairs={{0,1},{1,2},{2,3},{4,5},{5,6},{6,7},{8,9},{9,10},{10,11},{12,13},{... | collective-permute-start | bytes 3145736 | tf_op jit(solution)/shard_map/ppermute | solution.py:41
  46.7 1.9 %collective-permute-start.3 = (bf16[2,512,512]{2,1,0:T(8,128)(2,1)}, bf16[2,512,512]{2,1,0:T(8,128)(2,1)}, u32[]{:S(2)}, u32[]{:S(2)}) collective-permute-start(bf16[2,512,512]{2,1,0:T(8,128)(2,1)} %get-tuple-element.24), channel_id=1, source_target_pairs={{0,1},{1,2},{2,3},{4,5},{5,6},{6,7},{8,9},{9,10},{10,11},{12,13},{... | collective-permute-start | bytes 3145736 | tf_op jit(solution)/shard_map/ppermute | solution.py:41
  48.6 0.1 collective-permute-start.7
  48.7 0.5 collective-permute-start.10
  49.2 14.3 %collective-permute-done.8.far_ref = bf16[3,256,512]{2,1,0:T(8,128)(2,1)} collective-permute-done((bf16[3,256,512]{2,1,0:T(8,128)(2,1)}, bf16[3,256,512]{2,1,0:T(8,128)(2,1)}, u32[]{:S(2)}, u32[]{:S(2)}) %collective-permute-start.8) | collective-permute-done | bytes 786464 | tf_op jit(solution)/shard_map/ppermute | solution.py:27
  63.5 0.0 collective-permute-start.9
  63.5 10.8 %collective-permute-done.4.kp_ref.vp_ref = bf16[2,512,512]{2,1,0:T(8,128)(2,1)} collective-permute-done((bf16[2,512,512]{2,1,0:T(8,128)(2,1)}, bf16[2,512,512]{2,1,0:T(8,128)(2,1)}, u32[]{:S(2)}, u32[]{:S(2)}) %collective-permute-start.4) | collective-permute-done | bytes 1048608 | tf_op jit(solution)/shard_map/ppermute | solution.py:41
  74.3 9.2 %attend_early.1 = (bf16[512,2048]{1,0:T(8,128)(2,1)}, f32[512,512]{1,0:T(8,128)}, f32[32,512]{1,0:T(8,128)}, f32[32,512]{1,0:T(8,128)}) custom-call(bf16[512,2048]{1,0:T(8,128)(2,1)} %query_ref.1, bf16[2,512,512]{2,1,0:T(8,128)(2,1)} %collective-permute-done.4.kp_ref.vp_ref, ...), custom_call_target="tpu_custom_call", output_to_operand_aliasing={{0}: (7, {})} | custom-call | flops 2684354560 | bytes 7340032 | tf_op jit(solution)/shard_map/attend_early/pallas_call | solution.py:378
  83.5 2.0 %collective-permute-done.3.prior_ref = bf16[2,512,512]{2,1,0:T(8,128)(2,1)} collective-permute-done((bf16[2,512,512]{2,1,0:T(8,128)(2,1)}, bf16[2,512,512]{2,1,0:T(8,128)(2,1)}, u32[]{:S(2)}, u32[]{:S(2)}) %collective-permute-start.3) | collective-permute-done | bytes 1048608 | tf_op jit(solution)/shard_map/ppermute | solution.py:41
  85.5 4.5 %attend_last.1 = bf16[512,2048]{1,0:T(8,128)(2,1)} custom-call(bf16[512,2048]{1,0:T(8,128)(2,1)} %query_ref.1, bf16[2,512,512]{2,1,0:T(8,128)(2,1)} %collective-permute-done.3.prior_ref, bf16[512,1024]{1,0:T(8,128)(2,1)} %ck_ref.3, bf16[512,1024]{1,0:T(8,128)(2,1)} %cv_ref.3, f32[512,512]{1,0:T(8,128)} %get-tuple-element.27.part_ref, ...), custom_call_target="tpu_custom_call", output_to_operand_aliasing={{}: (7, {})} | custom-call | flops 402653184 | bytes 3670016 | tf_op jit(solution)/shard_map/attend_last/pallas_call | solution.py:503
  90.0 0.0 collective-permute-done.7.other_ref
  90.0 0.0 collective-permute-done.10.pair_pack_ref
  90.0 0.0 collective-permute-done.9.other_far_ref
  90.1 12.8 %fast_recall.1 = bf16[512,2048]{1,0:T(8,128)(2,1)} custom-call(bf16[3,256,512]{2,1,0:T(8,128)(2,1)} %get-tuple-element.36.mine_ref, bf16[3,256,512]{2,1,0:T(8,128)(2,1)} %collective-permute-done.7.other_ref, bf16[3,256,512]{2,1,0:T(8,128)(2,1)} %collective-permute-done.8.far_ref, bf16[3,256,512]{2,1,0:T(8,128)(2,1)} %collective-permute-done.9.other_far_ref, ...), custom_call_target="tpu_custom_call" | custom-call | flops 8053063680 | bytes 7340032 | tf_op jit(solution)/shard_map/fast_recall/pallas_call | solution.py:884
Async XLA Ops:
  0.6 29.8 %collective-permute-start.5 = (bf16[512,2048]{1,0:T(8,128)(2,1)}, bf16[512,2048]{1,0:T(8,128)(2,1)}, u32[]{:S(2)}, u32[]{:S(2)}) collective-permute-start(bf16[512,2048]{1,0:T(8,128)(2,1)} %refs_4_.1), channel_id=1, source_target_pairs={{0,1},{1,0},{2,3},{3,2},{4,5},{5,4},{6,7},{7,6},{8,9},{9,8},{10,11... | collective-permute-start | bytes 6291464 | tf_op jit(solution)/shard_map/ppermute | solution.py:27
  4.9 25.5 %collective-permute-start.6 = (bf16[512,2048]{1,0:T(8,128)(2,1)}, bf16[512,2048]{1,0:T(8,128)(2,1)}, u32[]{:S(2)}, u32[]{:S(2)}) collective-permute-start(bf16[512,2048]{1,0:T(8,128)(2,1)} %get-tuple-element.35.refs_5_), channel_id=1, source_target_pairs={{0,1},{1,0},{2,3},{3,2},{4,5},{5,4},{6,7},{7,6},{8,9},{9,8},{10,11... | collective-permute-start | bytes 6291464 | tf_op jit(solution)/shard_map/ppermute | solution.py:27
  8.0 17.0 %collective-permute-start = (bf16[3,256,512]{2,1,0:T(8,128)(2,1)}, bf16[3,256,512]{2,1,0:T(8,128)(2,1)}, u32[]{:S(2)}, u32[]{:S(2)}) collective-permute-start(bf16[3,256,512]{2,1,0:T(8,128)(2,1)} %get-tuple-element.21), channel_id=1, source_target_pairs={{0,1},{4,5},{9,8},{13,12},{18,19},{22,23},{27,26},{31,30}} | collective-permute-start | bytes 2359304 | tf_op jit(solution)/shard_map/ppermute | solution.py:942
  10.9 14.1 %collective-permute-start.1 = (bf16[3,256,512]{2,1,0:T(8,128)(2,1)}, bf16[3,256,512]{2,1,0:T(8,128)(2,1)}, u32[]{:S(2)}, u32[]{:S(2)}) collective-permute-start(bf16[3,256,512]{2,1,0:T(8,128)(2,1)} %get-tuple-element.31.refs_0_), channel_id=1, source_target_pairs={{0,2},{4,6},{9,11},{13,15},{18,16},{22,20},{27,25},{31,29}} | collective-permute-start | bytes 2359304 | tf_op jit(solution)/shard_map/ppermute | solution.py:942
  13.1 17.3 %collective-permute-start.2 = (bf16[3,256,512]{2,1,0:T(8,128)(2,1)}, bf16[3,256,512]{2,1,0:T(8,128)(2,1)}, u32[]{:S(2)}, u32[]{:S(2)}) collective-permute-start(bf16[3,256,512]{2,1,0:T(8,128)(2,1)} %get-tuple-element.21), channel_id=1, source_target_pairs={{0,3},{4,7},{9,10},{13,14},{18,17},{22,21},{27,24},{31,28}} | collective-permute-start | bytes 2359304 | tf_op jit(solution)/shard_map/ppermute | solution.py:942
  42.7 20.8 %collective-permute-start.8 = (bf16[3,256,512]{2,1,0:T(8,128)(2,1)}, bf16[3,256,512]{2,1,0:T(8,128)(2,1)}, u32[]{:S(2)}, u32[]{:S(2)}) collective-permute-start(bf16[3,256,512]{2,1,0:T(8,128)(2,1)} %get-tuple-element.36.mine_ref), channel_id=1, source_target_pairs={{0,2},{1,3},{2,0},{3,1},{4,6},{5,7},{6,4},{7,5},{8,10},{9,11},{10,... | collective-permute-start | bytes 2359304 | tf_op jit(solution)/shard_map/ppermute | solution.py:27
  42.8 31.5 %collective-permute-start.4 = (bf16[2,512,512]{2,1,0:T(8,128)(2,1)}, bf16[2,512,512]{2,1,0:T(8,128)(2,1)}, u32[]{:S(2)}, u32[]{:S(2)}) collective-permute-start(bf16[2,512,512]{2,1,0:T(8,128)(2,1)} %get-tuple-element.25), channel_id=1, source_target_pairs={{0,1},{1,2},{2,3},{4,5},{5,6},{6,7},{8,9},{9,10},{10,11},{12,13},{... | collective-permute-start | bytes 3145736 | tf_op jit(solution)/shard_map/ppermute | solution.py:41
  46.7 38.9 %collective-permute-start.3 = (bf16[2,512,512]{2,1,0:T(8,128)(2,1)}, bf16[2,512,512]{2,1,0:T(8,128)(2,1)}, u32[]{:S(2)}, u32[]{:S(2)}) collective-permute-start(bf16[2,512,512]{2,1,0:T(8,128)(2,1)} %get-tuple-element.24), channel_id=1, source_target_pairs={{0,1},{1,2},{2,3},{4,5},{5,6},{6,7},{8,9},{9,10},{10,11},{12,13},{... | collective-permute-start | bytes 3145736 | tf_op jit(solution)/shard_map/ppermute | solution.py:41
  48.6 41.4 %collective-permute-start.7 = (bf16[3,256,512]{2,1,0:T(8,128)(2,1)}, bf16[3,256,512]{2,1,0:T(8,128)(2,1)}, u32[]{:S(2)}, u32[]{:S(2)}) collective-permute-start(bf16[3,256,512]{2,1,0:T(8,128)(2,1)} %get-tuple-element.36.mine_ref), channel_id=1, source_target_pairs={{0,1},{1,0},{2,3},{3,2},{4,5},{5,4},{6,7},{7,6},{8,9},{9,8},{10,11... | collective-permute-start | bytes 2359304 | tf_op jit(solution)/shard_map/ppermute | solution.py:27
  48.7 41.4 %collective-permute-start.10 = (bf16[3,256,512]{2,1,0:T(8,128)(2,1)}, bf16[3,256,512]{2,1,0:T(8,128)(2,1)}, u32[]{:S(2)}, u32[]{:S(2)}) collective-permute-start(bf16[3,256,512]{2,1,0:T(8,128)(2,1)} %get-tuple-element.37.pack_ref), channel_id=1, source_target_pairs={{0,1},{1,0},{2,3},{3,2},{4,5},{5,4},{6,7},{7,6},{8,9},{9,8},{10,11... | collective-permute-start | bytes 2359304 | tf_op jit(solution)/shard_map/ppermute | solution.py:27
  63.5 26.6 %collective-permute-start.9 = (bf16[3,256,512]{2,1,0:T(8,128)(2,1)}, bf16[3,256,512]{2,1,0:T(8,128)(2,1)}, u32[]{:S(2)}, u32[]{:S(2)}) collective-permute-start(bf16[3,256,512]{2,1,0:T(8,128)(2,1)} %collective-permute-done.8.far_ref), channel_id=1, source_target_pairs={{0,1},{1,0},{2,3},{3,2},{4,5},{5,4},{6,7},{7,6},{8,9},{9,8},{10,11... | collective-permute-start | bytes 2359304 | tf_op jit(solution)/shard_map/ppermute | solution.py:27

commit v8 on v7

--- a/solution.py
+++ b/solution.py
@@ -652,7 +652,7 @@
     )(keys, values, rates)
 
 
-def sums_body(*refs, owned, block):
+def sums_body(*refs, owned, cuts):
     sources = refs[:-15]
     (
         key_ref, target_ref, pair_key_ref, pair_target_ref,
@@ -661,46 +661,39 @@
     ) = refs[-15:]
     _, tokens = key_ref.shape
     half = pack_ref.shape[1]
-    count = tokens // block
     role = lax.axis_index("narrow") ^ (lax.axis_index("wide") // owned)
 
-    def moved(keys, targets, index, slot):
-        source = slice(index * block, (index + 1) * block)
-        place = slice(slot * block, (slot + 1) * block)
-        return (
+    for place, source in enumerate(sources):
+
+        @pl.when(role == place)
+        def _(source=source):
+            pltpu.make_async_copy(source, pack_ref, sem).start()
+
+    spans = [(key_ref, target_ref, 0, begin, end) for begin, end in zip(cuts, cuts[1:])]
+    spans.append((pair_key_ref, pair_target_ref, tokens, 0, tokens))
+    arrivals = []
+    for slot, (keys, targets, base, begin, end) in enumerate(spans):
+        source, place = slice(begin, end), slice(base + begin, base + end)
+        copies = (
             pltpu.make_async_copy(keys.at[:, source], keys_ref.at[:, place], sem_in.at[0, slot]),
             pltpu.make_async_copy(
                 targets.at[:, source], targets_ref.at[:, place], sem_in.at[1, slot]
             ),
         )
-
-    for place, source in enumerate(sources):
-
-        @pl.when(role == place)
-        def _(source=source):
-            pltpu.make_async_copy(source, pack_ref, sem).start()
-
-    arrivals = [moved(key_ref, target_ref, index, index) for index in range(count)]
-    arrivals += [moved(pair_key_ref, pair_target_ref, index, count + index) for index in range(count)]
-    for copies in arrivals:
         for copy in copies:
             copy.start()
+        arrivals.append((place, *copies))
     pltpu.make_async_copy(sources[0], pack_ref, sem).wait()
     leaving = [pltpu.make_async_copy(pack_ref, pack_out, sem_out.at[3])]
     leaving[0].start()
     gate_lift = jnp.concatenate([pack_ref[0] * jnp.bfloat16(0.5), pack_ref[1]], axis=0)
     down = pack_ref[2]
 
-    def multiply(slot):
-        for copy in arrivals[slot]:
-            copy.wait()
-        at = slice(slot * block, (slot + 1) * block)
+    for at, keys, targets in arrivals:
+        keys.wait()
         pre = jnp.dot(gate_lift, keys_ref[:, at], preferred_element_type=jnp.float32)
+        targets.wait()
         back_hidden = jnp.dot(down, targets_ref[:, at], preferred_element_type=jnp.float32)
-        return pre, back_hidden
-
-    def combine(slot, pre, back_hidden):
-        at = slice(slot * block, (slot + 1) * block)
         half_gate = pre[:half]
         pre_lift = pre[half:]
         twice = jnp.tanh(half_gate) + 1.0
@@ -710,9 +703,6 @@
         back_ref[:half, at] = (back_hidden * pre_lift * slope).astype(jnp.bfloat16)
         back_ref[half:, at] = (back_hidden * silu_gate).astype(jnp.bfloat16)
 
-    for slot in range(2 * count):
-        combine(slot, *multiply(slot))
-
     def leave(place, value):
         send_ref[place] = value.astype(jnp.bfloat16)
         leaving.append(
@@ -738,9 +728,9 @@
     features, tokens = keys.shape
     shape = sources[0].shape
     half = shape[1]
-    block = tokens
+    cuts = (0, tokens)
     return pl.pallas_call(
-        functools.partial(sums_body, owned=owned, block=block),
+        functools.partial(sums_body, owned=owned, cuts=cuts),
         out_shape=(jax.ShapeDtypeStruct(shape, jnp.bfloat16),) * 2,
         in_specs=anywhere(len(sources) + 4),
         out_specs=tuple(anywhere(2)),
@@ -752,7 +742,7 @@
             pltpu.VMEM((half, 2 * tokens), jnp.bfloat16),
             pltpu.VMEM((2 * half, 2 * tokens), jnp.bfloat16),
             pltpu.SemaphoreType.DMA(()),
-            pltpu.SemaphoreType.DMA((2, 2 * tokens // block)),
+            pltpu.SemaphoreType.DMA((2, len(cuts))),
             pltpu.SemaphoreType.DMA((4,)),
         ],
         cost_estimate=pl.CostEstimate(
@@ -951,7 +941,8 @@
     pair_targets = swapped(targets, "narrow", 0)
     attended = attend_late(query_states, key_states, value_states)
     sources = [own] + [arrivals[step] for step in range(1, narrow_count)]
-    sources, attended, ends = lax.optimization_barrier((sources, attended, ends))
+    attended, ends = lax.optimization_barrier((attended, ends))
+    sources, attended = lax.optimization_barrier((sources, attended))
     prior = []
     for end in ends:
         prior.append(from_behind(end, "narrow", 1))

time: 103 us -> 103 us (level)
  no operation moved by 1% of the time
where the time goes in v8:
time: 103 us
  Pallas kernels  55 us (53%)
  waiting for transfers between devices  32.6 us (32%)
  starting transfers between devices  14.4 us (14%)
    ppermute x6, waiting for transfers between devices, swapped(): lax.ppermute(array, axis, [(i, i ^ 1 << distance) for i in range(lax.axis...  14.3 us
    ppermute x2, waiting for transfers between devices, from_behind(): lax.ppermute(value, axis, [(source, source + steps) for source in range(i...  12.9 us
    pallas_call x1, Pallas kernels, fast_recall(): pl.pallas_call(recall_body, out_shape=jax.ShapeDtypeStruct((features, tok...  12.8 us
    pallas_call x1, Pallas kernels, fast_sums(): pl.pallas_call(functools.partial(sums_body, owned=owned, cuts=cuts), out_...  12.2 us
    pallas_call x1, Pallas kernels, attend_late(): pl.pallas_call(functools.partial(attend_body, block=min(256, WINDOW), win...  9.69 us
    pallas_call x1, Pallas kernels, attend_early(): pl.pallas_call(functools.partial(early_body, block=min(256, near)), out_s...  9.2 us
    ppermute x3, starting transfers between devices, from_owner(): return lax.ppermute(value, ('wide', 'narrow'), pairs)  7.28 us
    ppermute x2, starting transfers between devices, from_behind(): lax.ppermute(value, axis, [(source, source + steps) for source in range(i...  5.83 us
  transfers between devices with their start and end apart: 11, of which 4 were waited for; matrix products, arithmetic and copies ran while one was open for 0% of the time, Pallas kernels for 29%

profile of v8, /device:TPU:20, one launch (start us, length us, event | category | flops | bytes accessed | tf_op | source)
XLA Modules:
  0.0 103.0 jit_solution(929836803844073773)
XLA Ops:
  0.6 0.1 collective-permute-start.5
  0.7 4.2 %stage.1 = (bf16[512,2048]{1,0:T(8,128)(2,1)}, bf16[2,512,512]{2,1,0:T(8,128)(2,1)}, bf16[2,512,512]{2,1,0:T(8,128)(2,1)}) custom-call(bf16[512,2048]{1,0:T(8,128)(2,1)} %refs_4_.1, bf16[512,2048]{1,0:T(8,128)(2,1)} %vc_ref.3, f32[8,8192]{1,0:T(8,128)} %rate_ref.1), custom_call_target="tpu_custom_call" | custom-call | flops 1048576 | bytes 8388608 | tf_op jit(solution)/shard_map/stage/pallas_call | solution.py:632
  4.9 0.6 collective-permute-start.6
  5.5 2.5 %prepare.1 = (bf16[3,256,512]{2,1,0:T(8,128)(2,1)}, bf16[3,256,512]{2,1,0:T(8,128)(2,1)}) custom-call(bf16[2,512,512]{2,1,0:T(8,128)(2,1)} %gate_ref.1, bf16[2,512,512]{2,1,0:T(8,128)(2,1)} %lift_ref.1, bf16[2,512,512]{2,1,0:T(8,128)(2,1)} %down_ref.1), custom_call_target="tpu_custom_call" | custom-call | bytes 3145728 | tf_op jit(solution)/shard_map/prepare/pallas_call | solution.py:570
  8.0 2.9 %collective-permute-start.2 = (bf16[3,256,512]{2,1,0:T(8,128)(2,1)}, bf16[3,256,512]{2,1,0:T(8,128)(2,1)}, u32[]{:S(2)}, u32[]{:S(2)}) collective-permute-start(bf16[3,256,512]{2,1,0:T(8,128)(2,1)} %get-tuple-element.26), channel_id=1, source_target_pairs={{0,1},{4,5},{9,8},{13,12},{18,19},{22,23},{27,26},{31,30}} | collective-permute-start | bytes 2359304 | tf_op jit(solution)/shard_map/ppermute | solution.py:932
  10.9 2.2 %collective-permute-start.3 = (bf16[3,256,512]{2,1,0:T(8,128)(2,1)}, bf16[3,256,512]{2,1,0:T(8,128)(2,1)}, u32[]{:S(2)}, u32[]{:S(2)}) collective-permute-start(bf16[3,256,512]{2,1,0:T(8,128)(2,1)} %get-tuple-element.33.refs_0_), channel_id=1, source_target_pairs={{0,2},{4,6},{9,11},{13,15},{18,16},{22,20},{27,25},{31,29}} | collective-permute-start | bytes 2359304 | tf_op jit(solution)/shard_map/ppermute | solution.py:932
  13.1 2.2 %collective-permute-start.4 = (bf16[3,256,512]{2,1,0:T(8,128)(2,1)}, bf16[3,256,512]{2,1,0:T(8,128)(2,1)}, u32[]{:S(2)}, u32[]{:S(2)}) collective-permute-start(bf16[3,256,512]{2,1,0:T(8,128)(2,1)} %get-tuple-element.26), channel_id=1, source_target_pairs={{0,3},{4,7},{9,10},{13,14},{18,17},{22,21},{27,24},{31,28}} | collective-permute-start | bytes 2359304 | tf_op jit(solution)/shard_map/ppermute | solution.py:932
  15.3 9.7 %attend_late.1._ = bf16[512,2048]{1,0:T(8,128)(2,1)} custom-call(bf16[512,2048]{1,0:T(8,128)(2,1)} %query_ref.1, bf16[512,2048]{1,0:T(8,128)(2,1)} %refs_4_.1, bf16[512,2048]{1,0:T(8,128)(2,1)} %vc_ref.3, bf16[512,2048]{1,0:T(8,128)(2,1)} %refs_4_.1, bf16[512,2048]{1,0:T(8,128)(2,1)} %vc_ref.3), custom_call_target="tpu_custom_call" | custom-call | flops 2684354560 | bytes 5242880 | tf_op jit(solution)/shard_map/attend_late/pallas_call | solution.py:269
  25.0 0.0 collective-permute-done.2.refs_1_
  25.0 0.0 collective-permute-done.3.refs_2_
  25.0 5.5 %collective-permute-done.4.refs_3_ = bf16[3,256,512]{2,1,0:T(8,128)(2,1)} collective-permute-done((bf16[3,256,512]{2,1,0:T(8,128)(2,1)}, bf16[3,256,512]{2,1,0:T(8,128)(2,1)}, u32[]{:S(2)}, u32[]{:S(2)}) %collective-permute-start.4) | collective-permute-done | bytes 786464 | tf_op jit(solution)/shard_map/ppermute | solution.py:932
  30.4 0.0 collective-permute-done.5.refs_6_
  30.4 0.0 collective-permute-done.6.refs_7_
  30.4 12.2 %fast_sums.1 = (bf16[3,256,512]{2,1,0:T(8,128)(2,1)}, bf16[3,256,512]{2,1,0:T(8,128)(2,1)}) custom-call(bf16[3,256,512]{2,1,0:T(8,128)(2,1)} %get-tuple-element.33.refs_0_, bf16[3,256,512]{2,1,0:T(8,128)(2,1)} %collective-permute-done.2.refs_1_, bf16[3,256,512]{2,1,0:T(8,128)(2,1)} %collective-permute-done.3.refs_2_, ...), custom_call_target="tpu_custom_call" | custom-call | flops 6442450944 | bytes 10747904 | tf_op jit(solution)/shard_map/fast_sums/pallas_call | solution.py:732
  42.6 0.1 collective-permute-start.8
  42.7 3.9 %collective-permute-start.1 = (bf16[2,512,512]{2,1,0:T(8,128)(2,1)}, bf16[2,512,512]{2,1,0:T(8,128)(2,1)}, u32[]{:S(2)}, u32[]{:S(2)}) collective-permute-start(bf16[2,512,512]{2,1,0:T(8,128)(2,1)} %get-tuple-element.24), channel_id=1, source_target_pairs={{0,1},{1,2},{2,3},{4,5},{5,6},{6,7},{8,9},{9,10},{10,11},{12,13},{... | collective-permute-start | bytes 3145736 | tf_op jit(solution)/shard_map/ppermute | solution.py:41
  46.6 1.9 %collective-permute-start = (bf16[2,512,512]{2,1,0:T(8,128)(2,1)}, bf16[2,512,512]{2,1,0:T(8,128)(2,1)}, u32[]{:S(2)}, u32[]{:S(2)}) collective-permute-start(bf16[2,512,512]{2,1,0:T(8,128)(2,1)} %get-tuple-element.23), channel_id=1, source_target_pairs={{0,1},{1,2},{2,3},{4,5},{5,6},{6,7},{8,9},{9,10},{10,11},{12,13},{... | collective-permute-start | bytes 3145736 | tf_op jit(solution)/shard_map/ppermute | solution.py:41
  48.6 0.1 collective-permute-start.7
  48.6 0.5 collective-permute-start.10
  49.1 14.3 %collective-permute-done.8.far_ref = bf16[3,256,512]{2,1,0:T(8,128)(2,1)} collective-permute-done((bf16[3,256,512]{2,1,0:T(8,128)(2,1)}, bf16[3,256,512]{2,1,0:T(8,128)(2,1)}, u32[]{:S(2)}, u32[]{:S(2)}) %collective-permute-start.8) | collective-permute-done | bytes 786464 | tf_op jit(solution)/shard_map/ppermute | solution.py:27
  63.4 0.0 collective-permute-start.9
  63.4 10.8 %collective-permute-done.1.kp_ref.vp_ref = bf16[2,512,512]{2,1,0:T(8,128)(2,1)} collective-permute-done((bf16[2,512,512]{2,1,0:T(8,128)(2,1)}, bf16[2,512,512]{2,1,0:T(8,128)(2,1)}, u32[]{:S(2)}, u32[]{:S(2)}) %collective-permute-start.1) | collective-permute-done | bytes 1048608 | tf_op jit(solution)/shard_map/ppermute | solution.py:41
  74.3 9.2 %attend_early.1 = (bf16[512,2048]{1,0:T(8,128)(2,1)}, f32[512,512]{1,0:T(8,128)}, f32[32,512]{1,0:T(8,128)}, f32[32,512]{1,0:T(8,128)}) custom-call(bf16[512,2048]{1,0:T(8,128)(2,1)} %query_ref.1, bf16[2,512,512]{2,1,0:T(8,128)(2,1)} %collective-permute-done.1.kp_ref.vp_ref, ...), custom_call_target="tpu_custom_call", output_to_operand_aliasing={{0}: (7, {})} | custom-call | flops 2684354560 | bytes 7340032 | tf_op jit(solution)/shard_map/attend_early/pallas_call | solution.py:378
  83.5 2.0 %collective-permute-done.prior_ref = bf16[2,512,512]{2,1,0:T(8,128)(2,1)} collective-permute-done((bf16[2,512,512]{2,1,0:T(8,128)(2,1)}, bf16[2,512,512]{2,1,0:T(8,128)(2,1)}, u32[]{:S(2)}, u32[]{:S(2)}) %collective-permute-start) | collective-permute-done | bytes 1048608 | tf_op jit(solution)/shard_map/ppermute | solution.py:41
  85.5 4.5 %attend_last.1 = bf16[512,2048]{1,0:T(8,128)(2,1)} custom-call(bf16[512,2048]{1,0:T(8,128)(2,1)} %query_ref.1, bf16[2,512,512]{2,1,0:T(8,128)(2,1)} %collective-permute-done.prior_ref, bf16[512,1024]{1,0:T(8,128)(2,1)} %ck_ref.3, bf16[512,1024]{1,0:T(8,128)(2,1)} %cv_ref.3, f32[512,512]{1,0:T(8,128)} %get-tuple-element.29.part_ref, ...), custom_call_target="tpu_custom_call", output_to_operand_aliasing={{}: (7, {})} | custom-call | flops 402653184 | bytes 3670016 | tf_op jit(solution)/shard_map/attend_last/pallas_call | solution.py:503
  90.0 0.0 collective-permute-done.7.other_ref
  90.0 0.0 collective-permute-done.10.pair_pack_ref
  90.0 0.0 collective-permute-done.9.other_far_ref
  90.0 12.8 %fast_recall.1 = bf16[512,2048]{1,0:T(8,128)(2,1)} custom-call(bf16[3,256,512]{2,1,0:T(8,128)(2,1)} %get-tuple-element.38.mine_ref, bf16[3,256,512]{2,1,0:T(8,128)(2,1)} %collective-permute-done.7.other_ref, bf16[3,256,512]{2,1,0:T(8,128)(2,1)} %collective-permute-done.8.far_ref, bf16[3,256,512]{2,1,0:T(8,128)(2,1)} %collective-permute-done.9.other_far_ref, ...), custom_call_target="tpu_custom_call" | custom-call | flops 8053063680 | bytes 7340032 | tf_op jit(solution)/shard_map/fast_recall/pallas_call | solution.py:874
Async XLA Ops:
  0.6 29.8 %collective-permute-start.5 = (bf16[512,2048]{1,0:T(8,128)(2,1)}, bf16[512,2048]{1,0:T(8,128)(2,1)}, u32[]{:S(2)}, u32[]{:S(2)}) collective-permute-start(bf16[512,2048]{1,0:T(8,128)(2,1)} %refs_4_.1), channel_id=1, source_target_pairs={{0,1},{1,0},{2,3},{3,2},{4,5},{5,4},{6,7},{7,6},{8,9},{9,8},{10,11... | collective-permute-start | bytes 6291464 | tf_op jit(solution)/shard_map/ppermute | solution.py:27
  4.9 25.5 %collective-permute-start.6 = (bf16[512,2048]{1,0:T(8,128)(2,1)}, bf16[512,2048]{1,0:T(8,128)(2,1)}, u32[]{:S(2)}, u32[]{:S(2)}) collective-permute-start(bf16[512,2048]{1,0:T(8,128)(2,1)} %get-tuple-element.37.refs_5_), channel_id=1, source_target_pairs={{0,1},{1,0},{2,3},{3,2},{4,5},{5,4},{6,7},{7,6},{8,9},{9,8},{10,11... | collective-permute-start | bytes 6291464 | tf_op jit(solution)/shard_map/ppermute | solution.py:27
  8.0 17.0 %collective-permute-start.2 = (bf16[3,256,512]{2,1,0:T(8,128)(2,1)}, bf16[3,256,512]{2,1,0:T(8,128)(2,1)}, u32[]{:S(2)}, u32[]{:S(2)}) collective-permute-start(bf16[3,256,512]{2,1,0:T(8,128)(2,1)} %get-tuple-element.26), channel_id=1, source_target_pairs={{0,1},{4,5},{9,8},{13,12},{18,19},{22,23},{27,26},{31,30}} | collective-permute-start | bytes 2359304 | tf_op jit(solution)/shard_map/ppermute | solution.py:932
  10.9 14.1 %collective-permute-start.3 = (bf16[3,256,512]{2,1,0:T(8,128)(2,1)}, bf16[3,256,512]{2,1,0:T(8,128)(2,1)}, u32[]{:S(2)}, u32[]{:S(2)}) collective-permute-start(bf16[3,256,512]{2,1,0:T(8,128)(2,1)} %get-tuple-element.33.refs_0_), channel_id=1, source_target_pairs={{0,2},{4,6},{9,11},{13,15},{18,16},{22,20},{27,25},{31,29}} | collective-permute-start | bytes 2359304 | tf_op jit(solution)/shard_map/ppermute | solution.py:932
  13.1 17.3 %collective-permute-start.4 = (bf16[3,256,512]{2,1,0:T(8,128)(2,1)}, bf16[3,256,512]{2,1,0:T(8,128)(2,1)}, u32[]{:S(2)}, u32[]{:S(2)}) collective-permute-start(bf16[3,256,512]{2,1,0:T(8,128)(2,1)} %get-tuple-element.26), channel_id=1, source_target_pairs={{0,3},{4,7},{9,10},{13,14},{18,17},{22,21},{27,24},{31,28}} | collective-permute-start | bytes 2359304 | tf_op jit(solution)/shard_map/ppermute | solution.py:932
  42.6 20.8 %collective-permute-start.8 = (bf16[3,256,512]{2,1,0:T(8,128)(2,1)}, bf16[3,256,512]{2,1,0:T(8,128)(2,1)}, u32[]{:S(2)}, u32[]{:S(2)}) collective-permute-start(bf16[3,256,512]{2,1,0:T(8,128)(2,1)} %get-tuple-element.38.mine_ref), channel_id=1, source_target_pairs={{0,2},{1,3},{2,0},{3,1},{4,6},{5,7},{6,4},{7,5},{8,10},{9,11},{10,... | collective-permute-start | bytes 2359304 | tf_op jit(solution)/shard_map/ppermute | solution.py:27
  42.7 31.5 %collective-permute-start.1 = (bf16[2,512,512]{2,1,0:T(8,128)(2,1)}, bf16[2,512,512]{2,1,0:T(8,128)(2,1)}, u32[]{:S(2)}, u32[]{:S(2)}) collective-permute-start(bf16[2,512,512]{2,1,0:T(8,128)(2,1)} %get-tuple-element.24), channel_id=1, source_target_pairs={{0,1},{1,2},{2,3},{4,5},{5,6},{6,7},{8,9},{9,10},{10,11},{12,13},{... | collective-permute-start | bytes 3145736 | tf_op jit(solution)/shard_map/ppermute | solution.py:41
  46.6 38.9 %collective-permute-start = (bf16[2,512,512]{2,1,0:T(8,128)(2,1)}, bf16[2,512,512]{2,1,0:T(8,128)(2,1)}, u32[]{:S(2)}, u32[]{:S(2)}) collective-permute-start(bf16[2,512,512]{2,1,0:T(8,128)(2,1)} %get-tuple-element.23), channel_id=1, source_target_pairs={{0,1},{1,2},{2,3},{4,5},{5,6},{6,7},{8,9},{9,10},{10,11},{12,13},{... | collective-permute-start | bytes 3145736 | tf_op jit(solution)/shard_map/ppermute | solution.py:41
  48.6 41.4 %collective-permute-start.7 = (bf16[3,256,512]{2,1,0:T(8,128)(2,1)}, bf16[3,256,512]{2,1,0:T(8,128)(2,1)}, u32[]{:S(2)}, u32[]{:S(2)}) collective-permute-start(bf16[3,256,512]{2,1,0:T(8,128)(2,1)} %get-tuple-element.38.mine_ref), channel_id=1, source_target_pairs={{0,1},{1,0},{2,3},{3,2},{4,5},{5,4},{6,7},{7,6},{8,9},{9,8},{10,11... | collective-permute-start | bytes 2359304 | tf_op jit(solution)/shard_map/ppermute | solution.py:27
  48.6 41.4 %collective-permute-start.10 = (bf16[3,256,512]{2,1,0:T(8,128)(2,1)}, bf16[3,256,512]{2,1,0:T(8,128)(2,1)}, u32[]{:S(2)}, u32[]{:S(2)}) collective-permute-start(bf16[3,256,512]{2,1,0:T(8,128)(2,1)} %get-tuple-element.39.pack_ref), channel_id=1, source_target_pairs={{0,1},{1,0},{2,3},{3,2},{4,5},{5,4},{6,7},{7,6},{8,9},{9,8},{10,11... | collective-permute-start | bytes 2359304 | tf_op jit(solution)/shard_map/ppermute | solution.py:27
  63.4 26.6 %collective-permute-start.9 = (bf16[3,256,512]{2,1,0:T(8,128)(2,1)}, bf16[3,256,512]{2,1,0:T(8,128)(2,1)}, u32[]{:S(2)}, u32[]{:S(2)}) collective-permute-start(bf16[3,256,512]{2,1,0:T(8,128)(2,1)} %collective-permute-done.8.far_ref), channel_id=1, source_target_pairs={{0,1},{1,0},{2,3},{3,2},{4,5},{5,4},{6,7},{7,6},{8,9},{9,8},{10,11... | collective-permute-start | bytes 2359304 | tf_op jit(solution)/shard_map/ppermute | solution.py:27

commit v9 on v8

--- a/solution.py
+++ b/solution.py
@@ -311,7 +311,7 @@
 
     @pl.when(leading)
     def _():
-        placed(ck_ref, cv_ref, kt_ref, v_ref, 0)
+        placed(ck_ref.at[:, window - near :], cv_ref.at[:, window - near :], kt_ref, v_ref, 0)
 
     @pl.when(jnp.logical_not(leading))
     def _():
@@ -347,7 +347,7 @@
         span = v_ref[:, chunk(max(b, missing)).start : chunk(b + inner).stop]
         out = jnp.dot(span, jnp.concatenate(raised, axis=0), preferred_element_type=jnp.float32)
         if b >= missing:
-            at = slice((b - missing) * block, (b - missing + 1) * block)
+            at = slice(b * block, (b + 1) * block)
             o_ref[:, at] = (out[:hd] * (1.0 / out[hd : hd + 1])).astype(jnp.bfloat16)
         else:
             at = slice(b * block, (b + 1) * block)
@@ -369,14 +369,13 @@
     near = prior.shape[2]
     far = WINDOW - near
     here = pl.BlockSpec((HEAD_SIZE, WINDOW), lambda h: (h, 0))
-    nearer = pl.BlockSpec((HEAD_SIZE, near), lambda h: (h, far // near))
     prior_keys = pl.BlockSpec((None, HEAD_SIZE, near), lambda h: (0, h, 0))
     prior_values = pl.BlockSpec((None, HEAD_SIZE, near), lambda h: (1, h, 0))
     rows = 8
     stats = jax.ShapeDtypeStruct((heads * rows, far), jnp.float32)
     stat = pl.BlockSpec((rows, far), lambda h: (h, 0))
     return pl.pallas_call(
-        functools.partial(early_body, block=min(256, near)),
+        functools.partial(early_body, block=min(256, far)),
         out_shape=(
             jax.ShapeDtypeStruct((features, tokens), jnp.bfloat16),
             jax.ShapeDtypeStruct((features, far), jnp.float32),
@@ -384,9 +383,9 @@
             stats,
         ),
         grid=(heads,),
-        in_specs=[here, prior_keys, prior_values, here, here, nearer, nearer]
+        in_specs=[here, prior_keys, prior_values, here, here, here, here]
         + [pl.BlockSpec(memory_space=pl.ANY)],
-        out_specs=(nearer, pl.BlockSpec((HEAD_SIZE, far), lambda h: (h, 0)), stat, stat),
+        out_specs=(here, pl.BlockSpec((HEAD_SIZE, far), lambda h: (h, 0)), stat, stat),
         scratch_shapes=[
             pltpu.VMEM((near + WINDOW, 2 * HEAD_SIZE), jnp.bfloat16),
             pltpu.VMEM((HEAD_SIZE + 16, near + WINDOW), jnp.bfloat16),
@@ -588,9 +587,11 @@
 def stage_body(key_ref, value_ref, rate_ref, target_ref, *refs):
     end_refs, (held_ref, values_ref, made_ref, sem, sem_end) = refs[:-5], refs[-5:]
     features, tokens = key_ref.shape
-    width = end_refs[0].shape[2]
     step = HEAD_SIZE
-    lasts = [slice(tokens - (part + 1) * width, tokens - part * width) for part in range(len(end_refs))]
+    lasts, stop = [], tokens
+    for end_ref in end_refs:
+        lasts.append(slice(stop - end_ref.shape[2], stop))
+        stop -= end_ref.shape[2]
     begin = pl.multiple_of(lax.axis_index("narrow") * tokens, tokens)
     rates = -rate_ref[pl.ds(lax.axis_index("wide"), 1), pl.ds(begin, tokens)]
     values = [
@@ -601,7 +602,7 @@
     ]
     keys = [
         pltpu.make_async_copy(
-            key_ref.at[:, last], held_ref.at[part], sem_end.at[0, part]
+            key_ref.at[:, last], held_ref.at[:, last.start - stop : last.stop - stop], sem_end.at[0, part]
         )
         for part, last in enumerate(lasts)
     ]
@@ -621,22 +622,25 @@
     for part, end_ref in enumerate(end_refs):
         leave(values_ref.at[:, lasts[part]], end_ref.at[1], sem_end.at[1, part])
         keys[part].wait()
-        leave(held_ref.at[part], end_ref.at[0], sem_end.at[2, part])
+        last = lasts[part]
+        leave(
+            held_ref.at[:, last.start - stop : last.stop - stop], end_ref.at[0], sem_end.at[2, part]
+        )
     for copy in leaving:
         copy.wait()
 
 
-def stage(keys, values, rates, parts):
+def stage(keys, values, rates, widths):
     features, tokens = keys.shape
-    width = WINDOW // parts
+    parts = len(widths)
     return pl.pallas_call(
         stage_body,
         out_shape=(jax.ShapeDtypeStruct((features, tokens), jnp.bfloat16),)
-        + (jax.ShapeDtypeStruct((2, features, width), jnp.bfloat16),) * parts,
+        + tuple(jax.ShapeDtypeStruct((2, features, width), jnp.bfloat16) for width in widths),
         in_specs=anywhere(2) + [pl.BlockSpec(memory_space=pltpu.VMEM)],
         out_specs=tuple(anywhere(1 + parts)),
         scratch_shapes=[
-            pltpu.VMEM((parts, features, width), jnp.bfloat16),
+            pltpu.VMEM((features, sum(widths)), jnp.bfloat16),
             pltpu.VMEM((features, tokens), jnp.bfloat16),
             pltpu.VMEM((features, tokens), jnp.bfloat16),
             pltpu.SemaphoreType.DMA((2, features // HEAD_SIZE)),
@@ -934,10 +938,13 @@
     own, other = prepare(gate_fast, lift_fast, down_fast)
     arrivals = {}
     for step in sorted(range(1, narrow_count), key=lambda step: step < 2):
-        arrivals[step] = from_owner((own, other)[step % 2], step)
+        if step == 1:
+            arrivals[step] = swapped(other, "narrow", 0)
+        else:
+            arrivals[step] = from_owner((own, other)[step % 2], step)
     pair_keys = swapped(key_states, "narrow", 0)
-    parts = 2
-    targets, *ends = stage(key_states, value_states, token_rates, parts)
+    widths = (WINDOW - WINDOW // 4, WINDOW // 4)
+    targets, *ends = stage(key_states, value_states, token_rates, widths)
     pair_targets = swapped(targets, "narrow", 0)
     attended = attend_late(query_states, key_states, value_states)
     sources = [own] + [arrivals[step] for step in range(1, narrow_count)]

time: 103 us -> 98.3 us (0.954)
  the two profiles are of different devices: /device:TPU:20 before, /device:TPU:0 now
where the time goes in v9:
time: 98.3 us; the launch traced here: 98 us
  Pallas kernels  54.2 us (55%)
  waiting for transfers between devices  26.2 us (27%)
  starting transfers between devices  16.8 us (17%)
    ppermute x7, waiting for transfers between devices, swapped(): lax.ppermute(array, axis, [(i, i ^ 1 << distance) for i in range(lax.axis...  18.3 us
    pallas_call x1, Pallas kernels, fast_recall(): pl.pallas_call(recall_body, out_shape=jax.ShapeDtypeStruct((features, tok...  12.8 us
    pallas_call x1, Pallas kernels, fast_sums(): pl.pallas_call(functools.partial(sums_body, owned=owned, cuts=cuts), out_...  12.2 us
    pallas_call x1, Pallas kernels, attend_early(): pl.pallas_call(functools.partial(early_body, block=min(256, far)), out_sh...  9.7 us
    pallas_call x1, Pallas kernels, attend_late(): pl.pallas_call(functools.partial(attend_body, block=min(256, WINDOW), win...  9.69 us
    ppermute x2, waiting for transfers between devices, from_owner(): return lax.ppermute(value, ('wide', 'narrow'), pairs)  7.89 us
    ppermute x2, starting transfers between devices, from_owner(): return lax.ppermute(value, ('wide', 'narrow'), pairs)  7.51 us
    ppermute x2, starting transfers between devices, from_behind(): lax.ppermute(value, axis, [(source, source + steps) for source in range(i...  5.67 us
  transfers between devices with their start and end apart: 11, of which 2 were waited for; matrix products, arithmetic and copies ran while one was open for 0% of the time, Pallas kernels for 42%

profile of v9, /device:TPU:0, one launch (start us, length us, event | category | flops | bytes accessed | tf_op | source)
XLA Modules:
  0.0 98.0 jit_solution(13704179457590505073)
XLA Ops:
  0.6 0.6 collective-permute-start.5
  1.2 4.2 %stage.1 = (bf16[512,2048]{1,0:T(8,128)(2,1)}, bf16[2,512,768]{2,1,0:T(8,128)(2,1)}, bf16[2,512,256]{2,1,0:T(8,128)(2,1)}) custom-call(bf16[512,2048]{1,0:T(8,128)(2,1)} %refs_4_.1, bf16[512,2048]{1,0:T(8,128)(2,1)} %vc_ref.3, f32[8,8192]{1,0:T(8,128)} %rate_ref.1), custom_call_target="tpu_custom_call" | custom-call | flops 1048576 | bytes 8388608 | tf_op jit(solution)/shard_map/stage/pallas_call | solution.py:636
  5.4 0.1 collective-permute-start.6
  5.5 2.5 %prepare.1 = (bf16[3,256,512]{2,1,0:T(8,128)(2,1)}, bf16[3,256,512]{2,1,0:T(8,128)(2,1)}) custom-call(bf16[2,512,512]{2,1,0:T(8,128)(2,1)} %gate_ref.1, bf16[2,512,512]{2,1,0:T(8,128)(2,1)} %lift_ref.1, bf16[2,512,512]{2,1,0:T(8,128)(2,1)} %down_ref.1), custom_call_target="tpu_custom_call" | custom-call | bytes 3145728 | tf_op jit(solution)/shard_map/prepare/pallas_call | solution.py:569
  8.0 0.5 collective-permute-start.2
  8.5 5.3 %collective-permute-start.3 = (bf16[3,256,512]{2,1,0:T(8,128)(2,1)}, bf16[3,256,512]{2,1,0:T(8,128)(2,1)}, u32[]{:S(2)}, u32[]{:S(2)}) collective-permute-start(bf16[3,256,512]{2,1,0:T(8,128)(2,1)} %get-tuple-element.33.refs_0_), channel_id=1, source_target_pairs={{0,2},{4,6},{9,11},{13,15},{18,16},{22,20},{27,25},{31,29}} | collective-permute-start | bytes 2359304 | tf_op jit(solution)/shard_map/ppermute | solution.py:936
  13.9 2.2 %collective-permute-start.4 = (bf16[3,256,512]{2,1,0:T(8,128)(2,1)}, bf16[3,256,512]{2,1,0:T(8,128)(2,1)}, u32[]{:S(2)}, u32[]{:S(2)}) collective-permute-start(bf16[3,256,512]{2,1,0:T(8,128)(2,1)} %get-tuple-element.26), channel_id=1, source_target_pairs={{0,3},{4,7},{9,10},{13,14},{18,17},{22,21},{27,24},{31,28}} | collective-permute-start | bytes 2359304 | tf_op jit(solution)/shard_map/ppermute | solution.py:936
  16.0 9.7 %attend_late.1._ = bf16[512,2048]{1,0:T(8,128)(2,1)} custom-call(bf16[512,2048]{1,0:T(8,128)(2,1)} %query_ref.1, bf16[512,2048]{1,0:T(8,128)(2,1)} %refs_4_.1, bf16[512,2048]{1,0:T(8,128)(2,1)} %vc_ref.3, bf16[512,2048]{1,0:T(8,128)(2,1)} %refs_4_.1, bf16[512,2048]{1,0:T(8,128)(2,1)} %vc_ref.3), custom_call_target="tpu_custom_call" | custom-call | flops 2684354560 | bytes 5242880 | tf_op jit(solution)/shard_map/attend_late/pallas_call | solution.py:269
  25.7 0.0 collective-permute-done.2.refs_1_
  25.7 2.5 %collective-permute-start.1 = (bf16[2,512,768]{2,1,0:T(8,128)(2,1)}, bf16[2,512,768]{2,1,0:T(8,128)(2,1)}, u32[]{:S(2)}, u32[]{:S(2)}) collective-permute-start(bf16[2,512,768]{2,1,0:T(8,128)(2,1)} %get-tuple-element.24), channel_id=1, source_target_pairs={{0,1},{1,2},{2,3},{4,5},{5,6},{6,7},{8,9},{9,10},{10,11},{12,13},{... | collective-permute-start | bytes 4718600 | tf_op jit(solution)/shard_map/ppermute | solution.py:41
  28.2 0.0 collective-permute-done.3.refs_2_
  28.2 7.9 %collective-permute-done.4.refs_3_ = bf16[3,256,512]{2,1,0:T(8,128)(2,1)} collective-permute-done((bf16[3,256,512]{2,1,0:T(8,128)(2,1)}, bf16[3,256,512]{2,1,0:T(8,128)(2,1)}, u32[]{:S(2)}, u32[]{:S(2)}) %collective-permute-start.4) | collective-permute-done | bytes 786464 | tf_op jit(solution)/shard_map/ppermute | solution.py:936
  36.1 0.0 collective-permute-done.5.refs_6_
  36.1 0.0 collective-permute-done.6.refs_7_
  36.1 12.2 %fast_sums.1 = (bf16[3,256,512]{2,1,0:T(8,128)(2,1)}, bf16[3,256,512]{2,1,0:T(8,128)(2,1)}) custom-call(bf16[3,256,512]{2,1,0:T(8,128)(2,1)} %get-tuple-element.33.refs_0_, bf16[3,256,512]{2,1,0:T(8,128)(2,1)} %collective-permute-done.2.refs_1_, bf16[3,256,512]{2,1,0:T(8,128)(2,1)} %collective-permute-done.3.refs_2_, ...), custom_call_target="tpu_custom_call" | custom-call | flops 6442450944 | bytes 10747904 | tf_op jit(solution)/shard_map/fast_sums/pallas_call | solution.py:736
  48.3 0.1 collective-permute-start.8
  48.4 2.3 %collective-permute-start.7 = (bf16[3,256,512]{2,1,0:T(8,128)(2,1)}, bf16[3,256,512]{2,1,0:T(8,128)(2,1)}, u32[]{:S(2)}, u32[]{:S(2)}) collective-permute-start(bf16[3,256,512]{2,1,0:T(8,128)(2,1)} %get-tuple-element.38.mine_ref), channel_id=1, source_target_pairs={{0,1},{1,0},{2,3},{3,2},{4,5},{5,4},{6,7},{7,6},{8,9},{9,8},{10,11... | collective-permute-start | bytes 2359304 | tf_op jit(solution)/shard_map/ppermute | solution.py:27
  50.7 0.0 collective-permute-start.10
  50.7 18.3 %collective-permute-done.8.far_ref = bf16[3,256,512]{2,1,0:T(8,128)(2,1)} collective-permute-done((bf16[3,256,512]{2,1,0:T(8,128)(2,1)}, bf16[3,256,512]{2,1,0:T(8,128)(2,1)}, u32[]{:S(2)}, u32[]{:S(2)}) %collective-permute-start.8) | collective-permute-done | bytes 786464 | tf_op jit(solution)/shard_map/ppermute | solution.py:27
  69.0 0.0 collective-permute-start.9
  69.0 3.2 %collective-permute-start = (bf16[2,512,256]{2,1,0:T(8,128)(2,1)}, bf16[2,512,256]{2,1,0:T(8,128)(2,1)}, u32[]{:S(2)}, u32[]{:S(2)}) collective-permute-start(bf16[2,512,256]{2,1,0:T(8,128)(2,1)} %get-tuple-element.23), channel_id=1, source_target_pairs={{0,1},{1,2},{2,3},{4,5},{5,6},{6,7},{8,9},{9,10},{10,11},{12,13},{... | collective-permute-start | bytes 1572872 | tf_op jit(solution)/shard_map/ppermute | solution.py:41
  72.2 0.0 collective-permute-done.1.kp_ref.vp_ref
  72.2 9.7 %attend_early.1 = (bf16[512,2048]{1,0:T(8,128)(2,1)}, f32[512,256]{1,0:T(8,128)}, f32[32,256]{1,0:T(8,128)}, f32[32,256]{1,0:T(8,128)}) custom-call(bf16[512,2048]{1,0:T(8,128)(2,1)} %query_ref.1, bf16[2,512,768]{2,1,0:T(8,128)(2,1)} %collective-permute-done.1.kp_ref.vp_ref, ...), custom_call_target="tpu_custom_call", output_to_operand_aliasing={{0}: (7, {})} | custom-call | flops 2684354560 | bytes 7340032 | tf_op jit(solution)/shard_map/attend_early/pallas_call | solution.py:377
  81.9 0.0 collective-permute-done.prior_ref
  81.9 3.1 %attend_last.1 = bf16[512,2048]{1,0:T(8,128)(2,1)} custom-call(bf16[512,2048]{1,0:T(8,128)(2,1)} %query_ref.1, bf16[2,512,256]{2,1,0:T(8,128)(2,1)} %collective-permute-done.prior_ref, bf16[512,1024]{1,0:T(8,128)(2,1)} %ck_ref.3, bf16[512,1024]{1,0:T(8,128)(2,1)} %cv_ref.3, f32[512,256]{1,0:T(8,128)} %get-tuple-element.29.part_ref, ...), custom_call_target="tpu_custom_call", output_to_operand_aliasing={{}: (7, {})} | custom-call | flops 100663296 | bytes 1835008 | tf_op jit(solution)/shard_map/attend_last/pallas_call | solution.py:502
  85.1 0.0 collective-permute-done.7.other_ref
  85.1 0.0 collective-permute-done.10.pair_pack_ref
  85.1 0.0 collective-permute-done.9.other_far_ref
  85.1 12.8 %fast_recall.1 = bf16[512,2048]{1,0:T(8,128)(2,1)} custom-call(bf16[3,256,512]{2,1,0:T(8,128)(2,1)} %get-tuple-element.38.mine_ref, bf16[3,256,512]{2,1,0:T(8,128)(2,1)} %collective-permute-done.7.other_ref, bf16[3,256,512]{2,1,0:T(8,128)(2,1)} %collective-permute-done.8.far_ref, bf16[3,256,512]{2,1,0:T(8,128)(2,1)} %collective-permute-done.9.other_far_ref, ...), custom_call_target="tpu_custom_call" | custom-call | flops 8053063680 | bytes 7340032 | tf_op jit(solution)/shard_map/fast_recall/pallas_call | solution.py:878
Async XLA Ops:
  0.6 35.5 %collective-permute-start.5 = (bf16[512,2048]{1,0:T(8,128)(2,1)}, bf16[512,2048]{1,0:T(8,128)(2,1)}, u32[]{:S(2)}, u32[]{:S(2)}) collective-permute-start(bf16[512,2048]{1,0:T(8,128)(2,1)} %refs_4_.1), channel_id=1, source_target_pairs={{0,1},{1,0},{2,3},{3,2},{4,5},{5,4},{6,7},{7,6},{8,9},{9,8},{10,11... | collective-permute-start | bytes 6291464 | tf_op jit(solution)/shard_map/ppermute | solution.py:27
  5.4 30.7 %collective-permute-start.6 = (bf16[512,2048]{1,0:T(8,128)(2,1)}, bf16[512,2048]{1,0:T(8,128)(2,1)}, u32[]{:S(2)}, u32[]{:S(2)}) collective-permute-start(bf16[512,2048]{1,0:T(8,128)(2,1)} %get-tuple-element.37.refs_5_), channel_id=1, source_target_pairs={{0,1},{1,0},{2,3},{3,2},{4,5},{5,4},{6,7},{7,6},{8,9},{9,8},{10,11... | collective-permute-start | bytes 6291464 | tf_op jit(solution)/shard_map/ppermute | solution.py:27
  8.0 17.7 %collective-permute-start.2 = (bf16[3,256,512]{2,1,0:T(8,128)(2,1)}, bf16[3,256,512]{2,1,0:T(8,128)(2,1)}, u32[]{:S(2)}, u32[]{:S(2)}) collective-permute-start(bf16[3,256,512]{2,1,0:T(8,128)(2,1)} %get-tuple-element.26), channel_id=1, source_target_pairs={{0,1},{1,0},{2,3},{3,2},{4,5},{5,4},{6,7},{7,6},{8,9},{9,8},{10,11... | collective-permute-start | bytes 2359304 | tf_op jit(solution)/shard_map/ppermute | solution.py:27
  8.5 19.7 %collective-permute-start.3 = (bf16[3,256,512]{2,1,0:T(8,128)(2,1)}, bf16[3,256,512]{2,1,0:T(8,128)(2,1)}, u32[]{:S(2)}, u32[]{:S(2)}) collective-permute-start(bf16[3,256,512]{2,1,0:T(8,128)(2,1)} %get-tuple-element.33.refs_0_), channel_id=1, source_target_pairs={{0,2},{4,6},{9,11},{13,15},{18,16},{22,20},{27,25},{31,29}} | collective-permute-start | bytes 2359304 | tf_op jit(solution)/shard_map/ppermute | solution.py:936
  13.9 22.2 %collective-permute-start.4 = (bf16[3,256,512]{2,1,0:T(8,128)(2,1)}, bf16[3,256,512]{2,1,0:T(8,128)(2,1)}, u32[]{:S(2)}, u32[]{:S(2)}) collective-permute-start(bf16[3,256,512]{2,1,0:T(8,128)(2,1)} %get-tuple-element.26), channel_id=1, source_target_pairs={{0,3},{4,7},{9,10},{13,14},{18,17},{22,21},{27,24},{31,28}} | collective-permute-start | bytes 2359304 | tf_op jit(solution)/shard_map/ppermute | solution.py:936
  25.7 46.5 %collective-permute-start.1 = (bf16[2,512,768]{2,1,0:T(8,128)(2,1)}, bf16[2,512,768]{2,1,0:T(8,128)(2,1)}, u32[]{:S(2)}, u32[]{:S(2)}) collective-permute-start(bf16[2,512,768]{2,1,0:T(8,128)(2,1)} %get-tuple-element.24), channel_id=1, source_target_pairs={{0,1},{1,2},{2,3},{4,5},{5,6},{6,7},{8,9},{9,10},{10,11},{12,13},{... | collective-permute-start | bytes 4718600 | tf_op jit(solution)/shard_map/ppermute | solution.py:41
  48.3 20.7 %collective-permute-start.8 = (bf16[3,256,512]{2,1,0:T(8,128)(2,1)}, bf16[3,256,512]{2,1,0:T(8,128)(2,1)}, u32[]{:S(2)}, u32[]{:S(2)}) collective-permute-start(bf16[3,256,512]{2,1,0:T(8,128)(2,1)} %get-tuple-element.38.mine_ref), channel_id=1, source_target_pairs={{0,2},{1,3},{2,0},{3,1},{4,6},{5,7},{6,4},{7,5},{8,10},{9,11},{10,... | collective-permute-start | bytes 2359304 | tf_op jit(solution)/shard_map/ppermute | solution.py:27
  48.4 36.7 %collective-permute-start.7 = (bf16[3,256,512]{2,1,0:T(8,128)(2,1)}, bf16[3,256,512]{2,1,0:T(8,128)(2,1)}, u32[]{:S(2)}, u32[]{:S(2)}) collective-permute-start(bf16[3,256,512]{2,1,0:T(8,128)(2,1)} %get-tuple-element.38.mine_ref), channel_id=1, source_target_pairs={{0,1},{1,0},{2,3},{3,2},{4,5},{5,4},{6,7},{7,6},{8,9},{9,8},{10,11... | collective-permute-start | bytes 2359304 | tf_op jit(solution)/shard_map/ppermute | solution.py:27
  50.7 34.4 %collective-permute-start.10 = (bf16[3,256,512]{2,1,0:T(8,128)(2,1)}, bf16[3,256,512]{2,1,0:T(8,128)(2,1)}, u32[]{:S(2)}, u32[]{:S(2)}) collective-permute-start(bf16[3,256,512]{2,1,0:T(8,128)(2,1)} %get-tuple-element.39.pack_ref), channel_id=1, source_target_pairs={{0,1},{1,0},{2,3},{3,2},{4,5},{5,4},{6,7},{7,6},{8,9},{9,8},{10,11... | collective-permute-start | bytes 2359304 | tf_op jit(solution)/shard_map/ppermute | solution.py:27
  69.0 16.1 %collective-permute-start.9 = (bf16[3,256,512]{2,1,0:T(8,128)(2,1)}, bf16[3,256,512]{2,1,0:T(8,128)(2,1)}, u32[]{:S(2)}, u32[]{:S(2)}) collective-permute-start(bf16[3,256,512]{2,1,0:T(8,128)(2,1)} %collective-permute-done.8.far_ref), channel_id=1, source_target_pairs={{0,1},{1,0},{2,3},{3,2},{4,5},{5,4},{6,7},{7,6},{8,9},{9,8},{10,11... | collective-permute-start | bytes 2359304 | tf_op jit(solution)/shard_map/ppermute | solution.py:27
  69.0 12.9 %collective-permute-start = (bf16[2,512,256]{2,1,0:T(8,128)(2,1)}, bf16[2,512,256]{2,1,0:T(8,128)(2,1)}, u32[]{:S(2)}, u32[]{:S(2)}) collective-permute-start(bf16[2,512,256]{2,1,0:T(8,128)(2,1)} %get-tuple-element.23), channel_id=1, source_target_pairs={{0,1},{1,2},{2,3},{4,5},{5,6},{6,7},{8,9},{9,10},{10,11},{12,13},{... | collective-permute-start | bytes 1572872 | tf_op jit(solution)/shard_map/ppermute | solution.py:41

commit v10 on v8

--- a/solution.py
+++ b/solution.py
@@ -501,7 +501,7 @@
     far = part.shape[1]
     pieces = pltpu.VMEM((features, far), jnp.bfloat16)
     return pl.pallas_call(
-        functools.partial(last_body, block=min(256, far)),
+        functools.partial(last_body, block=min(512, far)),
         out_shape=jax.ShapeDtypeStruct((features, tokens), jnp.bfloat16),
         in_specs=[pl.BlockSpec(memory_space=pl.ANY)] * 8,
         out_specs=pl.BlockSpec(memory_space=pl.ANY),
@@ -934,7 +934,10 @@
     own, other = prepare(gate_fast, lift_fast, down_fast)
     arrivals = {}
     for step in sorted(range(1, narrow_count), key=lambda step: step < 2):
-        arrivals[step] = from_owner((own, other)[step % 2], step)
+        if step == 1:
+            arrivals[step] = swapped(other, "narrow", 0)
+        else:
+            arrivals[step] = from_owner((own, other)[step % 2], step)
     pair_keys = swapped(key_states, "narrow", 0)
     parts = 2
     targets, *ends = stage(key_states, value_states, token_rates, parts)

time: 103 us -> 101 us (0.981)
  the two profiles are of different devices: /device:TPU:20 before, /device:TPU:1 now
where the time goes in v10:
time: 101 us
  Pallas kernels  54.6 us (54%)
  waiting for transfers between devices  23.2 us (23%)
  starting transfers between devices  22.2 us (22%)
    ppermute x7, starting transfers between devices, swapped(): lax.ppermute(array, axis, [(i, i ^ 1 << distance) for i in range(lax.axis...  14.9 us
    pallas_call x1, Pallas kernels, fast_recall(): pl.pallas_call(recall_body, out_shape=jax.ShapeDtypeStruct((features, tok...  12.8 us
    ppermute x7, waiting for transfers between devices, swapped(): lax.ppermute(array, axis, [(i, i ^ 1 << distance) for i in range(lax.axis...  12.3 us
    pallas_call x1, Pallas kernels, fast_sums(): pl.pallas_call(functools.partial(sums_body, owned=owned, cuts=cuts), out_...  12.2 us
    ppermute x2, waiting for transfers between devices, from_behind(): lax.ppermute(value, axis, [(source, source + steps) for source in range(i...  10.8 us
    pallas_call x1, Pallas kernels, attend_late(): pl.pallas_call(functools.partial(attend_body, block=min(256, WINDOW), win...  9.69 us
    pallas_call x1, Pallas kernels, attend_early(): pl.pallas_call(functools.partial(early_body, block=min(256, near)), out_s...  9.19 us
    ppermute x2, starting transfers between devices, from_behind(): lax.ppermute(value, axis, [(source, source + steps) for source in range(i...  4.23 us
  transfers between devices with their start and end apart: 11, of which 3 were waited for; matrix products, arithmetic and copies ran while one was open for 0% of the time, Pallas kernels for 29%

profile of v10, /device:TPU:1, one launch (start us, length us, event | category | flops | bytes accessed | tf_op | source)
XLA Modules:
  0.0 100.9 jit_solution(13406451328691994408)
XLA Ops:
  0.6 0.1 collective-permute-start.5
  0.7 4.2 %stage.1 = (bf16[512,2048]{1,0:T(8,128)(2,1)}, bf16[2,512,512]{2,1,0:T(8,128)(2,1)}, bf16[2,512,512]{2,1,0:T(8,128)(2,1)}) custom-call(bf16[512,2048]{1,0:T(8,128)(2,1)} %refs_4_.1, bf16[512,2048]{1,0:T(8,128)(2,1)} %vc_ref.3, f32[8,8192]{1,0:T(8,128)} %rate_ref.1), custom_call_target="tpu_custom_call" | custom-call | flops 1048576 | bytes 8388608 | tf_op jit(solution)/shard_map/stage/pallas_call | solution.py:632
  4.9 0.6 collective-permute-start.6
  5.5 2.5 %prepare.1 = (bf16[3,256,512]{2,1,0:T(8,128)(2,1)}, bf16[3,256,512]{2,1,0:T(8,128)(2,1)}) custom-call(bf16[2,512,512]{2,1,0:T(8,128)(2,1)} %gate_ref.1, bf16[2,512,512]{2,1,0:T(8,128)(2,1)} %lift_ref.1, bf16[2,512,512]{2,1,0:T(8,128)(2,1)} %down_ref.1), custom_call_target="tpu_custom_call" | custom-call | bytes 3145728 | tf_op jit(solution)/shard_map/prepare/pallas_call | solution.py:570
  8.0 0.1 collective-permute-start.2
  8.1 1.6 %collective-permute-start.3 = (bf16[3,256,512]{2,1,0:T(8,128)(2,1)}, bf16[3,256,512]{2,1,0:T(8,128)(2,1)}, u32[]{:S(2)}, u32[]{:S(2)}) collective-permute-start(bf16[3,256,512]{2,1,0:T(8,128)(2,1)} %get-tuple-element.33.refs_0_), channel_id=1, source_target_pairs={{0,2},{4,6},{9,11},{13,15},{18,16},{22,20},{27,25},{31,29}} | collective-permute-start | bytes 2359304 | tf_op jit(solution)/shard_map/ppermute | solution.py:932
  9.6 1.5 %collective-permute-start.4 = (bf16[3,256,512]{2,1,0:T(8,128)(2,1)}, bf16[3,256,512]{2,1,0:T(8,128)(2,1)}, u32[]{:S(2)}, u32[]{:S(2)}) collective-permute-start(bf16[3,256,512]{2,1,0:T(8,128)(2,1)} %get-tuple-element.26), channel_id=1, source_target_pairs={{0,3},{4,7},{9,10},{13,14},{18,17},{22,21},{27,24},{31,28}} | collective-permute-start | bytes 2359304 | tf_op jit(solution)/shard_map/ppermute | solution.py:932
  11.2 9.7 %attend_late.1._ = bf16[512,2048]{1,0:T(8,128)(2,1)} custom-call(bf16[512,2048]{1,0:T(8,128)(2,1)} %query_ref.1, bf16[512,2048]{1,0:T(8,128)(2,1)} %refs_4_.1, bf16[512,2048]{1,0:T(8,128)(2,1)} %vc_ref.3, bf16[512,2048]{1,0:T(8,128)(2,1)} %refs_4_.1, bf16[512,2048]{1,0:T(8,128)(2,1)} %vc_ref.3), custom_call_target="tpu_custom_call" | custom-call | flops 2684354560 | bytes 5242880 | tf_op jit(solution)/shard_map/attend_late/pallas_call | solution.py:269
  20.9 0.0 collective-permute-done.2.refs_1_
  20.9 0.0 collective-permute-done.3.refs_2_
  20.9 0.0 collective-permute-done.4.refs_3_
  20.9 0.0 collective-permute-done.5.refs_6_
  20.9 0.0 collective-permute-done.6.refs_7_
  20.9 12.2 %fast_sums.1 = (bf16[3,256,512]{2,1,0:T(8,128)(2,1)}, bf16[3,256,512]{2,1,0:T(8,128)(2,1)}) custom-call(bf16[3,256,512]{2,1,0:T(8,128)(2,1)} %get-tuple-element.33.refs_0_, bf16[3,256,512]{2,1,0:T(8,128)(2,1)} %collective-permute-done.2.refs_1_, bf16[3,256,512]{2,1,0:T(8,128)(2,1)} %collective-permute-done.3.refs_2_, ...), custom_call_target="tpu_custom_call" | custom-call | flops 6442450944 | bytes 10747904 | tf_op jit(solution)/shard_map/fast_sums/pallas_call | solution.py:732
  33.1 11.9 %collective-permute-start.8 = (bf16[3,256,512]{2,1,0:T(8,128)(2,1)}, bf16[3,256,512]{2,1,0:T(8,128)(2,1)}, u32[]{:S(2)}, u32[]{:S(2)}) collective-permute-start(bf16[3,256,512]{2,1,0:T(8,128)(2,1)} %get-tuple-element.38.mine_ref), channel_id=1, source_target_pairs={{0,2},{1,3},{2,0},{3,1},{4,6},{5,7},{6,4},{7,5},{8,10},{9,11},{10,... | collective-permute-start | bytes 2359304 | tf_op jit(solution)/shard_map/ppermute | solution.py:27
  45.0 2.0 %collective-permute-start.1 = (bf16[2,512,512]{2,1,0:T(8,128)(2,1)}, bf16[2,512,512]{2,1,0:T(8,128)(2,1)}, u32[]{:S(2)}, u32[]{:S(2)}) collective-permute-start(bf16[2,512,512]{2,1,0:T(8,128)(2,1)} %get-tuple-element.24), channel_id=1, source_target_pairs={{0,1},{1,2},{2,3},{4,5},{5,6},{6,7},{8,9},{9,10},{10,11},{12,13},{... | collective-permute-start | bytes 3145736 | tf_op jit(solution)/shard_map/ppermute | solution.py:41
  47.0 2.2 %collective-permute-start = (bf16[2,512,512]{2,1,0:T(8,128)(2,1)}, bf16[2,512,512]{2,1,0:T(8,128)(2,1)}, u32[]{:S(2)}, u32[]{:S(2)}) collective-permute-start(bf16[2,512,512]{2,1,0:T(8,128)(2,1)} %get-tuple-element.23), channel_id=1, source_target_pairs={{0,1},{1,2},{2,3},{4,5},{5,6},{6,7},{8,9},{9,10},{10,11},{12,13},{... | collective-permute-start | bytes 3145736 | tf_op jit(solution)/shard_map/ppermute | solution.py:41
  49.3 1.4 %collective-permute-start.7 = (bf16[3,256,512]{2,1,0:T(8,128)(2,1)}, bf16[3,256,512]{2,1,0:T(8,128)(2,1)}, u32[]{:S(2)}, u32[]{:S(2)}) collective-permute-start(bf16[3,256,512]{2,1,0:T(8,128)(2,1)} %get-tuple-element.38.mine_ref), channel_id=1, source_target_pairs={{0,1},{1,0},{2,3},{3,2},{4,5},{5,4},{6,7},{7,6},{8,9},{9,8},{10,11... | collective-permute-start | bytes 2359304 | tf_op jit(solution)/shard_map/ppermute | solution.py:27
  50.7 0.0 collective-permute-start.10
  50.7 12.3 %collective-permute-done.8.far_ref = bf16[3,256,512]{2,1,0:T(8,128)(2,1)} collective-permute-done((bf16[3,256,512]{2,1,0:T(8,128)(2,1)}, bf16[3,256,512]{2,1,0:T(8,128)(2,1)}, u32[]{:S(2)}, u32[]{:S(2)}) %collective-permute-start.8) | collective-permute-done | bytes 786464 | tf_op jit(solution)/shard_map/ppermute | solution.py:27
  63.0 0.8 collective-permute-start.9
  63.8 8.8 %collective-permute-done.1.kp_ref.vp_ref = bf16[2,512,512]{2,1,0:T(8,128)(2,1)} collective-permute-done((bf16[2,512,512]{2,1,0:T(8,128)(2,1)}, bf16[2,512,512]{2,1,0:T(8,128)(2,1)}, u32[]{:S(2)}, u32[]{:S(2)}) %collective-permute-start.1) | collective-permute-done | bytes 1048608 | tf_op jit(solution)/shard_map/ppermute | solution.py:41
  72.6 9.2 %attend_early.1 = (bf16[512,2048]{1,0:T(8,128)(2,1)}, f32[512,512]{1,0:T(8,128)}, f32[32,512]{1,0:T(8,128)}, f32[32,512]{1,0:T(8,128)}) custom-call(bf16[512,2048]{1,0:T(8,128)(2,1)} %query_ref.1, bf16[2,512,512]{2,1,0:T(8,128)(2,1)} %collective-permute-done.1.kp_ref.vp_ref, ...), custom_call_target="tpu_custom_call", output_to_operand_aliasing={{0}: (7, {})} | custom-call | flops 2684354560 | bytes 7340032 | tf_op jit(solution)/shard_map/attend_early/pallas_call | solution.py:378
  81.8 2.0 %collective-permute-done.prior_ref = bf16[2,512,512]{2,1,0:T(8,128)(2,1)} collective-permute-done((bf16[2,512,512]{2,1,0:T(8,128)(2,1)}, bf16[2,512,512]{2,1,0:T(8,128)(2,1)}, u32[]{:S(2)}, u32[]{:S(2)}) %collective-permute-start) | collective-permute-done | bytes 1048608 | tf_op jit(solution)/shard_map/ppermute | solution.py:41
  83.8 4.1 %attend_last.1 = bf16[512,2048]{1,0:T(8,128)(2,1)} custom-call(bf16[512,2048]{1,0:T(8,128)(2,1)} %query_ref.1, bf16[2,512,512]{2,1,0:T(8,128)(2,1)} %collective-permute-done.prior_ref, bf16[512,1024]{1,0:T(8,128)(2,1)} %ck_ref.3, bf16[512,1024]{1,0:T(8,128)(2,1)} %cv_ref.3, f32[512,512]{1,0:T(8,128)} %get-tuple-element.29.part_ref, ...), custom_call_target="tpu_custom_call", output_to_operand_aliasing={{}: (7, {})} | custom-call | flops 402653184 | bytes 3670016 | tf_op jit(solution)/shard_map/attend_last/pallas_call | solution.py:503
  87.9 0.0 collective-permute-done.7.other_ref
  87.9 0.0 collective-permute-done.10.pair_pack_ref
  87.9 0.0 collective-permute-done.9.other_far_ref
  88.0 12.8 %fast_recall.1 = bf16[512,2048]{1,0:T(8,128)(2,1)} custom-call(bf16[3,256,512]{2,1,0:T(8,128)(2,1)} %get-tuple-element.38.mine_ref, bf16[3,256,512]{2,1,0:T(8,128)(2,1)} %collective-permute-done.7.other_ref, bf16[3,256,512]{2,1,0:T(8,128)(2,1)} %collective-permute-done.8.far_ref, bf16[3,256,512]{2,1,0:T(8,128)(2,1)} %collective-permute-done.9.other_far_ref, ...), custom_call_target="tpu_custom_call" | custom-call | flops 8053063680 | bytes 7340032 | tf_op jit(solution)/shard_map/fast_recall/pallas_call | solution.py:874
Async XLA Ops:
  0.6 20.3 %collective-permute-start.5 = (bf16[512,2048]{1,0:T(8,128)(2,1)}, bf16[512,2048]{1,0:T(8,128)(2,1)}, u32[]{:S(2)}, u32[]{:S(2)}) collective-permute-start(bf16[512,2048]{1,0:T(8,128)(2,1)} %refs_4_.1), channel_id=1, source_target_pairs={{0,1},{1,0},{2,3},{3,2},{4,5},{5,4},{6,7},{7,6},{8,9},{9,8},{10,11... | collective-permute-start | bytes 6291464 | tf_op jit(solution)/shard_map/ppermute | solution.py:27
  4.9 16.0 %collective-permute-start.6 = (bf16[512,2048]{1,0:T(8,128)(2,1)}, bf16[512,2048]{1,0:T(8,128)(2,1)}, u32[]{:S(2)}, u32[]{:S(2)}) collective-permute-start(bf16[512,2048]{1,0:T(8,128)(2,1)} %get-tuple-element.37.refs_5_), channel_id=1, source_target_pairs={{0,1},{1,0},{2,3},{3,2},{4,5},{5,4},{6,7},{7,6},{8,9},{9,8},{10,11... | collective-permute-start | bytes 6291464 | tf_op jit(solution)/shard_map/ppermute | solution.py:27
  8.0 12.9 %collective-permute-start.2 = (bf16[3,256,512]{2,1,0:T(8,128)(2,1)}, bf16[3,256,512]{2,1,0:T(8,128)(2,1)}, u32[]{:S(2)}, u32[]{:S(2)}) collective-permute-start(bf16[3,256,512]{2,1,0:T(8,128)(2,1)} %get-tuple-element.26), channel_id=1, source_target_pairs={{0,1},{1,0},{2,3},{3,2},{4,5},{5,4},{6,7},{7,6},{8,9},{9,8},{10,11... | collective-permute-start | bytes 2359304 | tf_op jit(solution)/shard_map/ppermute | solution.py:27
  8.1 12.8 %collective-permute-start.3 = (bf16[3,256,512]{2,1,0:T(8,128)(2,1)}, bf16[3,256,512]{2,1,0:T(8,128)(2,1)}, u32[]{:S(2)}, u32[]{:S(2)}) collective-permute-start(bf16[3,256,512]{2,1,0:T(8,128)(2,1)} %get-tuple-element.33.refs_0_), channel_id=1, source_target_pairs={{0,2},{4,6},{9,11},{13,15},{18,16},{22,20},{27,25},{31,29}} | collective-permute-start | bytes 2359304 | tf_op jit(solution)/shard_map/ppermute | solution.py:932
  9.6 11.3 %collective-permute-start.4 = (bf16[3,256,512]{2,1,0:T(8,128)(2,1)}, bf16[3,256,512]{2,1,0:T(8,128)(2,1)}, u32[]{:S(2)}, u32[]{:S(2)}) collective-permute-start(bf16[3,256,512]{2,1,0:T(8,128)(2,1)} %get-tuple-element.26), channel_id=1, source_target_pairs={{0,3},{4,7},{9,10},{13,14},{18,17},{22,21},{27,24},{31,28}} | collective-permute-start | bytes 2359304 | tf_op jit(solution)/shard_map/ppermute | solution.py:932
  33.1 29.9 %collective-permute-start.8 = (bf16[3,256,512]{2,1,0:T(8,128)(2,1)}, bf16[3,256,512]{2,1,0:T(8,128)(2,1)}, u32[]{:S(2)}, u32[]{:S(2)}) collective-permute-start(bf16[3,256,512]{2,1,0:T(8,128)(2,1)} %get-tuple-element.38.mine_ref), channel_id=1, source_target_pairs={{0,2},{1,3},{2,0},{3,1},{4,6},{5,7},{6,4},{7,5},{8,10},{9,11},{10,... | collective-permute-start | bytes 2359304 | tf_op jit(solution)/shard_map/ppermute | solution.py:27
  45.0 27.6 %collective-permute-start.1 = (bf16[2,512,512]{2,1,0:T(8,128)(2,1)}, bf16[2,512,512]{2,1,0:T(8,128)(2,1)}, u32[]{:S(2)}, u32[]{:S(2)}) collective-permute-start(bf16[2,512,512]{2,1,0:T(8,128)(2,1)} %get-tuple-element.24), channel_id=1, source_target_pairs={{0,1},{1,2},{2,3},{4,5},{5,6},{6,7},{8,9},{9,10},{10,11},{12,13},{... | collective-permute-start | bytes 3145736 | tf_op jit(solution)/shard_map/ppermute | solution.py:41
  47.0 36.8 %collective-permute-start = (bf16[2,512,512]{2,1,0:T(8,128)(2,1)}, bf16[2,512,512]{2,1,0:T(8,128)(2,1)}, u32[]{:S(2)}, u32[]{:S(2)}) collective-permute-start(bf16[2,512,512]{2,1,0:T(8,128)(2,1)} %get-tuple-element.23), channel_id=1, source_target_pairs={{0,1},{1,2},{2,3},{4,5},{5,6},{6,7},{8,9},{9,10},{10,11},{12,13},{... | collective-permute-start | bytes 3145736 | tf_op jit(solution)/shard_map/ppermute | solution.py:41
  49.3 38.7 %collective-permute-start.7 = (bf16[3,256,512]{2,1,0:T(8,128)(2,1)}, bf16[3,256,512]{2,1,0:T(8,128)(2,1)}, u32[]{:S(2)}, u32[]{:S(2)}) collective-permute-start(bf16[3,256,512]{2,1,0:T(8,128)(2,1)} %get-tuple-element.38.mine_ref), channel_id=1, source_target_pairs={{0,1},{1,0},{2,3},{3,2},{4,5},{5,4},{6,7},{7,6},{8,9},{9,8},{10,11... | collective-permute-start | bytes 2359304 | tf_op jit(solution)/shard_map/ppermute | solution.py:27
  50.7 37.2 %collective-permute-start.10 = (bf16[3,256,512]{2,1,0:T(8,128)(2,1)}, bf16[3,256,512]{2,1,0:T(8,128)(2,1)}, u32[]{:S(2)}, u32[]{:S(2)}) collective-permute-start(bf16[3,256,512]{2,1,0:T(8,128)(2,1)} %get-tuple-element.39.pack_ref), channel_id=1, source_target_pairs={{0,1},{1,0},{2,3},{3,2},{4,5},{5,4},{6,7},{7,6},{8,9},{9,8},{10,11... | collective-permute-start | bytes 2359304 | tf_op jit(solution)/shard_map/ppermute | solution.py:27
  63.0 24.9 %collective-permute-start.9 = (bf16[3,256,512]{2,1,0:T(8,128)(2,1)}, bf16[3,256,512]{2,1,0:T(8,128)(2,1)}, u32[]{:S(2)}, u32[]{:S(2)}) collective-permute-start(bf16[3,256,512]{2,1,0:T(8,128)(2,1)} %collective-permute-done.8.far_ref), channel_id=1, source_target_pairs={{0,1},{1,0},{2,3},{3,2},{4,5},{5,4},{6,7},{7,6},{8,9},{9,8},{10,11... | collective-permute-start | bytes 2359304 | tf_op jit(solution)/shard_map/ppermute | solution.py:27

commit v11 on v10

--- a/solution.py
+++ b/solution.py
@@ -586,13 +586,14 @@
 
 
 def stage_body(key_ref, value_ref, rate_ref, target_ref, *refs):
-    end_refs, (held_ref, values_ref, made_ref, sem, sem_end) = refs[:-5], refs[-5:]
+    end_refs, (held_ref, values_ref, made_ref, rates_ref, sem, sem_end) = refs[:-6], refs[-6:]
     features, tokens = key_ref.shape
     width = end_refs[0].shape[2]
     step = HEAD_SIZE
     lasts = [slice(tokens - (part + 1) * width, tokens - part * width) for part in range(len(end_refs))]
     begin = pl.multiple_of(lax.axis_index("narrow") * tokens, tokens)
-    rates = -rate_ref[pl.ds(lax.axis_index("wide"), 1), pl.ds(begin, tokens)]
+    rates = pltpu.make_async_copy(rate_ref.at[:, pl.ds(begin, tokens)], rates_ref, sem_end.at[0, len(end_refs)])
+    rates.start()
     values = [
         pltpu.make_async_copy(
             value_ref.at[at : at + step], values_ref.at[at : at + step], sem.at[0, at // step]
@@ -613,6 +614,8 @@
         leaving.append(pltpu.make_async_copy(source, target, mark))
         leaving[-1].start()
 
+    rates.wait()
+    rates = -rates_ref[pl.ds(lax.axis_index("wide"), 1), :]
     for place, copy in enumerate(values):
         at = slice(place * step, (place + 1) * step)
         copy.wait()
@@ -633,14 +636,15 @@
         stage_body,
         out_shape=(jax.ShapeDtypeStruct((features, tokens), jnp.bfloat16),)
         + (jax.ShapeDtypeStruct((2, features, width), jnp.bfloat16),) * parts,
-        in_specs=anywhere(2) + [pl.BlockSpec(memory_space=pltpu.VMEM)],
+        in_specs=anywhere(3),
         out_specs=tuple(anywhere(1 + parts)),
         scratch_shapes=[
             pltpu.VMEM((parts, features, width), jnp.bfloat16),
             pltpu.VMEM((features, tokens), jnp.bfloat16),
             pltpu.VMEM((features, tokens), jnp.bfloat16),
+            pltpu.VMEM((rates.shape[0], tokens), jnp.float32),
             pltpu.SemaphoreType.DMA((2, features // HEAD_SIZE)),
-            pltpu.SemaphoreType.DMA((3, parts)),
+            pltpu.SemaphoreType.DMA((3, parts + 1)),
         ],
         cost_estimate=pl.CostEstimate(
             flops=features * tokens,

time: 101 us -> 100 us (0.990)
  no operation moved by 1% of the time
where the time goes in v11:
time: 100 us
  Pallas kernels  53.8 us (54%)
  waiting for transfers between devices  23.2 us (23%)
  starting transfers between devices  22.2 us (22%)
    ppermute x7, starting transfers between devices, swapped(): lax.ppermute(array, axis, [(i, i ^ 1 << distance) for i in range(lax.axis...  14.9 us
    pallas_call x1, Pallas kernels, fast_recall(): pl.pallas_call(recall_body, out_shape=jax.ShapeDtypeStruct((features, tok...  12.8 us
    ppermute x7, waiting for transfers between devices, swapped(): lax.ppermute(array, axis, [(i, i ^ 1 << distance) for i in range(lax.axis...  12.3 us
    pallas_call x1, Pallas kernels, fast_sums(): pl.pallas_call(functools.partial(sums_body, owned=owned, cuts=cuts), out_...  12.2 us
    ppermute x2, waiting for transfers between devices, from_behind(): lax.ppermute(value, axis, [(source, source + steps) for source in range(i...  10.8 us
    pallas_call x1, Pallas kernels, attend_late(): pl.pallas_call(functools.partial(attend_body, block=min(256, WINDOW), win...  9.69 us
    pallas_call x1, Pallas kernels, attend_early(): pl.pallas_call(functools.partial(early_body, block=min(256, near)), out_s...  9.19 us
    ppermute x2, starting transfers between devices, from_behind(): lax.ppermute(value, axis, [(source, source + steps) for source in range(i...  4.23 us
  transfers between devices with their start and end apart: 11, of which 3 were waited for; matrix products, arithmetic and copies ran while one was open for 0% of the time, Pallas kernels for 29%

profile of v11, /device:TPU:1, one launch (start us, length us, event | category | flops | bytes accessed | tf_op | source)
XLA Modules:
  0.0 100.1 jit_solution(16094896226750994822)
XLA Ops:
  0.6 0.1 collective-permute-start.5
  0.7 3.4 %stage.1 = (bf16[512,2048]{1,0:T(8,128)(2,1)}, bf16[2,512,512]{2,1,0:T(8,128)(2,1)}, bf16[2,512,512]{2,1,0:T(8,128)(2,1)}) custom-call(bf16[512,2048]{1,0:T(8,128)(2,1)} %refs_4_.1, bf16[512,2048]{1,0:T(8,128)(2,1)} %vc_ref.3, f32[8,8192]{1,0:T(8,128)} %rate_ref.1), custom_call_target="tpu_custom_call" | custom-call | flops 1048576 | bytes 8388608 | tf_op jit(solution)/shard_map/stage/pallas_call | solution.py:635
  4.1 0.6 collective-permute-start.6
  4.7 2.5 %prepare.1 = (bf16[3,256,512]{2,1,0:T(8,128)(2,1)}, bf16[3,256,512]{2,1,0:T(8,128)(2,1)}) custom-call(bf16[2,512,512]{2,1,0:T(8,128)(2,1)} %gate_ref.1, bf16[2,512,512]{2,1,0:T(8,128)(2,1)} %lift_ref.1, bf16[2,512,512]{2,1,0:T(8,128)(2,1)} %down_ref.1), custom_call_target="tpu_custom_call" | custom-call | bytes 3145728 | tf_op jit(solution)/shard_map/prepare/pallas_call | solution.py:570
  7.2 0.1 collective-permute-start.2
  7.3 1.6 %collective-permute-start.3 = (bf16[3,256,512]{2,1,0:T(8,128)(2,1)}, bf16[3,256,512]{2,1,0:T(8,128)(2,1)}, u32[]{:S(2)}, u32[]{:S(2)}) collective-permute-start(bf16[3,256,512]{2,1,0:T(8,128)(2,1)} %get-tuple-element.33.refs_0_), channel_id=1, source_target_pairs={{0,2},{4,6},{9,11},{13,15},{18,16},{22,20},{27,25},{31,29}} | collective-permute-start | bytes 2359304 | tf_op jit(solution)/shard_map/ppermute | solution.py:936
  8.8 1.5 %collective-permute-start.4 = (bf16[3,256,512]{2,1,0:T(8,128)(2,1)}, bf16[3,256,512]{2,1,0:T(8,128)(2,1)}, u32[]{:S(2)}, u32[]{:S(2)}) collective-permute-start(bf16[3,256,512]{2,1,0:T(8,128)(2,1)} %get-tuple-element.26), channel_id=1, source_target_pairs={{0,3},{4,7},{9,10},{13,14},{18,17},{22,21},{27,24},{31,28}} | collective-permute-start | bytes 2359304 | tf_op jit(solution)/shard_map/ppermute | solution.py:936
  10.4 9.7 %attend_late.1._ = bf16[512,2048]{1,0:T(8,128)(2,1)} custom-call(bf16[512,2048]{1,0:T(8,128)(2,1)} %query_ref.1, bf16[512,2048]{1,0:T(8,128)(2,1)} %refs_4_.1, bf16[512,2048]{1,0:T(8,128)(2,1)} %vc_ref.3, bf16[512,2048]{1,0:T(8,128)(2,1)} %refs_4_.1, bf16[512,2048]{1,0:T(8,128)(2,1)} %vc_ref.3), custom_call_target="tpu_custom_call" | custom-call | flops 2684354560 | bytes 5242880 | tf_op jit(solution)/shard_map/attend_late/pallas_call | solution.py:269
  20.1 0.0 collective-permute-done.2.refs_1_
  20.1 0.0 collective-permute-done.3.refs_2_
  20.1 0.0 collective-permute-done.4.refs_3_
  20.1 0.0 collective-permute-done.5.refs_6_
  20.1 0.0 collective-permute-done.6.refs_7_
  20.1 12.2 %fast_sums.1 = (bf16[3,256,512]{2,1,0:T(8,128)(2,1)}, bf16[3,256,512]{2,1,0:T(8,128)(2,1)}) custom-call(bf16[3,256,512]{2,1,0:T(8,128)(2,1)} %get-tuple-element.33.refs_0_, bf16[3,256,512]{2,1,0:T(8,128)(2,1)} %collective-permute-done.2.refs_1_, bf16[3,256,512]{2,1,0:T(8,128)(2,1)} %collective-permute-done.3.refs_2_, ...), custom_call_target="tpu_custom_call" | custom-call | flops 6442450944 | bytes 10747904 | tf_op jit(solution)/shard_map/fast_sums/pallas_call | solution.py:736
  32.3 11.9 %collective-permute-start.8 = (bf16[3,256,512]{2,1,0:T(8,128)(2,1)}, bf16[3,256,512]{2,1,0:T(8,128)(2,1)}, u32[]{:S(2)}, u32[]{:S(2)}) collective-permute-start(bf16[3,256,512]{2,1,0:T(8,128)(2,1)} %get-tuple-element.38.mine_ref), channel_id=1, source_target_pairs={{0,2},{1,3},{2,0},{3,1},{4,6},{5,7},{6,4},{7,5},{8,10},{9,11},{10,... | collective-permute-start | bytes 2359304 | tf_op jit(solution)/shard_map/ppermute | solution.py:27
  44.2 2.0 %collective-permute-start.1 = (bf16[2,512,512]{2,1,0:T(8,128)(2,1)}, bf16[2,512,512]{2,1,0:T(8,128)(2,1)}, u32[]{:S(2)}, u32[]{:S(2)}) collective-permute-start(bf16[2,512,512]{2,1,0:T(8,128)(2,1)} %get-tuple-element.24), channel_id=1, source_target_pairs={{0,1},{1,2},{2,3},{4,5},{5,6},{6,7},{8,9},{9,10},{10,11},{12,13},{... | collective-permute-start | bytes 3145736 | tf_op jit(solution)/shard_map/ppermute | solution.py:41
  46.2 2.2 %collective-permute-start = (bf16[2,512,512]{2,1,0:T(8,128)(2,1)}, bf16[2,512,512]{2,1,0:T(8,128)(2,1)}, u32[]{:S(2)}, u32[]{:S(2)}) collective-permute-start(bf16[2,512,512]{2,1,0:T(8,128)(2,1)} %get-tuple-element.23), channel_id=1, source_target_pairs={{0,1},{1,2},{2,3},{4,5},{5,6},{6,7},{8,9},{9,10},{10,11},{12,13},{... | collective-permute-start | bytes 3145736 | tf_op jit(solution)/shard_map/ppermute | solution.py:41
  48.5 1.4 %collective-permute-start.7 = (bf16[3,256,512]{2,1,0:T(8,128)(2,1)}, bf16[3,256,512]{2,1,0:T(8,128)(2,1)}, u32[]{:S(2)}, u32[]{:S(2)}) collective-permute-start(bf16[3,256,512]{2,1,0:T(8,128)(2,1)} %get-tuple-element.38.mine_ref), channel_id=1, source_target_pairs={{0,1},{1,0},{2,3},{3,2},{4,5},{5,4},{6,7},{7,6},{8,9},{9,8},{10,11... | collective-permute-start | bytes 2359304 | tf_op jit(solution)/shard_map/ppermute | solution.py:27
  49.9 0.0 collective-permute-start.10
  49.9 12.3 %collective-permute-done.8.far_ref = bf16[3,256,512]{2,1,0:T(8,128)(2,1)} collective-permute-done((bf16[3,256,512]{2,1,0:T(8,128)(2,1)}, bf16[3,256,512]{2,1,0:T(8,128)(2,1)}, u32[]{:S(2)}, u32[]{:S(2)}) %collective-permute-start.8) | collective-permute-done | bytes 786464 | tf_op jit(solution)/shard_map/ppermute | solution.py:27
  62.2 0.8 collective-permute-start.9
  63.0 8.8 %collective-permute-done.1.kp_ref.vp_ref = bf16[2,512,512]{2,1,0:T(8,128)(2,1)} collective-permute-done((bf16[2,512,512]{2,1,0:T(8,128)(2,1)}, bf16[2,512,512]{2,1,0:T(8,128)(2,1)}, u32[]{:S(2)}, u32[]{:S(2)}) %collective-permute-start.1) | collective-permute-done | bytes 1048608 | tf_op jit(solution)/shard_map/ppermute | solution.py:41
  71.8 9.2 %attend_early.1 = (bf16[512,2048]{1,0:T(8,128)(2,1)}, f32[512,512]{1,0:T(8,128)}, f32[32,512]{1,0:T(8,128)}, f32[32,512]{1,0:T(8,128)}) custom-call(bf16[512,2048]{1,0:T(8,128)(2,1)} %query_ref.1, bf16[2,512,512]{2,1,0:T(8,128)(2,1)} %collective-permute-done.1.kp_ref.vp_ref, ...), custom_call_target="tpu_custom_call", output_to_operand_aliasing={{0}: (7, {})} | custom-call | flops 2684354560 | bytes 7340032 | tf_op jit(solution)/shard_map/attend_early/pallas_call | solution.py:378
  81.0 2.0 %collective-permute-done.prior_ref = bf16[2,512,512]{2,1,0:T(8,128)(2,1)} collective-permute-done((bf16[2,512,512]{2,1,0:T(8,128)(2,1)}, bf16[2,512,512]{2,1,0:T(8,128)(2,1)}, u32[]{:S(2)}, u32[]{:S(2)}) %collective-permute-start) | collective-permute-done | bytes 1048608 | tf_op jit(solution)/shard_map/ppermute | solution.py:41
  83.0 4.1 %attend_last.1 = bf16[512,2048]{1,0:T(8,128)(2,1)} custom-call(bf16[512,2048]{1,0:T(8,128)(2,1)} %query_ref.1, bf16[2,512,512]{2,1,0:T(8,128)(2,1)} %collective-permute-done.prior_ref, bf16[512,1024]{1,0:T(8,128)(2,1)} %ck_ref.3, bf16[512,1024]{1,0:T(8,128)(2,1)} %cv_ref.3, f32[512,512]{1,0:T(8,128)} %get-tuple-element.29.part_ref, ...), custom_call_target="tpu_custom_call", output_to_operand_aliasing={{}: (7, {})} | custom-call | flops 402653184 | bytes 3670016 | tf_op jit(solution)/shard_map/attend_last/pallas_call | solution.py:503
  87.1 0.0 collective-permute-done.7.other_ref
  87.1 0.0 collective-permute-done.10.pair_pack_ref
  87.1 0.0 collective-permute-done.9.other_far_ref
  87.2 12.8 %fast_recall.1 = bf16[512,2048]{1,0:T(8,128)(2,1)} custom-call(bf16[3,256,512]{2,1,0:T(8,128)(2,1)} %get-tuple-element.38.mine_ref, bf16[3,256,512]{2,1,0:T(8,128)(2,1)} %collective-permute-done.7.other_ref, bf16[3,256,512]{2,1,0:T(8,128)(2,1)} %collective-permute-done.8.far_ref, bf16[3,256,512]{2,1,0:T(8,128)(2,1)} %collective-permute-done.9.other_far_ref, ...), custom_call_target="tpu_custom_call" | custom-call | flops 8053063680 | bytes 7340032 | tf_op jit(solution)/shard_map/fast_recall/pallas_call | solution.py:878
Async XLA Ops:
  0.6 19.5 %collective-permute-start.5 = (bf16[512,2048]{1,0:T(8,128)(2,1)}, bf16[512,2048]{1,0:T(8,128)(2,1)}, u32[]{:S(2)}, u32[]{:S(2)}) collective-permute-start(bf16[512,2048]{1,0:T(8,128)(2,1)} %refs_4_.1), channel_id=1, source_target_pairs={{0,1},{1,0},{2,3},{3,2},{4,5},{5,4},{6,7},{7,6},{8,9},{9,8},{10,11... | collective-permute-start | bytes 6291464 | tf_op jit(solution)/shard_map/ppermute | solution.py:27
  4.1 16.0 %collective-permute-start.6 = (bf16[512,2048]{1,0:T(8,128)(2,1)}, bf16[512,2048]{1,0:T(8,128)(2,1)}, u32[]{:S(2)}, u32[]{:S(2)}) collective-permute-start(bf16[512,2048]{1,0:T(8,128)(2,1)} %get-tuple-element.37.refs_5_), channel_id=1, source_target_pairs={{0,1},{1,0},{2,3},{3,2},{4,5},{5,4},{6,7},{7,6},{8,9},{9,8},{10,11... | collective-permute-start | bytes 6291464 | tf_op jit(solution)/shard_map/ppermute | solution.py:27
  7.2 12.9 %collective-permute-start.2 = (bf16[3,256,512]{2,1,0:T(8,128)(2,1)}, bf16[3,256,512]{2,1,0:T(8,128)(2,1)}, u32[]{:S(2)}, u32[]{:S(2)}) collective-permute-start(bf16[3,256,512]{2,1,0:T(8,128)(2,1)} %get-tuple-element.26), channel_id=1, source_target_pairs={{0,1},{1,0},{2,3},{3,2},{4,5},{5,4},{6,7},{7,6},{8,9},{9,8},{10,11... | collective-permute-start | bytes 2359304 | tf_op jit(solution)/shard_map/ppermute | solution.py:27
  7.3 12.8 %collective-permute-start.3 = (bf16[3,256,512]{2,1,0:T(8,128)(2,1)}, bf16[3,256,512]{2,1,0:T(8,128)(2,1)}, u32[]{:S(2)}, u32[]{:S(2)}) collective-permute-start(bf16[3,256,512]{2,1,0:T(8,128)(2,1)} %get-tuple-element.33.refs_0_), channel_id=1, source_target_pairs={{0,2},{4,6},{9,11},{13,15},{18,16},{22,20},{27,25},{31,29}} | collective-permute-start | bytes 2359304 | tf_op jit(solution)/shard_map/ppermute | solution.py:936
  8.8 11.2 %collective-permute-start.4 = (bf16[3,256,512]{2,1,0:T(8,128)(2,1)}, bf16[3,256,512]{2,1,0:T(8,128)(2,1)}, u32[]{:S(2)}, u32[]{:S(2)}) collective-permute-start(bf16[3,256,512]{2,1,0:T(8,128)(2,1)} %get-tuple-element.26), channel_id=1, source_target_pairs={{0,3},{4,7},{9,10},{13,14},{18,17},{22,21},{27,24},{31,28}} | collective-permute-start | bytes 2359304 | tf_op jit(solution)/shard_map/ppermute | solution.py:936
  32.3 29.9 %collective-permute-start.8 = (bf16[3,256,512]{2,1,0:T(8,128)(2,1)}, bf16[3,256,512]{2,1,0:T(8,128)(2,1)}, u32[]{:S(2)}, u32[]{:S(2)}) collective-permute-start(bf16[3,256,512]{2,1,0:T(8,128)(2,1)} %get-tuple-element.38.mine_ref), channel_id=1, source_target_pairs={{0,2},{1,3},{2,0},{3,1},{4,6},{5,7},{6,4},{7,5},{8,10},{9,11},{10,... | collective-permute-start | bytes 2359304 | tf_op jit(solution)/shard_map/ppermute | solution.py:27
  44.2 27.6 %collective-permute-start.1 = (bf16[2,512,512]{2,1,0:T(8,128)(2,1)}, bf16[2,512,512]{2,1,0:T(8,128)(2,1)}, u32[]{:S(2)}, u32[]{:S(2)}) collective-permute-start(bf16[2,512,512]{2,1,0:T(8,128)(2,1)} %get-tuple-element.24), channel_id=1, source_target_pairs={{0,1},{1,2},{2,3},{4,5},{5,6},{6,7},{8,9},{9,10},{10,11},{12,13},{... | collective-permute-start | bytes 3145736 | tf_op jit(solution)/shard_map/ppermute | solution.py:41
  46.2 36.8 %collective-permute-start = (bf16[2,512,512]{2,1,0:T(8,128)(2,1)}, bf16[2,512,512]{2,1,0:T(8,128)(2,1)}, u32[]{:S(2)}, u32[]{:S(2)}) collective-permute-start(bf16[2,512,512]{2,1,0:T(8,128)(2,1)} %get-tuple-element.23), channel_id=1, source_target_pairs={{0,1},{1,2},{2,3},{4,5},{5,6},{6,7},{8,9},{9,10},{10,11},{12,13},{... | collective-permute-start | bytes 3145736 | tf_op jit(solution)/shard_map/ppermute | solution.py:41
  48.5 38.7 %collective-permute-start.7 = (bf16[3,256,512]{2,1,0:T(8,128)(2,1)}, bf16[3,256,512]{2,1,0:T(8,128)(2,1)}, u32[]{:S(2)}, u32[]{:S(2)}) collective-permute-start(bf16[3,256,512]{2,1,0:T(8,128)(2,1)} %get-tuple-element.38.mine_ref), channel_id=1, source_target_pairs={{0,1},{1,0},{2,3},{3,2},{4,5},{5,4},{6,7},{7,6},{8,9},{9,8},{10,11... | collective-permute-start | bytes 2359304 | tf_op jit(solution)/shard_map/ppermute | solution.py:27
  49.9 37.2 %collective-permute-start.10 = (bf16[3,256,512]{2,1,0:T(8,128)(2,1)}, bf16[3,256,512]{2,1,0:T(8,128)(2,1)}, u32[]{:S(2)}, u32[]{:S(2)}) collective-permute-start(bf16[3,256,512]{2,1,0:T(8,128)(2,1)} %get-tuple-element.39.pack_ref), channel_id=1, source_target_pairs={{0,1},{1,0},{2,3},{3,2},{4,5},{5,4},{6,7},{7,6},{8,9},{9,8},{10,11... | collective-permute-start | bytes 2359304 | tf_op jit(solution)/shard_map/ppermute | solution.py:27
  62.2 24.9 %collective-permute-start.9 = (bf16[3,256,512]{2,1,0:T(8,128)(2,1)}, bf16[3,256,512]{2,1,0:T(8,128)(2,1)}, u32[]{:S(2)}, u32[]{:S(2)}) collective-permute-start(bf16[3,256,512]{2,1,0:T(8,128)(2,1)} %collective-permute-done.8.far_ref), channel_id=1, source_target_pairs={{0,1},{1,0},{2,3},{3,2},{4,5},{5,4},{6,7},{7,6},{8,9},{9,8},{10,11... | collective-permute-start | bytes 2359304 | tf_op jit(solution)/shard_map/ppermute | solution.py:27
